TPU v7x, 256 devices: a whole 4x4x8 slice. The times are simulated.
256 devices in a mesh: gx: 4 (over y), gy: 8 (over x, core), gz: 8 (over z).
Axes of the slice: x: 4, y: 4, z: 8, core: 2. Of those that a mesh axis runs over, the one named last changes fastest.
Arguments:
- right_side: float32 [32, 256, 1024], P('gx', 'gy', 'gz'), may hold values from -8 to 8
- alpha_coef: float32 [32, 256, 1024], P('gx', 'gy', 'gz'), may hold values from 0.25 to 4
- beta_coef: float32 [32, 256, 1024], P('gx', 'gy', 'gz'), may hold values from 0.25 to 4
Outputs:
- solution_field: float32 [32, 256, 1024], P('gx', 'gy', 'gz')
- residual_field: float32 [32, 256, 1024], P('gx', 'gy', 'gz')
All inputs are finite; a program needn't handle non-finite values.
Results may differ from a plain program's by a relative error of at most 0.0003.
Values sent between devices are 32-bit elements; how exact they have to be, the bound alone decides.
A program may use at most 64 MiB of HBM per device.

v0:
```python
import jax
import jax.numpy as jnp
from jax import lax
from jax.sharding import PartitionSpec as P

LEVELS = 3
SWEEPS = 4
BOTTOM = 12


SHIFT_BASE = 0.01
UPPER_EIG = 2.0
SMOOTH_LOWER = 0.25
BOTTOM_LOWER = 0.02


def with_halo(block, sides, width):
    for axis, dim in sides:
        count = lax.axis_size(axis)
        forward = [(i, i + 1) for i in range(count - 1)]
        backward = [(target, source) for source, target in forward]
        low = lax.ppermute(
            lax.slice_in_dim(block, block.shape[dim] - width, None, axis=dim), axis, forward
        )
        high = lax.ppermute(lax.slice_in_dim(block, 0, width, axis=dim), axis, backward)
        block = jnp.concatenate([low, block, high], axis=dim)
    return block


def split_padded(padded):
    return (
        padded[:-2, 1:-1, 1:-1],
        padded[2:, 1:-1, 1:-1],
        padded[1:-1, :-2, 1:-1],
        padded[1:-1, 2:, 1:-1],
        padded[1:-1, 1:-1, :-2],
        padded[1:-1, 1:-1, 2:],
    )


def zero_pad(field):
    return jnp.pad(field, 1)


def rim_iterate(field):
    return with_halo(field, (("gx", 0), ("gy", 1), ("gz", 2)), 1)


def rim_coefficient(field):
    return with_halo(field, (("gx", 0), ("gy", 1), ("gz", 2)), 1)


def level_operator(beta_level, alpha_level, padded_beta, shift):
    coeffs = tuple((0.5 * (beta_level + other) for other in split_padded(padded_beta)))
    diagonal = shift * alpha_level
    for coeff in coeffs:
        diagonal = diagonal + coeff
    return (coeffs, diagonal)


def apply_operator(field, operator, pad_field):
    coeffs, diagonal = operator
    others = split_padded(pad_field(field))
    total = coeffs[0] * others[0]
    for index in range(1, 6):
        total = total + coeffs[index] * others[index]
    return diagonal * field - total


def chebyshev(iterate, rhs_level, operator, count, lower, zero_start, pad_field):
    diagonal = operator[1]
    center = (UPPER_EIG + lower) / 2.0
    half_width = (UPPER_EIG - lower) / 2.0
    sigma_ratio = center / half_width
    rho_old = 1.0 / sigma_ratio
    if zero_start:
        remain = rhs_level
    else:
        remain = rhs_level - apply_operator(iterate, operator, pad_field)
    update = remain / diagonal / center
    iterate = iterate + update
    for sweep_index in range(count - 1):
        remain = rhs_level - apply_operator(iterate, operator, pad_field)
        rho_new = 1.0 / (2.0 * sigma_ratio - rho_old)
        update = rho_new * rho_old * update + 2.0 * rho_new / half_width * (remain / diagonal)
        iterate = iterate + update
        rho_old = rho_new
    return iterate


def restrict_mean(field):
    first, second, third = field.shape
    blocks = field.reshape(first // 2, 2, second // 2, 2, third // 2, 2)
    return jnp.sum(blocks, axis=(1, 3, 5)) * 0.125


def prolong_copy(field):
    return jnp.repeat(jnp.repeat(jnp.repeat(field, 2, axis=0), 2, axis=1), 2, axis=2)


def shards(right_side, alpha_coef, beta_coef):
    betas = [beta_coef]
    alphas = [alpha_coef]
    for level in range(LEVELS):
        betas.append(restrict_mean(betas[-1]))
        alphas.append(restrict_mean(alphas[-1]))
    operators = []
    for level in range(LEVELS):
        padded_beta = rim_coefficient(betas[level])
        operators.append(
            level_operator(betas[level], alphas[level], padded_beta, SHIFT_BASE * 4.0**level)
        )
    rhs_levels = [right_side]
    smoothed = []
    for level in range(LEVELS):
        iterate = chebyshev(
            jnp.zeros_like(rhs_levels[level]),
            rhs_levels[level],
            operators[level],
            SWEEPS,
            SMOOTH_LOWER,
            True,
            rim_iterate,
        )
        remain = rhs_levels[level] - apply_operator(iterate, operators[level], rim_iterate)
        smoothed.append(iterate)
        rhs_levels.append(4.0 * restrict_mean(remain))
    coarse_rhs = rhs_levels[LEVELS]
    local_shape = coarse_rhs.shape
    packed = jnp.stack([coarse_rhs, betas[LEVELS], alphas[LEVELS]])
    index_x = lax.axis_index("gx")
    index_y = lax.axis_index("gy")
    index_z = lax.axis_index("gz")
    packed = lax.all_gather(packed, "gx", axis=1, tiled=True)
    packed = lax.all_gather(packed, "gy", axis=2, tiled=True)
    packed = lax.all_gather(packed, "gz", axis=3, tiled=True)
    whole_rhs = packed[0]
    whole_beta = packed[1]
    whole_alpha = packed[2]
    bottom_operator = level_operator(
        whole_beta, whole_alpha, zero_pad(whole_beta), SHIFT_BASE * 4.0**LEVELS
    )
    whole_correction = chebyshev(
        jnp.zeros_like(whole_rhs), whole_rhs, bottom_operator, BOTTOM, BOTTOM_LOWER, True, zero_pad
    )
    starts = (index_x * local_shape[0], index_y * local_shape[1], index_z * local_shape[2])
    correction = lax.dynamic_slice(whole_correction, starts, local_shape)
    for level in range(LEVELS - 1, -1, -1):
        start_field = smoothed[level] + prolong_copy(correction)
        correction = chebyshev(
            start_field,
            rhs_levels[level],
            operators[level],
            SWEEPS,
            SMOOTH_LOWER,
            False,
            rim_iterate,
        )
    residual_field = right_side - apply_operator(correction, operators[0], rim_iterate)
    return (correction, residual_field)


def solution(mesh):
    in_specs = (P("gx", "gy", "gz"), P("gx", "gy", "gz"), P("gx", "gy", "gz"))
    out_specs = (P("gx", "gy", "gz"), P("gx", "gy", "gz"))
    return jax.shard_map(shards, mesh=mesh, in_specs=in_specs, out_specs=out_specs, check_vma=False)
```

profile of v0, /device:TPU:1, one launch (start us, length us, event | category | flops | bytes accessed | tf_op | source)
XLA Modules:
  0.0 760.6 jit_solution(5426633637837439148)
XLA Ops:
  65.7 6.1 collective-permute-start.14
  89.2 9.7 %reshape.99 = f32[4,2,16,2,64,2]{5,4,3,2,1,0:T(8,128)} reshape(f32[8,32,128]{2,1,0:T(8,128)S(1)} %copy-done) | data formatting | bytes 262144 | tf_op jit(solution)/shard_map/reshape | solution.py:93
  112.4 5.8 collective-permute-start.22
  123.3 9.7 %reshape.98 = f32[4,2,16,2,64,2]{5,4,3,2,1,0:T(8,128)} reshape(f32[8,32,128]{2,1,0:T(8,128)S(1)} %copy-done.1) | data formatting | bytes 262144 | tf_op jit(solution)/shard_map/reshape | solution.py:93
  170.8 9.7 %reshape.97 = f32[4,2,16,2,64,2]{5,4,3,2,1,0:T(8,128)} reshape(f32[8,32,128]{2,1,0:T(8,128)S(1)} %fusion.79) | data formatting | bytes 262144 | tf_op jit(solution)/shard_map/reshape | solution.py:93
  200.7 6.6 collective-permute-start.40
  217.3 5.9 collective-permute-start.44
  241.0 5.8 collective-permute-start.50
  313.2 5.9 collective-permute-start.70
  328.8 5.9 collective-permute-start.74
  351.0 5.9 collective-permute-start.80
  373.7 5.9 collective-permute-start.86
  388.5 10.0 %all_gather.9 = f32[3,4,4,16]{3,2,1,0:T(4,128)S(1)} all-gather(f32[3,1,4,16]{3,2,1,0:T(4,128)S(1)} %pad_maximum_fusion.524), channel_id=1, replica_groups=mesh['gx'=4,'gy'=8,'gz'=8] {'gx'}, dimensions={1}, use_global_device_ids=true | all-gather | bytes 3840 | tf_op jit(solution)/shard_map/all_gather | solution.py:134
  398.6 16.7 %all_gather.10 = f32[3,4,32,16]{3,1,0,2:T(4,128)S(1)} all-gather(f32[3,4,4,16]{3,1,0,2:T(4,128)S(1)} %copy.376), channel_id=1, replica_groups=mesh['gx'=4,'gy'=8,'gz'=8] {'gy'}, dimensions={2}, use_global_device_ids=true | all-gather | bytes 27648 | tf_op jit(solution)/shard_map/all_gather | solution.py:135
  415.4 28.5 %all_gather.11 = f32[3,4,32,128]{2,1,0,3:T(4,128)S(1)} all-gather(f32[3,4,32,16]{2,1,0,3:T(4,128)S(1)} %copy.377), channel_id=1, replica_groups=mesh['gx'=4,'gy'=8,'gz'=8] {'gz'}, dimensions={3}, use_global_device_ids=true | all-gather | bytes 221184 | tf_op jit(solution)/shard_map/all_gather | solution.py:136
  452.5 9.0 %collective-permute-start.93 = (f32[4,1,32]{2,1,0:T(1,128)S(1)}, f32[4,1,32]{2,1,0:T(1,128)S(1)}, u32[]{:S(2)}, u32[]{:S(2)}) collective-permute-start(f32[4,1,32]{2,1,0:T(1,128)S(1)} %get-tuple-element.228), channel_id=1, source_target_pairs={{8,0},{16,8},{24,16},{32,24},{40,32},{48,40},{56,48},{9,1},{17,9},... | collective-permute-start | bytes 1544 | tf_op jit(solution)/shard_map/ppermute | solution.py:25
  523.9 5.9 collective-permute-start.110
  546.4 5.9 collective-permute-start.116
  569.1 5.9 collective-permute-start.122
  591.8 6.1 collective-permute-start.128
  615.6 5.9 collective-permute-start.134
  623.7 5.8 collective-permute-start.136
  640.1 5.9 collective-permute-start.140
  648.2 5.8 collective-permute-start.142
  665.6 5.9 collective-permute-start.146
  673.7 5.8 collective-permute-start.148
  691.2 6.7 collective-permute-start.152
  700.0 5.8 collective-permute-start.154
  717.5 5.9 collective-permute-start.158
  725.6 5.8 collective-permute-start.160
  743.0 5.9 collective-permute-start.164
  751.1 6.0 collective-permute-start.166
  (520 shorter events, 514.9 us)
Async XLA Ops:
  83.2 19.7 %collective-permute-start.19 = (f32[1,32,128]{2,1,0:T(8,128)S(1)}, f32[1,32,128]{2,1,0:T(8,128)S(1)}, u32[]{:S(2)}, u32[]{:S(2)}) collective-permute-start(f32[1,32,128]{2,1,0:T(8,128)S(1)} %get-tuple-element.142), channel_id=1, source_target_pairs={{64,0},{128,64},{192,128},{65,1},{129,65},{193,129},{66,2},{130,66... | collective-permute-start | bytes 49160 | tf_op jit(solution)/shard_map/ppermute | solution.py:25
  84.5 18.4 %collective-permute-start.18 = (f32[1,32,128]{2,1,0:T(8,128)S(1)}, f32[1,32,128]{2,1,0:T(8,128)S(1)}, u32[]{:S(2)}, u32[]{:S(2)}) collective-permute-start(f32[1,32,128]{2,1,0:T(8,128)S(1)} %get-tuple-element.141), channel_id=1, source_target_pairs={{0,64},{64,128},{128,192},{1,65},{65,129},{129,193},{2,66},{66,130... | collective-permute-start | bytes 49160 | tf_op jit(solution)/shard_map/ppermute | solution.py:22
  111.1 25.9 %collective-permute-start.23 = (f32[10,34,1]{2,1,0:T(8,128)S(1)}, f32[10,34,1]{2,1,0:T(8,128)S(1)}, u32[]{:S(2)}, u32[]{:S(2)}) collective-permute-start(f32[10,34,1]{2,1,0:T(8,128)S(1)} %get-tuple-element.102), channel_id=1, source_target_pairs={{1,0},{2,1},{3,2},{4,3},{5,4},{6,5},{7,6},{9,8},{10,9},{11,10},{12... | collective-permute-start | bytes 4088 | tf_op jit(solution)/shard_map/ppermute | solution.py:25
  112.4 24.6 %collective-permute-start.22 = (f32[10,34,1]{2,1,0:T(8,128)S(1)}, f32[10,34,1]{2,1,0:T(8,128)S(1)}, u32[]{:S(2)}, u32[]{:S(2)}) collective-permute-start(f32[10,34,1]{2,1,0:T(8,128)S(1)} %get-tuple-element.101), channel_id=1, source_target_pairs={{0,1},{1,2},{2,3},{3,4},{4,5},{5,6},{6,7},{8,9},{9,10},{10,11},{11... | collective-permute-start | bytes 4088 | tf_op jit(solution)/shard_map/ppermute | solution.py:22
  118.2 25.3 %collective-permute-start.30 = (f32[1,16,64]{2,1,0:T(8,128)S(1)}, f32[1,16,64]{2,1,0:T(8,128)S(1)}, u32[]{:S(2)}, u32[]{:S(2)}) collective-permute-start(f32[1,16,64]{2,1,0:T(8,128)S(1)} %get-tuple-element.220), channel_id=1, source_target_pairs={{0,64},{64,128},{128,192},{1,65},{65,129},{129,193},{2,66},{66,130... | collective-permute-start | bytes 12296 | tf_op jit(solution)/shard_map/ppermute | solution.py:22
  121.9 21.7 %collective-permute-start.31 = (f32[1,16,64]{2,1,0:T(8,128)S(1)}, f32[1,16,64]{2,1,0:T(8,128)S(1)}, u32[]{:S(2)}, u32[]{:S(2)}) collective-permute-start(f32[1,16,64]{2,1,0:T(8,128)S(1)} %get-tuple-element.219), channel_id=1, source_target_pairs={{64,0},{128,64},{192,128},{65,1},{129,65},{193,129},{66,2},{130,66... | collective-permute-start | bytes 12296 | tf_op jit(solution)/shard_map/ppermute | solution.py:25
  137.3 13.2 %collective-permute-start.25 = (f32[1,32,128]{2,1,0:T(8,128)S(1)}, f32[1,32,128]{2,1,0:T(8,128)S(1)}, u32[]{:S(2)}, u32[]{:S(2)}) collective-permute-start(f32[1,32,128]{2,1,0:T(8,128)S(1)} %get-tuple-element.140), channel_id=1, source_target_pairs={{64,0},{128,64},{192,128},{65,1},{129,65},{193,129},{66,2},{130,66... | collective-permute-start | bytes 49160 | tf_op jit(solution)/shard_map/ppermute | solution.py:25
  138.6 11.9 %collective-permute-start.24 = (f32[1,32,128]{2,1,0:T(8,128)S(1)}, f32[1,32,128]{2,1,0:T(8,128)S(1)}, u32[]{:S(2)}, u32[]{:S(2)}) collective-permute-start(f32[1,32,128]{2,1,0:T(8,128)S(1)} %get-tuple-element.139), channel_id=1, source_target_pairs={{0,64},{64,128},{128,192},{1,65},{65,129},{129,193},{2,66},{66,130... | collective-permute-start | bytes 49160 | tf_op jit(solution)/shard_map/ppermute | solution.py:22
  143.6 12.6 %collective-permute-start.32 = (f32[6,1,64]{2,1,0:T(1,128)S(1)}, f32[6,1,64]{2,1,0:T(1,128)S(1)}, u32[]{:S(2)}, u32[]{:S(2)}) collective-permute-start(f32[6,1,64]{2,1,0:T(1,128)S(1)} %get-tuple-element.184), channel_id=1, source_target_pairs={{0,8},{8,16},{16,24},{24,32},{32,40},{40,48},{48,56},{1,9},{9,17},... | collective-permute-start | bytes 4616 | tf_op jit(solution)/shard_map/ppermute | solution.py:22
  157.0 13.5 %collective-permute-start.29 = (f32[10,34,1]{2,1,0:T(8,128)S(1)}, f32[10,34,1]{2,1,0:T(8,128)S(1)}, u32[]{:S(2)}, u32[]{:S(2)}) collective-permute-start(f32[10,34,1]{2,1,0:T(8,128)S(1)} %get-tuple-element.100), channel_id=1, source_target_pairs={{1,0},{2,1},{3,2},{4,3},{5,4},{6,5},{7,6},{9,8},{10,9},{11,10},{12... | collective-permute-start | bytes 4088 | tf_op jit(solution)/shard_map/ppermute | solution.py:25
  158.3 12.2 %collective-permute-start.28 = (f32[10,34,1]{2,1,0:T(8,128)S(1)}, f32[10,34,1]{2,1,0:T(8,128)S(1)}, u32[]{:S(2)}, u32[]{:S(2)}) collective-permute-start(f32[10,34,1]{2,1,0:T(8,128)S(1)} %get-tuple-element.99), channel_id=1, source_target_pairs={{0,1},{1,2},{2,3},{3,4},{4,5},{5,6},{6,7},{8,9},{9,10},{10,11},{11... | collective-permute-start | bytes 4088 | tf_op jit(solution)/shard_map/ppermute | solution.py:22
  163.9 20.6 %collective-permute-start.34 = (f32[6,18,1]{2,1,0:T(8,128)S(1)}, f32[6,18,1]{2,1,0:T(8,128)S(1)}, u32[]{:S(2)}, u32[]{:S(2)}) collective-permute-start(f32[6,18,1]{2,1,0:T(8,128)S(1)} %get-tuple-element.166), channel_id=1, source_target_pairs={{0,1},{1,2},{2,3},{3,4},{4,5},{5,6},{6,7},{8,9},{9,10},{10,11},{11... | collective-permute-start | bytes 1304 | tf_op jit(solution)/shard_map/ppermute | solution.py:22
  169.2 15.3 %collective-permute-start.35 = (f32[6,18,1]{2,1,0:T(8,128)S(1)}, f32[6,18,1]{2,1,0:T(8,128)S(1)}, u32[]{:S(2)}, u32[]{:S(2)}) collective-permute-start(f32[6,18,1]{2,1,0:T(8,128)S(1)} %get-tuple-element.165), channel_id=1, source_target_pairs={{1,0},{2,1},{3,2},{4,3},{5,4},{6,5},{7,6},{9,8},{10,9},{11,10},{12... | collective-permute-start | bytes 1304 | tf_op jit(solution)/shard_map/ppermute | solution.py:25
  239.0 13.0 %collective-permute-start.51 = (f32[6,1,64]{2,1,0:T(1,128)S(1)}, f32[6,1,64]{2,1,0:T(1,128)S(1)}, u32[]{:S(2)}, u32[]{:S(2)}) collective-permute-start(f32[6,1,64]{2,1,0:T(1,128)S(1)} %get-tuple-element.178), channel_id=1, source_target_pairs={{8,0},{16,8},{24,16},{32,24},{40,32},{48,40},{56,48},{9,1},{17,9},... | collective-permute-start | bytes 4616 | tf_op jit(solution)/shard_map/ppermute | solution.py:25
  241.0 11.1 %collective-permute-start.50 = (f32[6,1,64]{2,1,0:T(1,128)S(1)}, f32[6,1,64]{2,1,0:T(1,128)S(1)}, u32[]{:S(2)}, u32[]{:S(2)}) collective-permute-start(f32[6,1,64]{2,1,0:T(1,128)S(1)} %get-tuple-element.177), channel_id=1, source_target_pairs={{0,8},{8,16},{16,24},{24,32},{32,40},{40,48},{48,56},{1,9},{9,17},... | collective-permute-start | bytes 4616 | tf_op jit(solution)/shard_map/ppermute | solution.py:22
  246.8 19.0 %collective-permute-start.60 = (f32[1,8,32]{2,1,0:T(8,128)S(1)}, f32[1,8,32]{2,1,0:T(8,128)S(1)}, u32[]{:S(2)}, u32[]{:S(2)}) collective-permute-start(f32[1,8,32]{2,1,0:T(8,128)S(1)} %get-tuple-element.258), channel_id=1, source_target_pairs={{0,64},{64,128},{128,192},{1,65},{65,129},{129,193},{2,66},{66,130... | collective-permute-start | bytes 3080 | tf_op jit(solution)/shard_map/ppermute | solution.py:22
  250.7 15.1 %collective-permute-start.61 = (f32[1,8,32]{2,1,0:T(8,128)S(1)}, f32[1,8,32]{2,1,0:T(8,128)S(1)}, u32[]{:S(2)}, u32[]{:S(2)}) collective-permute-start(f32[1,8,32]{2,1,0:T(8,128)S(1)} %get-tuple-element.257), channel_id=1, source_target_pairs={{64,0},{128,64},{192,128},{65,1},{129,65},{193,129},{66,2},{130,66... | collective-permute-start | bytes 3080 | tf_op jit(solution)/shard_map/ppermute | solution.py:25
  259.6 12.0 %collective-permute-start.55 = (f32[1,16,64]{2,1,0:T(8,128)S(1)}, f32[1,16,64]{2,1,0:T(8,128)S(1)}, u32[]{:S(2)}, u32[]{:S(2)}) collective-permute-start(f32[1,16,64]{2,1,0:T(8,128)S(1)} %get-tuple-element.212), channel_id=1, source_target_pairs={{64,0},{128,64},{192,128},{65,1},{129,65},{193,129},{66,2},{130,66... | collective-permute-start | bytes 12296 | tf_op jit(solution)/shard_map/ppermute | solution.py:25
  260.9 10.7 %collective-permute-start.54 = (f32[1,16,64]{2,1,0:T(8,128)S(1)}, f32[1,16,64]{2,1,0:T(8,128)S(1)}, u32[]{:S(2)}, u32[]{:S(2)}) collective-permute-start(f32[1,16,64]{2,1,0:T(8,128)S(1)} %get-tuple-element.211), channel_id=1, source_target_pairs={{0,64},{64,128},{128,192},{1,65},{65,129},{129,193},{2,66},{66,130... | collective-permute-start | bytes 12296 | tf_op jit(solution)/shard_map/ppermute | solution.py:22
  265.9 11.4 %collective-permute-start.62 = (f32[4,1,32]{2,1,0:T(1,128)S(1)}, f32[4,1,32]{2,1,0:T(1,128)S(1)}, u32[]{:S(2)}, u32[]{:S(2)}) collective-permute-start(f32[4,1,32]{2,1,0:T(1,128)S(1)} %get-tuple-element.238), channel_id=1, source_target_pairs={{0,8},{8,16},{16,24},{24,32},{32,40},{40,48},{48,56},{1,9},{9,17},... | collective-permute-start | bytes 1544 | tf_op jit(solution)/shard_map/ppermute | solution.py:22
  278.1 13.0 %collective-permute-start.59 = (f32[6,18,1]{2,1,0:T(8,128)S(1)}, f32[6,18,1]{2,1,0:T(8,128)S(1)}, u32[]{:S(2)}, u32[]{:S(2)}) collective-permute-start(f32[6,18,1]{2,1,0:T(8,128)S(1)} %get-tuple-element.158), channel_id=1, source_target_pairs={{1,0},{2,1},{3,2},{4,3},{5,4},{6,5},{7,6},{9,8},{10,9},{11,10},{12... | collective-permute-start | bytes 1304 | tf_op jit(solution)/shard_map/ppermute | solution.py:25
  279.4 11.7 %collective-permute-start.58 = (f32[6,18,1]{2,1,0:T(8,128)S(1)}, f32[6,18,1]{2,1,0:T(8,128)S(1)}, u32[]{:S(2)}, u32[]{:S(2)}) collective-permute-start(f32[6,18,1]{2,1,0:T(8,128)S(1)} %get-tuple-element.157), channel_id=1, source_target_pairs={{0,1},{1,2},{2,3},{3,4},{4,5},{5,6},{6,7},{8,9},{9,10},{10,11},{11... | collective-permute-start | bytes 1304 | tf_op jit(solution)/shard_map/ppermute | solution.py:22
  302.7 8.4 %collective-permute-start.69 = (f32[4,1,32]{2,1,0:T(1,128)S(1)}, f32[4,1,32]{2,1,0:T(1,128)S(1)}, u32[]{:S(2)}, u32[]{:S(2)}) collective-permute-start(f32[4,1,32]{2,1,0:T(1,128)S(1)} %get-tuple-element.236), channel_id=1, source_target_pairs={{8,0},{16,8},{24,16},{32,24},{40,32},{48,40},{56,48},{9,1},{17,9},... | collective-permute-start | bytes 1544 | tf_op jit(solution)/shard_map/ppermute | solution.py:25
  452.5 11.1 %collective-permute-start.93 = (f32[4,1,32]{2,1,0:T(1,128)S(1)}, f32[4,1,32]{2,1,0:T(1,128)S(1)}, u32[]{:S(2)}, u32[]{:S(2)}) collective-permute-start(f32[4,1,32]{2,1,0:T(1,128)S(1)} %get-tuple-element.228), channel_id=1, source_target_pairs={{8,0},{16,8},{24,16},{32,24},{40,32},{48,40},{56,48},{9,1},{17,9},... | collective-permute-start | bytes 1544 | tf_op jit(solution)/shard_map/ppermute | solution.py:25
  646.9 8.3 %collective-permute-start.143 = (f32[10,34,1]{2,1,0:T(8,128)S(1)}, f32[10,34,1]{2,1,0:T(8,128)S(1)}, u32[]{:S(2)}, u32[]{:S(2)}) collective-permute-start(f32[10,34,1]{2,1,0:T(8,128)S(1)} %get-tuple-element.98), channel_id=1, source_target_pairs={{1,0},{2,1},{3,2},{4,3},{5,4},{6,5},{7,6},{9,8},{10,9},{11,10},{12... | collective-permute-start | bytes 4088 | tf_op jit(solution)/shard_map/ppermute | solution.py:25
  648.2 8.5 %collective-permute-start.142 = (f32[10,34,1]{2,1,0:T(8,128)S(1)}, f32[10,34,1]{2,1,0:T(8,128)S(1)}, u32[]{:S(2)}, u32[]{:S(2)}) collective-permute-start(f32[10,34,1]{2,1,0:T(8,128)S(1)} %get-tuple-element.97), channel_id=1, source_target_pairs={{0,1},{1,2},{2,3},{3,4},{4,5},{5,6},{6,7},{8,9},{9,10},{10,11},{11... | collective-permute-start | bytes 4088 | tf_op jit(solution)/shard_map/ppermute | solution.py:22
  673.7 8.5 %collective-permute-start.148 = (f32[10,34,1]{2,1,0:T(8,128)S(1)}, f32[10,34,1]{2,1,0:T(8,128)S(1)}, u32[]{:S(2)}, u32[]{:S(2)}) collective-permute-start(f32[10,34,1]{2,1,0:T(8,128)S(1)} %get-tuple-element.95), channel_id=1, source_target_pairs={{0,1},{1,2},{2,3},{3,4},{4,5},{5,6},{6,7},{8,9},{9,10},{10,11},{11... | collective-permute-start | bytes 4088 | tf_op jit(solution)/shard_map/ppermute | solution.py:22
  689.2 8.6 %collective-permute-start.153 = (f32[10,1,128]{2,1,0:T(1,128)S(1)}, f32[10,1,128]{2,1,0:T(1,128)S(1)}, u32[]{:S(2)}, u32[]{:S(2)}) collective-permute-start(f32[10,1,128]{2,1,0:T(1,128)S(1)} %get-tuple-element.114), channel_id=1, source_target_pairs={{8,0},{16,8},{24,16},{32,24},{40,32},{48,40},{56,48},{9,1},{17,9},... | collective-permute-start | bytes 15368 | tf_op jit(solution)/shard_map/ppermute | solution.py:25
  700.0 8.5 %collective-permute-start.154 = (f32[10,34,1]{2,1,0:T(8,128)S(1)}, f32[10,34,1]{2,1,0:T(8,128)S(1)}, u32[]{:S(2)}, u32[]{:S(2)}) collective-permute-start(f32[10,34,1]{2,1,0:T(8,128)S(1)} %get-tuple-element.93), channel_id=1, source_target_pairs={{0,1},{1,2},{2,3},{3,4},{4,5},{5,6},{6,7},{8,9},{9,10},{10,11},{11... | collective-permute-start | bytes 4088 | tf_op jit(solution)/shard_map/ppermute | solution.py:22
  725.6 8.5 %collective-permute-start.160 = (f32[10,34,1]{2,1,0:T(8,128)S(1)}, f32[10,34,1]{2,1,0:T(8,128)S(1)}, u32[]{:S(2)}, u32[]{:S(2)}) collective-permute-start(f32[10,34,1]{2,1,0:T(8,128)S(1)} %get-tuple-element.91), channel_id=1, source_target_pairs={{0,1},{1,2},{2,3},{3,4},{4,5},{5,6},{6,7},{8,9},{9,10},{10,11},{11... | collective-permute-start | bytes 4088 | tf_op jit(solution)/shard_map/ppermute | solution.py:22
  749.8 8.5 %collective-permute-start.167 = (f32[10,34,1]{2,1,0:T(8,128)S(1)}, f32[10,34,1]{2,1,0:T(8,128)S(1)}, u32[]{:S(2)}, u32[]{:S(2)}) collective-permute-start(f32[10,34,1]{2,1,0:T(8,128)S(1)} %get-tuple-element.90), channel_id=1, source_target_pairs={{1,0},{2,1},{3,2},{4,3},{5,4},{6,5},{7,6},{9,8},{10,9},{11,10},{12... | collective-permute-start | bytes 4088 | tf_op jit(solution)/shard_map/ppermute | solution.py:25
  751.1 8.6 %collective-permute-start.166 = (f32[10,34,1]{2,1,0:T(8,128)S(1)}, f32[10,34,1]{2,1,0:T(8,128)S(1)}, u32[]{:S(2)}, u32[]{:S(2)}) collective-permute-start(f32[10,34,1]{2,1,0:T(8,128)S(1)} %get-tuple-element.89), channel_id=1, source_target_pairs={{0,1},{1,2},{2,3},{3,4},{4,5},{5,6},{6,7},{8,9},{9,10},{10,11},{11... | collective-permute-start | bytes 4088 | tf_op jit(solution)/shard_map/ppermute | solution.py:22
  (140 other events, 1031.6 us)
where the time goes:
time: 774 us; the launch traced here: 761 us
  starting transfers between devices  557 us (72%)
  waiting for transfers between devices  83.5 us (11%)
  blocking collectives  55.3 us (7%)
  local copies, waits for them, and re-layouts  38.3 us (5%)
  other arithmetic  23.5 us (3%)
    ppermute x84, starting transfers between devices, with_halo(): lax.ppermute(lax.slice_in_dim(block, block.shape[dim] - width, None, axis...  419 us
    ppermute x84, starting transfers between devices, with_halo(): lax.ppermute(lax.slice_in_dim(block, 0, width, axis=dim), axis, backward)  138 us
    ppermute x84, waiting for transfers between devices, with_halo(): lax.ppermute(lax.slice_in_dim(block, block.shape[dim] - width, None, axis...  61.5 us
    reshape x4, local copies, waits for them, and re-layouts, restrict_mean(): blocks = field.reshape(first // 2, 2, second // 2, 2, third // 2, 2)  30.1 us
    all_gather x1, blocking collectives, shards(): packed = lax.all_gather(packed, 'gz', axis=3, tiled=True)  28.5 us
    ppermute x84, waiting for transfers between devices, with_halo(): lax.ppermute(lax.slice_in_dim(block, 0, width, axis=dim), axis, backward)  22 us
    all_gather x1, blocking collectives, shards(): packed = lax.all_gather(packed, 'gy', axis=2, tiled=True)  16.7 us
  transfers between devices with their start and end apart: 168, of which 79 were waited for; matrix products, arithmetic and copies ran while one was open for 6% of the time, Pallas kernels for 0%

commit v1 on v0

--- a/solution.py
+++ b/solution.py
@@ -1,7 +1,14 @@
+import functools
+
 import jax
 import jax.numpy as jnp
 from jax import lax
+from jax.experimental import pallas as pl
+from jax.experimental.pallas import tpu as pltpu
 from jax.sharding import PartitionSpec as P
+
+MESH = pl.DeviceIdType.MESH
+AXES = ("gx", "gy", "gz")
 
 LEVELS = 3
 SWEEPS = 4
@@ -14,17 +21,96 @@
 BOTTOM_LOWER = 0.02
 
 
-def with_halo(block, sides, width):
-    for axis, dim in sides:
-        count = lax.axis_size(axis)
-        forward = [(i, i + 1) for i in range(count - 1)]
-        backward = [(target, source) for source, target in forward]
-        low = lax.ppermute(
-            lax.slice_in_dim(block, block.shape[dim] - width, None, axis=dim), axis, forward
-        )
-        high = lax.ppermute(lax.slice_in_dim(block, 0, width, axis=dim), axis, backward)
-        block = jnp.concatenate([low, block, high], axis=dim)
-    return block
+def halo_kernel(sizes, *refs):
+    sends, halos = refs[0:6], refs[6:12]
+    send_sem, recv_sem = refs[12], refs[13]
+    index = [lax.axis_index(axis) for axis in AXES]
+    targets = []
+    for k in range(6):
+        axis = k // 2
+        if k % 2 == 0:
+            exists = index[axis] > 0
+            other = index[axis] - 1
+        else:
+            exists = index[axis] < sizes[axis] - 1
+            other = index[axis] + 1
+        device = tuple(other if a == axis else index[a] for a in range(3))
+        targets.append((exists, device))
+    barrier = pltpu.get_barrier_semaphore()
+    count = jnp.int32(0)
+    for exists, device in targets:
+
+        @pl.when(exists)
+        def _():
+            pl.semaphore_signal(barrier, inc=1, device_id=device, device_id_type=MESH)
+
+        count = count + exists.astype(jnp.int32)
+    pl.semaphore_wait(barrier, count)
+    copies = []
+    for k, (exists, device) in enumerate(targets):
+        copy = pltpu.make_async_remote_copy(
+            src_ref=sends[k],
+            dst_ref=halos[k ^ 1],
+            send_sem=send_sem.at[k],
+            recv_sem=recv_sem.at[k ^ 1],
+            device_id=device,
+            device_id_type=MESH,
+        )
+        copies.append(copy)
+        pl.when(exists)(copy.start)
+    for k, (exists, device) in enumerate(targets):
+
+        @pl.when(jnp.logical_not(exists))
+        def _():
+            halos[k][...] = jnp.zeros(halos[k].shape, halos[k].dtype)
+
+    for k, (exists, device) in enumerate(targets):
+        incoming = pltpu.make_async_remote_copy(
+            src_ref=sends[k ^ 1],
+            dst_ref=halos[k],
+            send_sem=send_sem.at[k ^ 1],
+            recv_sem=recv_sem.at[k],
+            device_id=device,
+            device_id_type=MESH,
+        )
+        pl.when(exists)(copies[k].wait_send)
+        pl.when(exists)(incoming.wait_recv)
+
+
+SIZES = {}
+
+
+def exchange(faces):
+    shape = faces[0].shape + faces[2].shape + faces[4].shape
+    ident = SIZES.setdefault(shape, len(SIZES))
+    sizes = tuple(lax.axis_size(axis) for axis in AXES)
+    vmem = pl.BlockSpec(memory_space=pltpu.VMEM)
+    return pl.pallas_call(
+        functools.partial(halo_kernel, sizes),
+        out_shape=tuple(jax.ShapeDtypeStruct(f.shape, f.dtype) for f in faces),
+        in_specs=[vmem] * 6,
+        out_specs=tuple([vmem] * 6),
+        scratch_shapes=[pltpu.SemaphoreType.DMA((6,)), pltpu.SemaphoreType.DMA((6,))],
+        compiler_params=pltpu.CompilerParams(collective_id=ident, has_side_effects=True),
+    )(*faces)
+
+
+def neighbours(field):
+    last = [n - 1 for n in field.shape]
+    faces = (
+        field[0], field[last[0]],
+        field[:, 0], field[:, last[1]],
+        field[:, :, 0], field[:, :, last[2]],
+    )
+    halos = exchange(faces)
+    return (
+        jnp.concatenate([halos[0][None], field[:-1]], axis=0),
+        jnp.concatenate([field[1:], halos[1][None]], axis=0),
+        jnp.concatenate([halos[2][:, None], field[:, :-1]], axis=1),
+        jnp.concatenate([field[:, 1:], halos[3][:, None]], axis=1),
+        jnp.concatenate([halos[4][:, :, None], field[:, :, :-1]], axis=2),
+        jnp.concatenate([field[:, :, 1:], halos[5][:, :, None]], axis=2),
+    )
 
 
 def split_padded(padded):
@@ -39,19 +125,15 @@
 
 
 def zero_pad(field):
-    return jnp.pad(field, 1)
-
-
-def rim_iterate(field):
-    return with_halo(field, (("gx", 0), ("gy", 1), ("gz", 2)), 1)
-
-
-def rim_coefficient(field):
-    return with_halo(field, (("gx", 0), ("gy", 1), ("gz", 2)), 1)
-
-
-def level_operator(beta_level, alpha_level, padded_beta, shift):
-    coeffs = tuple((0.5 * (beta_level + other) for other in split_padded(padded_beta)))
+    return split_padded(jnp.pad(field, 1))
+
+
+rim_iterate = neighbours
+rim_coefficient = neighbours
+
+
+def level_operator(beta_level, alpha_level, beta_sides, shift):
+    coeffs = tuple((0.5 * (beta_level + other) for other in beta_sides))
     diagonal = shift * alpha_level
     for coeff in coeffs:
         diagonal = diagonal + coeff
@@ -60,7 +142,7 @@
 
 def apply_operator(field, operator, pad_field):
     coeffs, diagonal = operator
-    others = split_padded(pad_field(field))
+    others = pad_field(field)
     total = coeffs[0] * others[0]
     for index in range(1, 6):
         total = total + coeffs[index] * others[index]

time: 774 us -> 760 us (0.982)
  starting transfers between devices: 557 us -> 0 us
  local copies, waits for them, and re-layouts: 38.3 us -> 428 us
  Pallas kernels: 0 us -> 182 us
  waiting for transfers between devices: 83.5 us -> 0 us
  other arithmetic: 23.5 us -> 86.9 us
  blocking collectives: 55.3 us -> 46 us
    ppermute x168 -> x0, starting transfers between devices: 557 us -> none  [the longest x84 419 us: with_halo(): lax.ppermute(lax.slice_in_dim(block, block.shape[dim] - width, None, axis...]
    pallas_call x0 -> x28, Pallas kernels: none -> 182 us  [exchange(): pl.pallas_call(functools.partial(halo_kernel, sizes), out_shape=tuple((ja...]
    concatenate x1 -> x62, local copies, waits for them, and re-layouts: 0.01 us -> 142 us  [the longest x11 25.1 us: neighbours(): jnp.concatenate([field[1:], halos[1][None]], axis=0)]
    slice x57 -> x175, local copies, waits for them, and re-layouts: 3.41 us -> 122 us  [the longest x28 32.2 us: neighbours(): field[:, last[1]]]
    ppermute x168 -> x0, waiting for transfers between devices: 83.5 us -> none  [the longest x84 61.5 us: with_halo(): lax.ppermute(lax.slice_in_dim(block, block.shape[dim] - width, None, axis...]
    broadcast_in_dim x0 -> x56, local copies, waits for them, and re-layouts: none -> 62.1 us  [the longest x10 17.1 us: neighbours(): halos[2][:, None]]
    add x30, other arithmetic: 6.48 us -> 45.4 us  [chebyshev(): iterate = iterate + update]
    squeeze x0 -> x38, local copies, waits for them, and re-layouts: none -> 26.9 us  [the longest x10 8.02 us: neighbours(): field[:, :, last[2]]]
  transfers between devices with their start and end apart: 168 -> 0, of which waited for: 79 -> 0; matrix products, arithmetic and copies ran while one was open for 6% -> 0% of each run, Pallas kernels for 0% -> 0%
where the time goes in v1:
time: 760 us; the launch traced here: 745 us
  local copies, waits for them, and re-layouts  428 us (56%)
  Pallas kernels  182 us (24%)
  other arithmetic  86.9 us (11%)
  blocking collectives  46 us (6%)
    pallas_call x28, Pallas kernels, exchange(): pl.pallas_call(functools.partial(halo_kernel, sizes), out_shape=tuple((ja...  182 us
    add x30, other arithmetic, chebyshev(): iterate = iterate + update  45.4 us
    slice x28, local copies, waits for them, and re-layouts, neighbours(): field[:, last[1]]  32.2 us
    reshape x3, local copies, waits for them, and re-layouts, restrict_mean(): blocks = field.reshape(first // 2, 2, second // 2, 2, third // 2, 2)  29.4 us
    concatenate x11, local copies, waits for them, and re-layouts, neighbours(): jnp.concatenate([field[1:], halos[1][None]], axis=0)  25.1 us
    concatenate x11, local copies, waits for them, and re-layouts, neighbours(): jnp.concatenate([halos[0][None], field[:-1]], axis=0)  24.3 us
    concatenate x10, local copies, waits for them, and re-layouts, neighbours(): jnp.concatenate([field[:, :, 1:], halos[5][:, :, None]], axis=2)  24.2 us
    concatenate x10, local copies, waits for them, and re-layouts, neighbours(): jnp.concatenate([halos[4][:, :, None], field[:, :, :-1]], axis=2)  22.9 us

profile of v1, /device:TPU:1, one launch (start us, length us, event | category | flops | bytes accessed | tf_op | source)
XLA Modules:
  0.0 744.9 jit_solution(4444837639602102194)
XLA Ops:
  8.6 7.3 shard_map.50
  36.6 6.9 shard_map.51
  69.4 7.9 %shard_map.52 = (f32[32,128]{1,0:T(8,128)}, f32[32,128]{1,0:T(8,128)}, f32[8,128]{1,0:T(8,128)}, f32[8,128]{1,0:T(8,128)}, f32[8,32]{1,0:T(8,128)}, /*index=5*/f32[8,32]{1,0:T(8,128)}) custom-call(f32[32,128]{1,0:T(8,128)} %copy.1207.refs_0_, f32[32,128]{1,0:T(8,128)} %copy.1208.refs_1_, f32[8,128]{1,0:T(8,128)} %bitcast.613, f32[8,128]{1,0:T(8,128)} %bitcast.622, ...), custom_call_target="tpu_custom_call" | custom-call | tf_op jit(solution)/shard_map/pallas_call | solution.py:88
  102.5 6.3 shard_map.53
  124.9 9.8 %reshape.226 = f32[4,2,16,2,64,2]{5,4,3,2,1,0:T(8,128)} reshape(f32[8,32,128]{2,1,0:T(8,128)S(1)} %copy-done.13) | data formatting | bytes 262144 | tf_op jit(solution)/shard_map/reshape | solution.py:175
  146.6 6.3 shard_map.54
  164.3 9.8 %reshape.225 = f32[4,2,16,2,64,2]{5,4,3,2,1,0:T(8,128)} reshape(f32[8,32,128]{2,1,0:T(8,128)S(1)} %copy.1232) | data formatting | bytes 262144 | tf_op jit(solution)/shard_map/reshape | solution.py:175
  178.2 9.8 %reshape.227 = f32[4,2,16,2,64,2]{5,4,3,2,1,0:T(8,128)} reshape(f32[8,32,128]{2,1,0:T(8,128)S(1)} %copy-done.12) | data formatting | bytes 262144 | tf_op jit(solution)/shard_map/reshape | solution.py:175
  194.7 6.3 shard_map.55
  206.9 6.3 shard_map.56
  218.9 6.2 shard_map.57
  231.0 6.2 shard_map.58
  246.9 6.2 shard_map.59
  419.0 6.2 shard_map.60
  429.5 6.2 shard_map.61
  440.1 6.2 shard_map.62
  461.6 6.2 shard_map.64
  470.4 8.4 %all_gather.9 = f32[3,4,4,16]{3,2,1,0:T(4,128)S(1)} all-gather(f32[3,1,4,16]{3,2,1,0:T(4,128)S(1)} %pad_maximum_fusion.32), channel_id=1, replica_groups=mesh['gx'=4,'gy'=8,'gz'=8] {'gx'}, dimensions={1}, use_global_device_ids=true | all-gather | bytes 3840 | tf_op jit(solution)/shard_map/all_gather | solution.py:216
  478.9 16.5 %all_gather.10 = f32[3,4,32,16]{3,1,0,2:T(4,128)S(1)} all-gather(f32[3,4,4,16]{3,1,0,2:T(4,128)S(1)} %copy.1353), channel_id=1, replica_groups=mesh['gx'=4,'gy'=8,'gz'=8] {'gy'}, dimensions={2}, use_global_device_ids=true | all-gather | bytes 27648 | tf_op jit(solution)/shard_map/all_gather | solution.py:217
  495.5 21.1 %all_gather.11 = f32[3,4,32,128]{2,1,0,3:T(4,128)S(1)} all-gather(f32[3,4,32,16]{2,1,0,3:T(4,128)S(1)} %copy.1354), channel_id=1, replica_groups=mesh['gx'=4,'gy'=8,'gz'=8] {'gz'}, dimensions={3}, use_global_device_ids=true | all-gather | bytes 221184 | tf_op jit(solution)/shard_map/all_gather | solution.py:218
  528.3 10.1 %shard_map.65 = (f32[8,32]{1,0:T(8,128)}, f32[8,32]{1,0:T(8,128)}, f32[2,32]{1,0:T(2,128)}, f32[2,32]{1,0:T(2,128)}, f32[2,8]{1,0:T(2,128)}, /*index=5*/f32[2,8]{1,0:T(2,128)}) custom-call(f32[8,32]{1,0:T(8,128)} %get-tuple-element.732.refs_0_, f32[8,32]{1,0:T(8,128)} %get-tuple-element.734.refs_1_, f32[2,32]{1,0:T(2,128)} %bitcast.744, f32[2,32]{1,0:T(2,128)} %bitcast.743, ...), custom_call_target="tpu_custom_call" | custom-call | tf_op jit(solution)/shard_map/pallas_call | solution.py:88
  542.8 6.2 shard_map.66
  553.3 6.2 shard_map.67
  575.5 6.3 shard_map.69
  586.9 6.3 shard_map.70
  598.4 6.3 shard_map.71
  609.9 6.3 shard_map.72
  624.7 6.3 shard_map.73
  649.4 6.4 shard_map.74
  674.2 6.3 shard_map.75
  699.1 6.3 shard_map.76
  726.3 6.3 shard_map.77
  (514 shorter events, 497.6 us)
Async XLA Ops:
  4.1 19.2 %copy-start.11 = (f32[8,32,128]{1,0,2:T(8,128)}, f32[8,32,128]{1,0,2:T(8,128)S(1)}, u32[]{:S(2)}) copy-start(f32[8,32,128]{1,0,2:T(8,128)S(1)} %copy.1181) | copy-start | bytes 393220
  27.1 0.8 copy-start.7
  27.1 62.2 %copy-start.6 = (f32[8,32,128]{1,0,2:T(8,128)}, f32[8,32,128]{1,0,2:T(8,128)S(1)}, u32[]{:S(2)}) copy-start(f32[8,32,128]{1,0,2:T(8,128)S(1)} %get-tuple-element.462) | copy-start | bytes 393220
  27.1 132.1 %copy-start.4 = (f32[8,32,128]{1,0,2:T(8,128)}, f32[8,32,128]{1,0,2:T(8,128)S(1)}, u32[]{:S(2)}) copy-start(f32[8,32,128]{1,0,2:T(8,128)S(1)} %get-tuple-element.461) | copy-start | bytes 393220
  27.1 612.2 %copy-start = (f32[8,32,128]{1,0,2:T(8,128)}, f32[8,32,128]{1,0,2:T(8,128)S(1)}, u32[]{:S(2)}) copy-start(f32[8,32,128]{1,0,2:T(8,128)S(1)} %get-tuple-element.460) | copy-start | bytes 393220
  59.8 0.8 copy-start.8
  89.2 30.5 %copy-start.22 = (f32[8,32]{1,0:T(8,128)S(1)}, f32[8,32]{1,0:T(8,128)}, u32[]{:S(2)}) copy-start(f32[8,32]{1,0:T(8,128)} %get-tuple-element.186) | copy-start | bytes 3076
  89.3 30.5 %copy-start.23 = (f32[8,32]{1,0:T(8,128)S(1)}, f32[8,32]{1,0:T(8,128)}, u32[]{:S(2)}) copy-start(f32[8,32]{1,0:T(8,128)} %get-tuple-element.187) | copy-start | bytes 3076
  93.0 0.8 copy-start.9
  93.9 23.9 %copy-start.10 = (f32[8,32,128]{1,0,2:T(8,128)S(1)}, f32[8,32,128]{1,0,2:T(8,128)}, u32[]{:S(2)}) copy-start(f32[8,32,128]{1,0,2:T(8,128)} %copy-done.9) | copy-start | bytes 393220
  116.9 8.0 %copy-start.13 = (f32[8,32,128]{2,1,0:T(8,128)S(1)}, f32[8,32,128]{2,1,0:T(8,128)}, u32[]{:S(2)}) copy-start(f32[8,32,128]{2,1,0:T(8,128)} %param.4) | copy-start | bytes 393220
  164.3 13.8 %copy-start.12 = (f32[8,32,128]{2,1,0:T(8,128)S(1)}, f32[8,32,128]{2,1,0:T(8,128)}, u32[]{:S(2)}) copy-start(f32[8,32,128]{2,1,0:T(8,128)} %param.5) | copy-start | bytes 393220
  279.9 39.4 %copy-start.21 = (f32[4,16,64]{2,0,1:T(4,128)S(1)}, f32[4,16,64]{2,0,1:T(4,128)}, u32[]{:S(2)}) copy-start(f32[4,16,64]{2,0,1:T(4,128)} %get-tuple-element.435) | copy-start | bytes 49156
  285.0 38.9 %copy-start.27 = (f32[4,64]{1,0:T(4,128)S(1)}, f32[4,64]{1,0:T(4,128)}, u32[]{:S(2)}) copy-start(f32[4,64]{1,0:T(4,128)} %get-tuple-element.215) | copy-start | bytes 3076
  290.2 38.1 %copy-start.26 = (f32[4,64]{1,0:T(4,128)S(1)}, f32[4,64]{1,0:T(4,128)}, u32[]{:S(2)}) copy-start(f32[4,64]{1,0:T(4,128)} %get-tuple-element.214) | copy-start | bytes 3076
  311.9 36.2 %copy-start.20 = (f32[4,16,64]{2,0,1:T(4,128)S(1)}, f32[4,16,64]{2,0,1:T(4,128)}, u32[]{:S(2)}) copy-start(f32[4,16,64]{2,0,1:T(4,128)} %get-tuple-element.441) | copy-start | bytes 49156
  317.0 35.4 %copy-start.25 = (f32[4,64]{1,0:T(4,128)S(1)}, f32[4,64]{1,0:T(4,128)}, u32[]{:S(2)}) copy-start(f32[4,64]{1,0:T(4,128)} %get-tuple-element.209) | copy-start | bytes 3076
  321.4 35.4 %copy-start.24 = (f32[4,64]{1,0:T(4,128)S(1)}, f32[4,64]{1,0:T(4,128)}, u32[]{:S(2)}) copy-start(f32[4,64]{1,0:T(4,128)} %get-tuple-element.208) | copy-start | bytes 3076
  326.0 35.2 %copy-start.19 = (f32[4,16,64]{2,0,1:T(4,128)S(1)}, f32[4,16,64]{2,0,1:T(4,128)}, u32[]{:S(2)}) copy-start(f32[4,16,64]{2,0,1:T(4,128)} %get-tuple-element.440) | copy-start | bytes 49156
  330.4 35.2 %copy-start.18 = (f32[4,16,64]{2,0,1:T(4,128)S(1)}, f32[4,16,64]{2,0,1:T(4,128)}, u32[]{:S(2)}) copy-start(f32[4,16,64]{2,0,1:T(4,128)} %get-tuple-element.439) | copy-start | bytes 49156
  372.0 37.7 %copy-start.14 = (f32[2,2,8,2,32,2]{4,2,5,3,1,0:T(8,128)S(1)}, f32[2,2,8,2,32,2]{4,2,5,3,1,0:T(8,128)}, u32[]{:S(2)}) copy-start(f32[2,2,8,2,32,2]{4,2,5,3,1,0:T(8,128)} %copy.1319) | copy-start | bytes 49156
  372.0 37.7 %copy-start.15 = (f32[2,2,8,2,32,2]{4,2,5,3,1,0:T(8,128)S(1)}, f32[2,2,8,2,32,2]{4,2,5,3,1,0:T(8,128)}, u32[]{:S(2)}) copy-start(f32[2,2,8,2,32,2]{4,2,5,3,1,0:T(8,128)} %copy.1317) | copy-start | bytes 49156
  372.0 37.7 %copy-start.16 = (f32[2,2,8,2,32,2]{4,2,5,3,1,0:T(8,128)S(1)}, f32[2,2,8,2,32,2]{4,2,5,3,1,0:T(8,128)}, u32[]{:S(2)}) copy-start(f32[2,2,8,2,32,2]{4,2,5,3,1,0:T(8,128)} %copy.1312) | copy-start | bytes 49156
  372.0 37.7 %copy-start.17 = (f32[2,2,8,2,32,2]{4,2,5,3,1,0:T(8,128)S(1)}, f32[2,2,8,2,32,2]{4,2,5,3,1,0:T(8,128)}, u32[]{:S(2)}) copy-start(f32[2,2,8,2,32,2]{4,2,5,3,1,0:T(8,128)} %copy.1310) | copy-start | bytes 49156
  643.7 20.3 %copy-start.1 = (f32[8,32,128]{1,0,2:T(8,128)S(1)}, f32[8,32,128]{1,0,2:T(8,128)}, u32[]{:S(2)}) copy-start(f32[8,32,128]{1,0,2:T(8,128)} %copy-done) | copy-start | bytes 393220
  668.6 20.2 %copy-start.2 = (f32[8,32,128]{1,0,2:T(8,128)S(1)}, f32[8,32,128]{1,0,2:T(8,128)}, u32[]{:S(2)}) copy-start(f32[8,32,128]{1,0,2:T(8,128)} %copy-done) | copy-start | bytes 393220
  693.4 20.2 %copy-start.3 = (f32[8,32,128]{1,0,2:T(8,128)S(1)}, f32[8,32,128]{1,0,2:T(8,128)}, u32[]{:S(2)}) copy-start(f32[8,32,128]{1,0,2:T(8,128)} %copy-done) | copy-start | bytes 393220
  717.5 21.3 %copy-start.5 = (f32[8,32,128]{1,0,2:T(8,128)S(1)}, f32[8,32,128]{1,0,2:T(8,128)}, u32[]{:S(2)}) copy-start(f32[8,32,128]{1,0,2:T(8,128)} %copy-done.4) | copy-start | bytes 393220

commit v2 on v0

--- a/solution.py
+++ b/solution.py
@@ -1,7 +1,14 @@
+import functools
+
 import jax
 import jax.numpy as jnp
 from jax import lax
+from jax.experimental import pallas as pl
+from jax.experimental.pallas import tpu as pltpu
 from jax.sharding import PartitionSpec as P
+
+MESH = pl.DeviceIdType.MESH
+AXES = ("gx", "gy", "gz")
 
 LEVELS = 3
 SWEEPS = 4
@@ -14,17 +21,185 @@
 BOTTOM_LOWER = 0.02
 
 
-def with_halo(block, sides, width):
-    for axis, dim in sides:
-        count = lax.axis_size(axis)
-        forward = [(i, i + 1) for i in range(count - 1)]
-        backward = [(target, source) for source, target in forward]
-        low = lax.ppermute(
-            lax.slice_in_dim(block, block.shape[dim] - width, None, axis=dim), axis, forward
+def level_kernel(cfg, *refs):
+    sizes, shift, count, lower, zero_start, residual = cfg
+    n_in = 3 if zero_start else 4
+    b_ref, beta_ref, alpha_ref = refs[0:3]
+    v0_ref = None if zero_start else refs[3]
+    outs = refs[n_in : n_in + (2 if residual else 1)]
+    fld, xh, yzh, coef, dbuf, send_sem, recv_sem = refs[n_in + len(outs) :]
+    A, B, C = b_ref.shape
+    index = [lax.axis_index(axis) for axis in AXES]
+    targets = []
+    for k in range(6):
+        axis = k // 2
+        if k % 2 == 0:
+            exists = index[axis] > 0
+            other = index[axis] - 1
+        else:
+            exists = index[axis] < sizes[axis] - 1
+            other = index[axis] + 1
+        device = tuple(other if a == axis else index[a] for a in range(3))
+        targets.append((exists, device))
+
+    def halo(h, slot):
+        return xh.at[h, slot] if h < 2 else yzh.at[h - 2, slot]
+
+    barrier = pltpu.get_barrier_semaphore()
+    total = jnp.int32(0)
+    for exists, device in targets:
+
+        @pl.when(exists)
+        def _():
+            pl.semaphore_signal(barrier, inc=1, device_id=device, device_id_type=MESH)
+
+        total = total + exists.astype(jnp.int32)
+    for h, (exists, device) in enumerate(targets):
+
+        @pl.when(jnp.logical_not(exists))
+        def _():
+            for slot in range(2):
+                buf = halo(h, slot)
+                buf[...] = jnp.zeros(buf.shape, buf.dtype)
+
+    pl.semaphore_wait(barrier, total)
+
+    def exchange(src, slot):
+        sources = (src.at[0], src.at[A - 1], src, src, src, src)
+        copies = []
+        for k, (exists, device) in enumerate(targets):
+            copy = pltpu.make_async_remote_copy(
+                src_ref=sources[k],
+                dst_ref=halo(k ^ 1, slot),
+                send_sem=send_sem.at[k],
+                recv_sem=recv_sem.at[slot, k ^ 1],
+                device_id=device,
+                device_id_type=MESH,
+            )
+            copies.append(copy)
+            pl.when(exists)(copy.start)
+        for k, (exists, device) in enumerate(targets):
+            incoming = pltpu.make_async_remote_copy(
+                src_ref=sources[k ^ 1],
+                dst_ref=halo(k, slot),
+                send_sem=send_sem.at[k ^ 1],
+                recv_sem=recv_sem.at[slot, k],
+                device_id=device,
+                device_id_type=MESH,
+            )
+            pl.when(exists)(copies[k].wait_send)
+            pl.when(exists)(incoming.wait_recv)
+
+    rows = lax.broadcasted_iota(jnp.int32, (B, C), 0)
+    cols = lax.broadcasted_iota(jnp.int32, (B, C), 1)
+
+    def sides(src, i, slot):
+        here = src[i]
+        lower_x = src[i - 1] if i > 0 else xh[0, slot]
+        upper_x = src[i + 1] if i < A - 1 else xh[1, slot]
+        lower_y = jnp.where(rows == 0, pltpu.roll(yzh[0, slot, i], 1, 0), pltpu.roll(here, 1, 0))
+        upper_y = jnp.where(
+            rows == B - 1, pltpu.roll(yzh[1, slot, i], B - 1, 0), pltpu.roll(here, B - 1, 0)
         )
-        high = lax.ppermute(lax.slice_in_dim(block, 0, width, axis=dim), axis, backward)
-        block = jnp.concatenate([low, block, high], axis=dim)
-    return block
+        lower_z = jnp.where(cols == 0, pltpu.roll(yzh[2, slot, i], 1, 1), pltpu.roll(here, 1, 1))
+        upper_z = jnp.where(
+            cols == C - 1, pltpu.roll(yzh[3, slot, i], C - 1, 1), pltpu.roll(here, C - 1, 1)
+        )
+        return here, (lower_x, upper_x, lower_y, upper_y, lower_z, upper_z)
+
+    exchanges = [0]
+
+    def next_slot():
+        slot = exchanges[0] % 2
+        exchanges[0] += 1
+        return slot
+
+    slot = next_slot()
+    exchange(beta_ref, slot)
+    for i in range(A):
+        here, others = sides(beta_ref, i, slot)
+        diagonal = shift * alpha_ref[i]
+        for k in range(6):
+            face = 0.5 * (here + others[k])
+            coef[k, i] = face
+            diagonal = diagonal + face
+        coef[6, i] = diagonal
+
+    def apply_rows(src, slot, i):
+        here, others = sides(src, i, slot)
+        acc = coef[0, i] * others[0]
+        for k in range(1, 6):
+            acc = acc + coef[k, i] * others[k]
+        return b_ref[i] - (coef[6, i] * here - acc)
+
+    center = (UPPER_EIG + lower) / 2.0
+    half_width = (UPPER_EIG - lower) / 2.0
+    sigma_ratio = center / half_width
+    rho_old = 1.0 / sigma_ratio
+    current = 0
+    if zero_start:
+        for i in range(A):
+            update = b_ref[i] / coef[6, i] / center
+            dbuf[i] = update
+            fld[current, i] = update
+    else:
+        slot = next_slot()
+        exchange(v0_ref, slot)
+        for i in range(A):
+            remain = apply_rows(v0_ref, slot, i)
+            update = remain / coef[6, i] / center
+            dbuf[i] = update
+            fld[current, i] = v0_ref[i] + update
+    for sweep in range(count - 1):
+        rho_new = 1.0 / (2.0 * sigma_ratio - rho_old)
+        slot = next_slot()
+        src = fld.at[current]
+        exchange(src, slot)
+        last = sweep == count - 2
+        dst = outs[0] if last else fld.at[1 - current]
+        for i in range(A):
+            remain = apply_rows(src, slot, i)
+            update = (rho_new * rho_old) * dbuf[i] + (2.0 * rho_new / half_width) * (
+                remain / coef[6, i]
+            )
+            dbuf[i] = update
+            dst[i] = src[i] + update
+        rho_old = rho_new
+        current = 1 - current
+    if residual:
+        slot = next_slot()
+        exchange(outs[0], slot)
+        for i in range(A):
+            outs[1][i] = apply_rows(outs[0], slot, i)
+
+
+KERNELS = {}
+
+
+def smooth(level_args, shift, count, lower, zero_start, residual):
+    A, B, C = level_args[0].shape
+    sizes = tuple(lax.axis_size(axis) for axis in AXES)
+    cfg = (sizes, shift, count, lower, zero_start, residual)
+    ident = KERNELS.setdefault((A, B, C) + cfg[1:], len(KERNELS))
+    vmem = pl.BlockSpec(memory_space=pltpu.VMEM)
+    block = jax.ShapeDtypeStruct((A, B, C), jnp.float32)
+    n_out = 2 if residual else 1
+    return pl.pallas_call(
+        functools.partial(level_kernel, cfg),
+        out_shape=tuple([block] * n_out),
+        in_specs=[vmem] * len(level_args),
+        out_specs=tuple([vmem] * n_out),
+        scratch_shapes=[
+            pltpu.VMEM((2, A, B, C), jnp.float32),
+            pltpu.VMEM((2, 2, B, C), jnp.float32),
+            pltpu.VMEM((4, 2, A, B, C), jnp.float32),
+            pltpu.VMEM((7, A, B, C), jnp.float32),
+            pltpu.VMEM((A, B, C), jnp.float32),
+            pltpu.SemaphoreType.DMA((6,)),
+            pltpu.SemaphoreType.DMA((2, 6)),
+        ],
+        compiler_params=pltpu.CompilerParams(collective_id=ident, has_side_effects=True),
+    )(*level_args)
 
 
 def split_padded(padded):
@@ -39,19 +214,11 @@
 
 
 def zero_pad(field):
-    return jnp.pad(field, 1)
-
-
-def rim_iterate(field):
-    return with_halo(field, (("gx", 0), ("gy", 1), ("gz", 2)), 1)
-
-
-def rim_coefficient(field):
-    return with_halo(field, (("gx", 0), ("gy", 1), ("gz", 2)), 1)
-
-
-def level_operator(beta_level, alpha_level, padded_beta, shift):
-    coeffs = tuple((0.5 * (beta_level + other) for other in split_padded(padded_beta)))
+    return split_padded(jnp.pad(field, 1))
+
+
+def level_operator(beta_level, alpha_level, beta_sides, shift):
+    coeffs = tuple((0.5 * (beta_level + other) for other in beta_sides))
     diagonal = shift * alpha_level
     for coeff in coeffs:
         diagonal = diagonal + coeff
@@ -60,7 +227,7 @@
 
 def apply_operator(field, operator, pad_field):
     coeffs, diagonal = operator
-    others = split_padded(pad_field(field))
+    others = pad_field(field)
     total = coeffs[0] * others[0]
     for index in range(1, 6):
         total = total + coeffs[index] * others[index]
@@ -104,25 +271,17 @@
     for level in range(LEVELS):
         betas.append(restrict_mean(betas[-1]))
         alphas.append(restrict_mean(alphas[-1]))
-    operators = []
-    for level in range(LEVELS):
-        padded_beta = rim_coefficient(betas[level])
-        operators.append(
-            level_operator(betas[level], alphas[level], padded_beta, SHIFT_BASE * 4.0**level)
-        )
     rhs_levels = [right_side]
     smoothed = []
     for level in range(LEVELS):
-        iterate = chebyshev(
-            jnp.zeros_like(rhs_levels[level]),
-            rhs_levels[level],
-            operators[level],
+        iterate, remain = smooth(
+            (rhs_levels[level], betas[level], alphas[level]),
+            SHIFT_BASE * 4.0**level,
             SWEEPS,
             SMOOTH_LOWER,
             True,
-            rim_iterate,
+            True,
         )
-        remain = rhs_levels[level] - apply_operator(iterate, operators[level], rim_iterate)
         smoothed.append(iterate)
         rhs_levels.append(4.0 * restrict_mean(remain))
     coarse_rhs = rhs_levels[LEVELS]
@@ -147,16 +306,16 @@
     correction = lax.dynamic_slice(whole_correction, starts, local_shape)
     for level in range(LEVELS - 1, -1, -1):
         start_field = smoothed[level] + prolong_copy(correction)
-        correction = chebyshev(
-            start_field,
-            rhs_levels[level],
-            operators[level],
+        outs = smooth(
+            (rhs_levels[level], betas[level], alphas[level], start_field),
+            SHIFT_BASE * 4.0**level,
             SWEEPS,
             SMOOTH_LOWER,
             False,
-            rim_iterate,
+            level == 0,
         )
-    residual_field = right_side - apply_operator(correction, operators[0], rim_iterate)
+        correction = outs[0]
+    residual_field = outs[1]
     return (correction, residual_field)
 
 

time: 774 us -> 264 us (0.34); the launches traced: 761 us -> 264 us
  starting transfers between devices: 557 us -> 0 us
  Pallas kernels: 0 us -> 155 us
  waiting for transfers between devices: 83.5 us -> 0 us
  blocking collectives: 55.3 us -> 46.3 us
    ppermute x168 -> x0, starting transfers between devices: 557 us -> none  [the longest x84 419 us: with_halo(): lax.ppermute(lax.slice_in_dim(block, block.shape[dim] - width, None, axis...]
    pallas_call x0 -> x6, Pallas kernels: none -> 155 us  [smooth(): pl.pallas_call(functools.partial(level_kernel, cfg), out_shape=tuple([blo...]
    ppermute x168 -> x0, waiting for transfers between devices: 83.5 us -> none  [the longest x84 61.5 us: with_halo(): lax.ppermute(lax.slice_in_dim(block, block.shape[dim] - width, None, axis...]
  transfers between devices with their start and end apart: 168 -> 0, of which waited for: 79 -> 0; matrix products, arithmetic and copies ran while one was open for 6% -> 0% of each run, Pallas kernels for 0% -> 0%
where the time goes in v2:
time: 264 us
  Pallas kernels  155 us (59%)
  blocking collectives  46.3 us (18%)
  local copies, waits for them, and re-layouts  41 us (16%)
  other arithmetic  20 us (8%)
    pallas_call x6, Pallas kernels, smooth(): pl.pallas_call(functools.partial(level_kernel, cfg), out_shape=tuple([blo...  155 us
    reshape x4, local copies, waits for them, and re-layouts, restrict_mean(): blocks = field.reshape(first // 2, 2, second // 2, 2, third // 2, 2)  31.8 us
    all_gather x1, blocking collectives, shards(): packed = lax.all_gather(packed, 'gz', axis=3, tiled=True)  20.8 us
    all_gather x1, blocking collectives, shards(): packed = lax.all_gather(packed, 'gy', axis=2, tiled=True)  16.9 us
    reduce_sum x11, other arithmetic, restrict_mean(): return jnp.sum(blocks, axis=(1, 3, 5)) * 0.125  14.1 us
    all_gather x1, blocking collectives, shards(): packed = lax.all_gather(packed, 'gx', axis=1, tiled=True)  8.56 us

profile of v2, /device:TPU:1, one launch (start us, length us, event | category | flops | bytes accessed | tf_op | source)
XLA Modules:
  0.0 263.6 jit_solution(9778175724545603117)
XLA Ops:
  0.6 31.9 %shard_map.50 = (f32[8,32,128]{2,1,0:T(8,128)}, f32[8,32,128]{2,1,0:T(8,128)}) custom-call(f32[8,32,128]{2,1,0:T(8,128)} %refs_0_.3, f32[8,32,128]{2,1,0:T(8,128)} %refs_1_.3, f32[8,32,128]{2,1,0:T(8,128)} %refs_2_.3), custom_call_target="tpu_custom_call" | custom-call | tf_op jit(solution)/shard_map/pallas_call | solution.py:187
  32.5 10.5 %reshape.97 = f32[4,2,16,2,64,2]{5,4,3,2,1,0:T(8,128)} reshape(f32[8,32,128]{2,1,0:T(8,128)} %get-tuple-element.9) | data formatting | bytes 262144 | tf_op jit(solution)/shard_map/reshape | solution.py:260
  43.0 4.0 %reduce_sum.102 = f32[4,16,64]{2,1,0:T(8,128)S(1)} reduce(f32[4,2,16,2,64,2]{5,4,3,2,1,0:T(8,128)} %reshape.97, f32[]{:T(128)} %constant.35.clone.1), dimensions={1,3,5}, to_apply=%region_0.0 | reduce | flops 28672 | bytes 147460 | tf_op jit(solution)/shard_map/reduce_sum | solution.py:261
  47.1 0.6 broadcast_multiply_fusion.3.refs_0_
  47.7 9.7 %reshape.98 = f32[4,2,16,2,64,2]{5,4,3,2,1,0:T(8,128)} reshape(f32[8,32,128]{2,1,0:T(8,128)S(1)} %copy-done) | data formatting | bytes 262144 | tf_op jit(solution)/shard_map/reshape | solution.py:260
  57.4 4.0 %reduce_sum.103 = f32[4,16,64]{2,1,0:T(8,128)S(1)} reduce(f32[4,2,16,2,64,2]{5,4,3,2,1,0:T(8,128)} %reshape.98, f32[]{:T(128)} %constant.35.clone.1), dimensions={1,3,5}, to_apply=%region_1.0 | reduce | flops 28672 | bytes 147460 | tf_op jit(solution)/shard_map/reduce_sum | solution.py:261
  61.4 0.6 broadcast_multiply_fusion.2.refs_1_
  62.0 9.7 %reshape.99 = f32[4,2,16,2,64,2]{5,4,3,2,1,0:T(8,128)} reshape(f32[8,32,128]{2,1,0:T(8,128)S(1)} %copy-done.1) | data formatting | bytes 262144 | tf_op jit(solution)/shard_map/reshape | solution.py:260
  71.8 4.0 %reduce_sum.104 = f32[4,16,64]{2,1,0:T(8,128)S(1)} reduce(f32[4,2,16,2,64,2]{5,4,3,2,1,0:T(8,128)} %reshape.99, f32[]{:T(128)} %constant.35.clone.1), dimensions={1,3,5}, to_apply=%region_2.0 | reduce | flops 28672 | bytes 147460 | tf_op jit(solution)/shard_map/reduce_sum | solution.py:261
  75.8 0.6 broadcast_multiply_fusion.1.refs_2_
  76.4 22.1 %shard_map.51 = (f32[4,16,64]{2,1,0:T(8,128)}, f32[4,16,64]{2,1,0:T(8,128)}) custom-call(f32[4,16,64]{2,1,0:T(8,128)} %broadcast_multiply_fusion.3.refs_0_, f32[4,16,64]{2,1,0:T(8,128)} %broadcast_multiply_fusion.2.refs_1_, f32[4,16,64]{2,1,0:T(8,128)} %broadcast_multiply_fusion.1.refs_2_), custom_call_target="tpu_custom_call" | custom-call | tf_op jit(solution)/shard_map/pallas_call | solution.py:187
  98.5 1.8 reshape.100
  100.5 0.6 broadcast_multiply_fusion.6.refs_0_
  101.1 1.1 mul.481
  102.3 1.8 mul.483
  104.3 0.6 fusion.180
  104.9 20.5 %shard_map.52 = (f32[2,8,32]{2,1,0:T(8,128)}, f32[2,8,32]{2,1,0:T(8,128)}) custom-call(f32[2,8,32]{2,1,0:T(8,128)} %broadcast_multiply_fusion.6.refs_0_, f32[2,8,32]{2,1,0:T(8,128)} %get-tuple-element.47.refs_1_, f32[2,8,32]{2,1,0:T(8,128)} %get-tuple-element.50.refs_2_), custom_call_target="tpu_custom_call" | custom-call | tf_op jit(solution)/shard_map/pallas_call | solution.py:187
  125.8 0.7 reduce_sum.108
  126.8 8.6 %all_gather.9 = f32[3,4,4,16]{3,2,1,0:T(4,128)S(1)} all-gather(f32[3,1,4,16]{3,2,1,0:T(4,128)S(1)} %pad_maximum_fusion), channel_id=1, replica_groups=mesh['gx'=4,'gy'=8,'gz'=8] {'gx'}, dimensions={1}, use_global_device_ids=true | all-gather | bytes 3840 | tf_op jit(solution)/shard_map/all_gather | solution.py:293
  135.3 16.9 %all_gather.10 = f32[3,4,32,16]{3,1,0,2:T(4,128)S(1)} all-gather(f32[3,4,4,16]{3,1,0,2:T(4,128)S(1)} %copy.30), channel_id=1, replica_groups=mesh['gx'=4,'gy'=8,'gz'=8] {'gy'}, dimensions={2}, use_global_device_ids=true | all-gather | bytes 27648 | tf_op jit(solution)/shard_map/all_gather | solution.py:294
  152.4 20.8 %all_gather.11 = f32[3,4,32,128]{2,1,0,3:T(4,128)S(1)} all-gather(f32[3,4,32,16]{2,1,0,3:T(4,128)S(1)} %copy.31), channel_id=1, replica_groups=mesh['gx'=4,'gy'=8,'gz'=8] {'gz'}, dimensions={3}, use_global_device_ids=true | all-gather | bytes 221184 | tf_op jit(solution)/shard_map/all_gather | solution.py:295
  175.5 0.6 broadcast_add_fusion.refs_3_
  176.1 24.2 %shard_map.53 = f32[2,8,32]{2,1,0:T(8,128)} custom-call(f32[2,8,32]{2,1,0:T(8,128)} %broadcast_multiply_fusion.6.refs_0_, f32[2,8,32]{2,1,0:T(8,128)} %get-tuple-element.47.refs_1_, f32[2,8,32]{2,1,0:T(8,128)} %get-tuple-element.50.refs_2_, f32[2,8,32]{2,1,0:T(8,128)} %broadcast_add_fusion.refs_3_), custom_call_target="tpu_custom_call" | custom-call | tf_op jit(solution)/shard_map/pallas_call | solution.py:187
  200.3 0.7 broadcast_in_dim.36
  201.3 0.6 add.402.refs_3_
  201.9 22.0 %shard_map.54 = f32[4,16,64]{2,1,0:T(8,128)} custom-call(f32[4,16,64]{2,1,0:T(8,128)} %broadcast_multiply_fusion.3.refs_0_, f32[4,16,64]{2,1,0:T(8,128)} %broadcast_multiply_fusion.2.refs_1_, f32[4,16,64]{2,1,0:T(8,128)} %broadcast_multiply_fusion.1.refs_2_, f32[4,16,64]{2,1,0:T(8,128)} %add.402.refs_3_), custom_call_target="tpu_custom_call" | custom-call | tf_op jit(solution)/shard_map/pallas_call | solution.py:187
  223.9 0.8 copy.39
  225.0 0.2 copy.41
  225.2 0.7 add.403.refs_3_
  225.9 34.6 %shard_map.55 = (f32[8,32,128]{2,1,0:T(8,128)}, f32[8,32,128]{2,1,0:T(8,128)}) custom-call(f32[8,32,128]{2,1,0:T(8,128)} %refs_0_.3, f32[8,32,128]{2,1,0:T(8,128)} %refs_1_.3, f32[8,32,128]{2,1,0:T(8,128)} %refs_2_.3, f32[8,32,128]{2,1,0:T(8,128)} %add.403.refs_3_), custom_call_target="tpu_custom_call" | custom-call | tf_op jit(solution)/shard_map/pallas_call | solution.py:187
  260.4 1.6 copy.47
  262.0 1.6 copy.48
  (56 shorter events, 3.8 us)
Async XLA Ops:
  32.5 15.2 %copy-start = (f32[8,32,128]{2,1,0:T(8,128)S(1)}, f32[8,32,128]{2,1,0:T(8,128)}, u32[]{:S(2)}) copy-start(f32[8,32,128]{2,1,0:T(8,128)} %refs_1_.3) | copy-start | bytes 393220
  47.7 14.4 %copy-start.1 = (f32[8,32,128]{2,1,0:T(8,128)S(1)}, f32[8,32,128]{2,1,0:T(8,128)}, u32[]{:S(2)}) copy-start(f32[8,32,128]{2,1,0:T(8,128)} %refs_2_.3) | copy-start | bytes 393220
  62.0 39.0 %copy-start.2 = (f32[4,16,64]{2,1,0:T(8,128)S(1)}, f32[4,16,64]{2,1,0:T(8,128)}, u32[]{:S(2)}) copy-start(f32[4,16,64]{2,1,0:T(8,128)} %broadcast_multiply_fusion.2.refs_1_) | copy-start | bytes 49156
  104.9 96.4 %copy-start.4 = (f32[4,16,64]{2,1,0:T(8,128)S(1)}, f32[4,16,64]{2,1,0:T(8,128)}, u32[]{:S(2)}) copy-start(f32[4,16,64]{2,1,0:T(8,128)} %get-tuple-element.10) | copy-start | bytes 49156
  125.5 50.0 %copy-start.5 = (f32[2,8,32]{2,1,0:T(8,128)S(1)}, f32[2,8,32]{2,1,0:T(8,128)}, u32[]{:S(2)}) copy-start(f32[2,8,32]{2,1,0:T(8,128)} %get-tuple-element.12) | copy-start | bytes 6148
  173.2 52.0 %copy-start.3 = (f32[8,32,128]{2,1,0:T(8,128)S(1)}, f32[8,32,128]{2,1,0:T(8,128)}, u32[]{:S(2)}) copy-start(f32[8,32,128]{2,1,0:T(8,128)} %get-tuple-element.8) | copy-start | bytes 393220

commit v3 on v2

--- a/solution.py
+++ b/solution.py
@@ -22,11 +22,12 @@
 
 
 def level_kernel(cfg, *refs):
-    sizes, shift, count, lower, zero_start, residual = cfg
+    sizes, shift, count, lower, zero_start, residual, restrict = cfg
     n_in = 3 if zero_start else 4
     b_ref, beta_ref, alpha_ref = refs[0:3]
     v0_ref = None if zero_start else refs[3]
-    outs = refs[n_in : n_in + (2 if residual else 1)]
+    n_out = 1 + (1 if residual and not restrict else 0) + (3 if restrict else 0)
+    outs = refs[n_in : n_in + n_out]
     fld, xh, yzh, coef, dbuf, send_sem, recv_sem = refs[n_in + len(outs) :]
     A, B, C = b_ref.shape
     index = [lax.axis_index(axis) for axis in AXES]
@@ -62,6 +63,30 @@
                 buf = halo(h, slot)
                 buf[...] = jnp.zeros(buf.shape, buf.dtype)
 
+    if restrict:
+        coarse_rows = (
+            lax.broadcasted_iota(jnp.int32, (B // 2, B), 1) // 2
+            == lax.broadcasted_iota(jnp.int32, (B // 2, B), 0)
+        ).astype(jnp.float32)
+        coarse_cols = (
+            lax.broadcasted_iota(jnp.int32, (C, C // 2), 0) // 2
+            == lax.broadcasted_iota(jnp.int32, (C, C // 2), 1)
+        ).astype(jnp.float32)
+
+        def restrict_into(src, dst, scale):
+            for i in range(A // 2):
+                pair = src[2 * i] + src[2 * i + 1]
+                half = jnp.dot(
+                    coarse_rows, pair, precision=lax.Precision.HIGHEST,
+                    preferred_element_type=jnp.float32,
+                )
+                dst[i] = scale * jnp.dot(
+                    half, coarse_cols, precision=lax.Precision.HIGHEST,
+                    preferred_element_type=jnp.float32,
+                )
+
+        restrict_into(beta_ref, outs[2], 0.125)
+        restrict_into(alpha_ref, outs[3], 0.125)
     pl.semaphore_wait(barrier, total)
 
     def exchange(src, slot):
@@ -169,24 +194,29 @@
     if residual:
         slot = next_slot()
         exchange(outs[0], slot)
+        remain_ref = dbuf if restrict else outs[1]
         for i in range(A):
-            outs[1][i] = apply_rows(outs[0], slot, i)
+            remain_ref[i] = apply_rows(outs[0], slot, i)
+        if restrict:
+            restrict_into(dbuf, outs[1], 0.5)
 
 
 KERNELS = {}
 
 
-def smooth(level_args, shift, count, lower, zero_start, residual):
+def smooth(level_args, shift, count, lower, zero_start, residual, restrict=False):
     A, B, C = level_args[0].shape
     sizes = tuple(lax.axis_size(axis) for axis in AXES)
-    cfg = (sizes, shift, count, lower, zero_start, residual)
+    cfg = (sizes, shift, count, lower, zero_start, residual, restrict)
     ident = KERNELS.setdefault((A, B, C) + cfg[1:], len(KERNELS))
     vmem = pl.BlockSpec(memory_space=pltpu.VMEM)
     block = jax.ShapeDtypeStruct((A, B, C), jnp.float32)
-    n_out = 2 if residual else 1
+    coarse = jax.ShapeDtypeStruct((A // 2, B // 2, C // 2), jnp.float32)
+    shapes = [block] + ([block] if residual and not restrict else []) + ([coarse] * 3 if restrict else [])
+    n_out = len(shapes)
     return pl.pallas_call(
         functools.partial(level_kernel, cfg),
-        out_shape=tuple([block] * n_out),
+        out_shape=tuple(shapes),
         in_specs=[vmem] * len(level_args),
         out_specs=tuple([vmem] * n_out),
         scratch_shapes=[
@@ -268,31 +298,35 @@
 def shards(right_side, alpha_coef, beta_coef):
     betas = [beta_coef]
     alphas = [alpha_coef]
-    for level in range(LEVELS):
-        betas.append(restrict_mean(betas[-1]))
-        alphas.append(restrict_mean(alphas[-1]))
     rhs_levels = [right_side]
     smoothed = []
     for level in range(LEVELS):
-        iterate, remain = smooth(
+        iterate, coarse_rhs, coarse_beta, coarse_alpha = smooth(
             (rhs_levels[level], betas[level], alphas[level]),
             SHIFT_BASE * 4.0**level,
             SWEEPS,
             SMOOTH_LOWER,
             True,
             True,
+            True,
         )
         smoothed.append(iterate)
-        rhs_levels.append(4.0 * restrict_mean(remain))
+        rhs_levels.append(coarse_rhs)
+        betas.append(coarse_beta)
+        alphas.append(coarse_alpha)
     coarse_rhs = rhs_levels[LEVELS]
     local_shape = coarse_rhs.shape
     packed = jnp.stack([coarse_rhs, betas[LEVELS], alphas[LEVELS]])
     index_x = lax.axis_index("gx")
     index_y = lax.axis_index("gy")
     index_z = lax.axis_index("gz")
-    packed = lax.all_gather(packed, "gx", axis=1, tiled=True)
-    packed = lax.all_gather(packed, "gy", axis=2, tiled=True)
-    packed = lax.all_gather(packed, "gz", axis=3, tiled=True)
+    counts = tuple(lax.axis_size(axis) for axis in AXES)
+    packed = lax.all_gather(packed, AXES)
+    packed = packed.reshape(counts + packed.shape[1:])
+    packed = packed.transpose(3, 0, 4, 1, 5, 2, 6)
+    packed = packed.reshape(
+        (3,) + tuple(n * s for n, s in zip(counts, local_shape))
+    )
     whole_rhs = packed[0]
     whole_beta = packed[1]
     whole_alpha = packed[2]

time: 264 us -> 232 us (0.88)
  local copies, waits for them, and re-layouts: 41 us -> 6.18 us
  blocking collectives: 46.3 us -> 68.3 us
  other arithmetic: 20 us -> 4.32 us
  Pallas kernels: 155 us -> 150 us
    reshape x4 -> x1, local copies, waits for them, and re-layouts: 31.8 us -> 0.16 us  [shards(): packed = packed.reshape(counts + packed.shape[1:])]
    all_gather x3 -> x1, blocking collectives: 46.3 us -> 68.3 us  [shards(): packed = lax.all_gather(packed, AXES)]
    reduce_sum x11 -> x0, other arithmetic: 14.1 us -> none  [restrict_mean(): return jnp.sum(blocks, axis=(1, 3, 5)) * 0.125]
    pallas_call x6, Pallas kernels: 155 us -> 150 us  [smooth(): pl.pallas_call(functools.partial(level_kernel, cfg), out_shape=tuple(shap...]
    mul x2 -> x1, local copies, waits for them, and re-layouts: 2.89 us -> 0.19 us  [level_operator(): diagonal = shift * alpha_level]
where the time goes in v3:
time: 232 us; the launch traced here: 230 us
  Pallas kernels  150 us (65%)
  blocking collectives  68.3 us (29%)
  local copies, waits for them, and re-layouts  6.18 us (3%)
  other arithmetic  4.32 us (2%)
    pallas_call x6, Pallas kernels, smooth(): pl.pallas_call(functools.partial(level_kernel, cfg), out_shape=tuple(shap...  150 us
    all_gather x1, blocking collectives, shards(): packed = lax.all_gather(packed, AXES)  68.3 us

profile of v3, /device:TPU:1, one launch (start us, length us, event | category | flops | bytes accessed | tf_op | source)
XLA Modules:
  0.0 229.9 jit_solution(10320736841345910515)
XLA Ops:
  0.6 32.4 %shard_map.50 = (f32[8,32,128]{2,1,0:T(8,128)}, f32[4,16,64]{2,1,0:T(8,128)}, f32[4,16,64]{2,1,0:T(8,128)}, f32[4,16,64]{2,1,0:T(8,128)}) custom-call(f32[8,32,128]{2,1,0:T(8,128)} %refs_0_.3, f32[8,32,128]{2,1,0:T(8,128)} %refs_1_.3, f32[8,32,128]{2,1,0:T(8,128)} %refs_2_.3), custom_call_target="tpu_custom_call" | custom-call | tf_op jit(solution)/shard_map/pallas_call | solution.py:217
  33.0 22.6 %shard_map.51 = (f32[4,16,64]{2,1,0:T(8,128)}, f32[2,8,32]{2,1,0:T(8,128)}, f32[2,8,32]{2,1,0:T(8,128)}, f32[2,8,32]{2,1,0:T(8,128)}) custom-call(f32[4,16,64]{2,1,0:T(8,128)} %get-tuple-element.15.refs_0_, f32[4,16,64]{2,1,0:T(8,128)} %get-tuple-element.16.refs_1_, f32[4,16,64]{2,1,0:T(8,128)} %get-tuple-element.17.refs_2_), custom_call_target="tpu_custom_call" | custom-call | tf_op jit(solution)/shard_map/pallas_call | solution.py:217
  55.6 20.9 %shard_map.52 = (f32[2,8,32]{2,1,0:T(8,128)}, f32[1,4,16]{2,1,0:T(4,128)}, f32[1,4,16]{2,1,0:T(4,128)}, f32[1,4,16]{2,1,0:T(4,128)}) custom-call(f32[2,8,32]{2,1,0:T(8,128)} %get-tuple-element.19.refs_0_, f32[2,8,32]{2,1,0:T(8,128)} %get-tuple-element.20.refs_1_, f32[2,8,32]{2,1,0:T(8,128)} %get-tuple-element.21.refs_2_), custom_call_target="tpu_custom_call" | custom-call | tf_op jit(solution)/shard_map/pallas_call | solution.py:217
  76.5 0.7 pad_maximum_fusion
  77.2 68.3 %all-gather = f32[768,1,4,16]{3,2,1,0:T(4,128)S(1)} all-gather(f32[3,1,4,16]{3,2,1,0:T(4,128)S(1)} %pad_maximum_fusion), channel_id=2, replica_groups=mesh['gx'=4,'gy'=8,'gz'=8] {'gx','gy','gz'}, dimensions={0}, use_global_device_ids=true | all-gather | bytes 197376 | tf_op jit(solution)/shard_map/all_gather | solution.py:324
  145.6 0.2 copy.53
  145.8 0.2 fusion.183
  145.9 0.2 squeeze.7
  146.1 0.2 mul.398
  146.3 0.2 squeeze.8
  146.6 0.1 fusion.163
  146.8 0.1 fusion.164
  146.9 0.1 fusion.165
  147.0 0.1 fusion.166
  147.1 0.1 fusion.167
  147.3 0.1 fusion.168
  147.4 0.1 fusion.169
  147.5 0.1 fusion.170
  147.6 0.1 fusion.171
  147.8 0.1 fusion.175
  148.3 0.6 broadcast_add_fusion.refs_3_
  148.9 19.4 %shard_map.53 = f32[2,8,32]{2,1,0:T(8,128)} custom-call(f32[2,8,32]{2,1,0:T(8,128)} %get-tuple-element.19.refs_0_, f32[2,8,32]{2,1,0:T(8,128)} %get-tuple-element.20.refs_1_, f32[2,8,32]{2,1,0:T(8,128)} %get-tuple-element.21.refs_2_, f32[2,8,32]{2,1,0:T(8,128)} %broadcast_add_fusion.refs_3_), custom_call_target="tpu_custom_call" | custom-call | tf_op jit(solution)/shard_map/pallas_call | solution.py:217
  168.3 0.7 broadcast_in_dim.36
  169.3 0.6 add.402.refs_3_
  169.9 21.8 %shard_map.54 = f32[4,16,64]{2,1,0:T(8,128)} custom-call(f32[4,16,64]{2,1,0:T(8,128)} %get-tuple-element.15.refs_0_, f32[4,16,64]{2,1,0:T(8,128)} %get-tuple-element.16.refs_1_, f32[4,16,64]{2,1,0:T(8,128)} %get-tuple-element.17.refs_2_, f32[4,16,64]{2,1,0:T(8,128)} %add.402.refs_3_), custom_call_target="tpu_custom_call" | custom-call | tf_op jit(solution)/shard_map/pallas_call | solution.py:217
  191.7 0.8 copy.49
  192.5 0.2 copy.50
  192.8 0.2 copy.51
  192.9 0.7 add.403.refs_3_
  193.6 33.1 %shard_map.55 = (f32[8,32,128]{2,1,0:T(8,128)}, f32[8,32,128]{2,1,0:T(8,128)}) custom-call(f32[8,32,128]{2,1,0:T(8,128)} %refs_0_.3, f32[8,32,128]{2,1,0:T(8,128)} %refs_1_.3, f32[8,32,128]{2,1,0:T(8,128)} %refs_2_.3, f32[8,32,128]{2,1,0:T(8,128)} %add.403.refs_3_), custom_call_target="tpu_custom_call" | custom-call | tf_op jit(solution)/shard_map/pallas_call | solution.py:217
  226.8 1.6 copy.56
  228.4 1.6 copy.57
  (20 shorter events, 0.8 us)
Async XLA Ops:
  147.6 0.7 copy-start.2
  147.8 21.5 %copy-start.1 = (f32[4,16,64]{2,1,0:T(8,128)S(1)}, f32[4,16,64]{2,1,0:T(8,128)}, u32[]{:S(2)}) copy-start(f32[4,16,64]{2,1,0:T(8,128)} %get-tuple-element.18) | copy-start | bytes 49156
  148.0 44.9 %copy-start = (f32[8,32,128]{2,1,0:T(8,128)S(1)}, f32[8,32,128]{2,1,0:T(8,128)}, u32[]{:S(2)}) copy-start(f32[8,32,128]{2,1,0:T(8,128)} %get-tuple-element.14) | copy-start | bytes 393220

commit v4 on v3

--- a/solution.py
+++ b/solution.py
@@ -9,6 +9,7 @@
 
 MESH = pl.DeviceIdType.MESH
 AXES = ("gx", "gy", "gz")
+SLOTS = 3
 
 LEVELS = 3
 SWEEPS = 4
@@ -59,7 +60,7 @@
 
         @pl.when(jnp.logical_not(exists))
         def _():
-            for slot in range(2):
+            for slot in range(SLOTS):
                 buf = halo(h, slot)
                 buf[...] = jnp.zeros(buf.shape, buf.dtype)
 
@@ -89,31 +90,37 @@
         restrict_into(alpha_ref, outs[3], 0.125)
     pl.semaphore_wait(barrier, total)
 
-    def exchange(src, slot):
+    def exchange_start(src, slot):
         sources = (src.at[0], src.at[A - 1], src, src, src, src)
-        copies = []
+        waits = []
         for k, (exists, device) in enumerate(targets):
             copy = pltpu.make_async_remote_copy(
                 src_ref=sources[k],
                 dst_ref=halo(k ^ 1, slot),
-                send_sem=send_sem.at[k],
+                send_sem=send_sem.at[slot, k],
                 recv_sem=recv_sem.at[slot, k ^ 1],
                 device_id=device,
                 device_id_type=MESH,
             )
-            copies.append(copy)
             pl.when(exists)(copy.start)
-        for k, (exists, device) in enumerate(targets):
             incoming = pltpu.make_async_remote_copy(
                 src_ref=sources[k ^ 1],
                 dst_ref=halo(k, slot),
-                send_sem=send_sem.at[k ^ 1],
+                send_sem=send_sem.at[slot, k ^ 1],
                 recv_sem=recv_sem.at[slot, k],
                 device_id=device,
                 device_id_type=MESH,
             )
-            pl.when(exists)(copies[k].wait_send)
-            pl.when(exists)(incoming.wait_recv)
+            waits.append((exists, copy.wait_send))
+            waits.append((exists, incoming.wait_recv))
+        return waits
+
+    def exchange_finish(waits):
+        for exists, wait in waits:
+            pl.when(exists)(wait)
+
+    def exchange(src, slot):
+        exchange_finish(exchange_start(src, slot))
 
     rows = lax.broadcasted_iota(jnp.int32, (B, C), 0)
     cols = lax.broadcasted_iota(jnp.int32, (B, C), 1)
@@ -135,12 +142,17 @@
     exchanges = [0]
 
     def next_slot():
-        slot = exchanges[0] % 2
+        slot = exchanges[0] % SLOTS
         exchanges[0] += 1
         return slot
 
     slot = next_slot()
-    exchange(beta_ref, slot)
+    if zero_start:
+        exchange(beta_ref, slot)
+    else:
+        first_slot = next_slot()
+        first_waits = exchange_start(v0_ref, first_slot)
+        exchange(beta_ref, slot)
     for i in range(A):
         here, others = sides(beta_ref, i, slot)
         diagonal = shift * alpha_ref[i]
@@ -168,10 +180,9 @@
             dbuf[i] = update
             fld[current, i] = update
     else:
-        slot = next_slot()
-        exchange(v0_ref, slot)
+        exchange_finish(first_waits)
         for i in range(A):
-            remain = apply_rows(v0_ref, slot, i)
+            remain = apply_rows(v0_ref, first_slot, i)
             update = remain / coef[6, i] / center
             dbuf[i] = update
             fld[current, i] = v0_ref[i] + update
@@ -221,12 +232,12 @@
         out_specs=tuple([vmem] * n_out),
         scratch_shapes=[
             pltpu.VMEM((2, A, B, C), jnp.float32),
-            pltpu.VMEM((2, 2, B, C), jnp.float32),
-            pltpu.VMEM((4, 2, A, B, C), jnp.float32),
+            pltpu.VMEM((2, SLOTS, B, C), jnp.float32),
+            pltpu.VMEM((4, SLOTS, A, B, C), jnp.float32),
             pltpu.VMEM((7, A, B, C), jnp.float32),
             pltpu.VMEM((A, B, C), jnp.float32),
-            pltpu.SemaphoreType.DMA((6,)),
-            pltpu.SemaphoreType.DMA((2, 6)),
+            pltpu.SemaphoreType.DMA((SLOTS, 6)),
+            pltpu.SemaphoreType.DMA((SLOTS, 6)),
         ],
         compiler_params=pltpu.CompilerParams(collective_id=ident, has_side_effects=True),
     )(*level_args)
@@ -320,13 +331,9 @@
     index_x = lax.axis_index("gx")
     index_y = lax.axis_index("gy")
     index_z = lax.axis_index("gz")
-    counts = tuple(lax.axis_size(axis) for axis in AXES)
-    packed = lax.all_gather(packed, AXES)
-    packed = packed.reshape(counts + packed.shape[1:])
-    packed = packed.transpose(3, 0, 4, 1, 5, 2, 6)
-    packed = packed.reshape(
-        (3,) + tuple(n * s for n, s in zip(counts, local_shape))
-    )
+    packed = lax.all_gather(packed, "gx", axis=1, tiled=True)
+    packed = lax.all_gather(packed, "gy", axis=2, tiled=True)
+    packed = lax.all_gather(packed, "gz", axis=3, tiled=True)
     whole_rhs = packed[0]
     whole_beta = packed[1]
     whole_alpha = packed[2]

time: 232 us -> 207 us (0.89)
  blocking collectives: 68.3 us -> 46.6 us
    all_gather x1 -> x3, blocking collectives: 68.3 us -> 46.6 us  [the longest x1 21.3 us: shards(): packed = lax.all_gather(packed, 'gz', axis=3, tiled=True)]
    pallas_call x6, Pallas kernels: 150 us -> 148 us  [smooth(): pl.pallas_call(functools.partial(level_kernel, cfg), out_shape=tuple(shap...]
    unnamed x8 -> x19, local copies, waits for them, and re-layouts: 3.18 us -> 5.26 us
where the time goes in v4:
time: 207 us
  Pallas kernels  148 us (71%)
  blocking collectives  46.6 us (23%)
  local copies, waits for them, and re-layouts  7.79 us (4%)
  other arithmetic  3.45 us (2%)
    pallas_call x6, Pallas kernels, smooth(): pl.pallas_call(functools.partial(level_kernel, cfg), out_shape=tuple(shap...  148 us
    all_gather x1, blocking collectives, shards(): packed = lax.all_gather(packed, 'gz', axis=3, tiled=True)  21.3 us
    all_gather x1, blocking collectives, shards(): packed = lax.all_gather(packed, 'gy', axis=2, tiled=True)  16.8 us
    all_gather x1, blocking collectives, shards(): packed = lax.all_gather(packed, 'gx', axis=1, tiled=True)  8.54 us
    unnamed x19, local copies, waits for them, and re-layouts  5.26 us

profile of v4, /device:TPU:1, one launch (start us, length us, event | category | flops | bytes accessed | tf_op | source)
XLA Modules:
  0.0 206.6 jit_solution(15896443022784906574)
XLA Ops:
  0.6 32.5 %shard_map.50 = (f32[8,32,128]{2,1,0:T(8,128)}, f32[4,16,64]{2,1,0:T(8,128)}, f32[4,16,64]{2,1,0:T(8,128)}, f32[4,16,64]{2,1,0:T(8,128)}) custom-call(f32[8,32,128]{2,1,0:T(8,128)} %refs_0_.3, f32[8,32,128]{2,1,0:T(8,128)} %refs_1_.3, f32[8,32,128]{2,1,0:T(8,128)} %refs_2_.3), custom_call_target="tpu_custom_call" | custom-call | tf_op jit(solution)/shard_map/pallas_call | solution.py:228
  33.2 22.7 %shard_map.51 = (f32[4,16,64]{2,1,0:T(8,128)}, f32[2,8,32]{2,1,0:T(8,128)}, f32[2,8,32]{2,1,0:T(8,128)}, f32[2,8,32]{2,1,0:T(8,128)}) custom-call(f32[4,16,64]{2,1,0:T(8,128)} %get-tuple-element.15.refs_0_, f32[4,16,64]{2,1,0:T(8,128)} %get-tuple-element.16.refs_1_, f32[4,16,64]{2,1,0:T(8,128)} %get-tuple-element.17.refs_2_), custom_call_target="tpu_custom_call" | custom-call | tf_op jit(solution)/shard_map/pallas_call | solution.py:228
  55.9 21.1 %shard_map.52 = (f32[2,8,32]{2,1,0:T(8,128)}, f32[1,4,16]{2,1,0:T(4,128)}, f32[1,4,16]{2,1,0:T(4,128)}, f32[1,4,16]{2,1,0:T(4,128)}) custom-call(f32[2,8,32]{2,1,0:T(8,128)} %get-tuple-element.19.refs_0_, f32[2,8,32]{2,1,0:T(8,128)} %get-tuple-element.20.refs_1_, f32[2,8,32]{2,1,0:T(8,128)} %get-tuple-element.21.refs_2_), custom_call_target="tpu_custom_call" | custom-call | tf_op jit(solution)/shard_map/pallas_call | solution.py:228
  77.0 0.6 copy-done.6
  77.7 8.5 %all_gather.9 = f32[3,4,4,16]{3,2,1,0:T(4,128)S(1)} all-gather(f32[3,1,4,16]{3,2,1,0:T(4,128)S(1)} %pad_maximum_fusion), channel_id=1, replica_groups=mesh['gx'=4,'gy'=8,'gz'=8] {'gx'}, dimensions={1}, use_global_device_ids=true | all-gather | bytes 3840 | tf_op jit(solution)/shard_map/all_gather | solution.py:334
  86.2 16.8 %all_gather.10 = f32[3,4,32,16]{3,1,0,2:T(4,128)S(1)} all-gather(f32[3,4,4,16]{3,1,0,2:T(4,128)S(1)} %copy.30), channel_id=1, replica_groups=mesh['gx'=4,'gy'=8,'gz'=8] {'gy'}, dimensions={2}, use_global_device_ids=true | all-gather | bytes 27648 | tf_op jit(solution)/shard_map/all_gather | solution.py:335
  103.0 0.1 copy.31
  103.2 21.3 %all_gather.11 = f32[3,4,32,128]{2,1,0,3:T(4,128)S(1)} all-gather(f32[3,4,32,16]{2,1,0,3:T(4,128)S(1)} %copy.31), channel_id=1, replica_groups=mesh['gx'=4,'gy'=8,'gz'=8] {'gz'}, dimensions={3}, use_global_device_ids=true | all-gather | bytes 221184 | tf_op jit(solution)/shard_map/all_gather | solution.py:336
  124.4 0.1 fusion.189
  124.9 0.1 broadcast_multiply_fusion
  125.1 0.1 fusion.168
  125.2 0.1 fusion.169
  125.3 0.1 fusion.170
  125.4 0.1 fusion.171
  125.8 0.1 fusion.174
  126.1 0.1 fusion.176
  126.2 0.1 fusion.180
  126.7 0.6 copy-done.3
  127.3 0.6 broadcast_add_fusion.refs_3_
  127.9 20.7 %shard_map.53 = f32[2,8,32]{2,1,0:T(8,128)} custom-call(f32[2,8,32]{2,1,0:T(8,128)} %get-tuple-element.19.refs_0_, f32[2,8,32]{2,1,0:T(8,128)} %get-tuple-element.20.refs_1_, f32[2,8,32]{2,1,0:T(8,128)} %get-tuple-element.21.refs_2_, f32[2,8,32]{2,1,0:T(8,128)} %broadcast_add_fusion.refs_3_), custom_call_target="tpu_custom_call" | custom-call | tf_op jit(solution)/shard_map/pallas_call | solution.py:228
  148.7 0.7 broadcast_in_dim.36
  149.6 0.7 copy-done.2
  150.3 0.6 add.402.refs_3_
  150.9 18.7 %shard_map.54 = f32[4,16,64]{2,1,0:T(8,128)} custom-call(f32[4,16,64]{2,1,0:T(8,128)} %get-tuple-element.15.refs_0_, f32[4,16,64]{2,1,0:T(8,128)} %get-tuple-element.16.refs_1_, f32[4,16,64]{2,1,0:T(8,128)} %get-tuple-element.17.refs_2_, f32[4,16,64]{2,1,0:T(8,128)} %add.402.refs_3_), custom_call_target="tpu_custom_call" | custom-call | tf_op jit(solution)/shard_map/pallas_call | solution.py:228
  169.6 0.8 copy.39
  170.4 0.2 copy.40
  170.6 0.2 copy.41
  170.8 0.7 copy-done
  171.5 0.7 add.403.refs_3_
  172.2 32.1 %shard_map.55 = (f32[8,32,128]{2,1,0:T(8,128)}, f32[8,32,128]{2,1,0:T(8,128)}) custom-call(f32[8,32,128]{2,1,0:T(8,128)} %refs_0_.3, f32[8,32,128]{2,1,0:T(8,128)} %refs_1_.3, f32[8,32,128]{2,1,0:T(8,128)} %refs_2_.3, f32[8,32,128]{2,1,0:T(8,128)} %add.403.refs_3_), custom_call_target="tpu_custom_call" | custom-call | tf_op jit(solution)/shard_map/pallas_call | solution.py:228
  204.3 1.6 copy.47
  205.9 0.7 copy.48
  (31 shorter events, 1.4 us)
Async XLA Ops:
  77.0 0.7 copy-start.6
  77.0 0.7 copy-start.5
  77.0 0.7 copy-start.4
  126.6 0.7 copy-start.3
  149.5 0.8 copy-start.2
  170.6 0.9 copy-start
  204.3 1.6 copy-start.1

commit v5 on v4

--- a/solution.py
+++ b/solution.py
@@ -243,6 +243,90 @@
     )(*level_args)
 
 
+def gather_kernel(sizes, row_ref, out_ref, first, dense, second, send_sem, recv_sem):
+    index = [lax.axis_index(axis) for axis in AXES]
+    nx, ny, nz = sizes
+
+    def device(axis, step):
+        return tuple(
+            lax.rem(index[a] + step, sizes[a]) if a == axis else index[a] for a in range(3)
+        )
+
+    barrier = pltpu.get_barrier_semaphore()
+    partners = []
+    for axis in (2, 1, 0):
+        partners.append([device(axis, step) for step in range(1, sizes[axis])])
+    for group in partners:
+        for peer in group:
+            pl.semaphore_signal(barrier, inc=1, device_id=peer, device_id_type=MESH)
+    pl.semaphore_wait(barrier, sum(len(group) for group in partners))
+
+    stages = ((row_ref, first, 2), (dense, second, 1), (second, out_ref, 0))
+    for stage, (source, target, axis) in enumerate(stages):
+        mine = index[axis]
+        waits = []
+        for step in range(1, sizes[axis]):
+            peer = device(axis, step)
+            copy = pltpu.make_async_remote_copy(
+                src_ref=source,
+                dst_ref=target.at[mine],
+                send_sem=send_sem.at[stage, step],
+                recv_sem=recv_sem.at[stage, mine],
+                device_id=peer,
+                device_id_type=MESH,
+            )
+            copy.start()
+            origin = lax.rem(mine + sizes[axis] - step, sizes[axis])
+            incoming = pltpu.make_async_remote_copy(
+                src_ref=source,
+                dst_ref=target.at[origin],
+                send_sem=send_sem.at[stage, step],
+                recv_sem=recv_sem.at[stage, origin],
+                device_id=peer,
+                device_id_type=MESH,
+            )
+            waits.append((copy, incoming))
+        if stage == 0:
+            target[mine] = source[...]
+        else:
+            target[mine] = source[...]
+        for copy, incoming in waits:
+            copy.wait_send()
+            incoming.wait_recv()
+        if stage == 0:
+            for z in range(nz):
+                dense[z : z + 1, :] = first[z]
+
+
+def gather_bottom(packed):
+    sizes = tuple(lax.axis_size(axis) for axis in AXES)
+    nx, ny, nz = sizes
+    width = packed.size
+    lanes = -(-width // 128) * 128
+    row = jnp.pad(packed.reshape(1, width), ((0, 0), (0, lanes - width)))
+    vmem = pl.BlockSpec(memory_space=pltpu.VMEM)
+    top = max(sizes)
+    whole = pl.pallas_call(
+        functools.partial(gather_kernel, sizes),
+        out_shape=jax.ShapeDtypeStruct((nx, ny, nz, lanes), jnp.float32),
+        in_specs=[vmem],
+        out_specs=vmem,
+        scratch_shapes=[
+            pltpu.VMEM((nz, 1, lanes), jnp.float32),
+            pltpu.VMEM((nz, lanes), jnp.float32),
+            pltpu.VMEM((ny, nz, lanes), jnp.float32),
+            pltpu.SemaphoreType.DMA((3, top)),
+            pltpu.SemaphoreType.DMA((3, top)),
+        ],
+        compiler_params=pltpu.CompilerParams(collective_id=64, has_side_effects=True),
+    )(row)
+    whole = whole[..., :width].reshape((nx, ny, nz) + packed.shape)
+    whole = whole.transpose(3, 0, 4, 1, 5, 2, 6)
+    return whole.reshape(
+        (packed.shape[0],) + tuple(n * s for n, s in zip(sizes, packed.shape[1:]))
+    )
+
+
 def split_padded(padded):
     return (
         padded[:-2, 1:-1, 1:-1],
@@ -331,9 +415,7 @@
     index_x = lax.axis_index("gx")
     index_y = lax.axis_index("gy")
     index_z = lax.axis_index("gz")
-    packed = lax.all_gather(packed, "gx", axis=1, tiled=True)
-    packed = lax.all_gather(packed, "gy", axis=2, tiled=True)
-    packed = lax.all_gather(packed, "gz", axis=3, tiled=True)
+    packed = gather_bottom(packed)
     whole_rhs = packed[0]
     whole_beta = packed[1]
     whole_alpha = packed[2]

time: 207 us -> 179 us (0.86)
  blocking collectives: 46.6 us -> 0 us
  Pallas kernels: 148 us -> 164 us
    all_gather x3 -> x0, blocking collectives: 46.6 us -> none  [the longest x1 21.3 us: shards(): packed = lax.all_gather(packed, 'gz', axis=3, tiled=True)]
    pallas_call x0 -> x1, Pallas kernels: none -> 21.1 us  [gather_bottom(): pl.pallas_call(functools.partial(gather_kernel, sizes), out_shape=jax.Sha...]
    pallas_call x6, Pallas kernels: 148 us -> 143 us  [smooth(): pl.pallas_call(functools.partial(level_kernel, cfg), out_shape=tuple(shap...]
    unnamed x19 -> x8, local copies, waits for them, and re-layouts: 5.26 us -> 3.18 us
where the time goes in v5:
time: 179 us; the launch traced here: 178 us
  Pallas kernels  164 us (92%)
  local copies, waits for them, and re-layouts  8.56 us (5%)
  other arithmetic  4.33 us (2%)
    pallas_call x6, Pallas kernels, smooth(): pl.pallas_call(functools.partial(level_kernel, cfg), out_shape=tuple(shap...  143 us
    pallas_call x1, Pallas kernels, gather_bottom(): pl.pallas_call(functools.partial(gather_kernel, sizes), out_shape=jax.Sha...  21.1 us

profile of v5, /device:TPU:1, one launch (start us, length us, event | category | flops | bytes accessed | tf_op | source)
XLA Modules:
  0.0 178.1 jit_solution(1691008281163542133)
XLA Ops:
  0.6 32.5 %shard_map.50 = (f32[8,32,128]{2,1,0:T(8,128)}, f32[4,16,64]{2,1,0:T(8,128)}, f32[4,16,64]{2,1,0:T(8,128)}, f32[4,16,64]{2,1,0:T(8,128)}) custom-call(f32[8,32,128]{2,1,0:T(8,128)} %refs_0_.3, f32[8,32,128]{2,1,0:T(8,128)} %refs_1_.3, f32[8,32,128]{2,1,0:T(8,128)} %refs_2_.3), custom_call_target="tpu_custom_call" | custom-call | tf_op jit(solution)/shard_map/pallas_call | solution.py:228
  33.2 22.7 %shard_map.51 = (f32[4,16,64]{2,1,0:T(8,128)}, f32[2,8,32]{2,1,0:T(8,128)}, f32[2,8,32]{2,1,0:T(8,128)}, f32[2,8,32]{2,1,0:T(8,128)}) custom-call(f32[4,16,64]{2,1,0:T(8,128)} %get-tuple-element.15.refs_0_, f32[4,16,64]{2,1,0:T(8,128)} %get-tuple-element.16.refs_1_, f32[4,16,64]{2,1,0:T(8,128)} %get-tuple-element.17.refs_2_), custom_call_target="tpu_custom_call" | custom-call | tf_op jit(solution)/shard_map/pallas_call | solution.py:228
  55.9 21.1 %shard_map.52 = (f32[2,8,32]{2,1,0:T(8,128)}, f32[1,4,16]{2,1,0:T(4,128)}, f32[1,4,16]{2,1,0:T(4,128)}, f32[1,4,16]{2,1,0:T(4,128)}) custom-call(f32[2,8,32]{2,1,0:T(8,128)} %get-tuple-element.19.refs_0_, f32[2,8,32]{2,1,0:T(8,128)} %get-tuple-element.20.refs_1_, f32[2,8,32]{2,1,0:T(8,128)} %get-tuple-element.21.refs_2_), custom_call_target="tpu_custom_call" | custom-call | tf_op jit(solution)/shard_map/pallas_call | solution.py:228
  77.0 0.7 pad_maximum_fusion
  77.8 0.6 pad.41.row_ref
  78.4 21.1 %shard_map.53 = f32[4,8,8,256]{3,2,1,0:T(8,128)} custom-call(f32[1,256]{1,0:T(1,128)} %pad.41.row_ref), custom_call_target="tpu_custom_call" | custom-call | tf_op jit(solution)/shard_map/pallas_call | solution.py:309
  99.5 1.7 reshape.44
  101.2 0.2 copy.36
  101.4 0.2 fusion.183
  101.5 0.2 squeeze.7
  101.7 0.2 mul.398
  101.9 0.2 squeeze.8
  102.3 0.1 fusion.163
  102.4 0.1 fusion.164
  102.5 0.1 fusion.165
  102.6 0.1 fusion.166
  102.8 0.1 fusion.167
  103.0 0.1 fusion.169
  103.3 0.1 fusion.171
  103.4 0.1 fusion.175
  104.0 0.6 broadcast_add_fusion.refs_3_
  104.6 16.2 %shard_map.54 = f32[2,8,32]{2,1,0:T(8,128)} custom-call(f32[2,8,32]{2,1,0:T(8,128)} %get-tuple-element.19.refs_0_, f32[2,8,32]{2,1,0:T(8,128)} %get-tuple-element.20.refs_1_, f32[2,8,32]{2,1,0:T(8,128)} %get-tuple-element.21.refs_2_, f32[2,8,32]{2,1,0:T(8,128)} %broadcast_add_fusion.refs_3_), custom_call_target="tpu_custom_call" | custom-call | tf_op jit(solution)/shard_map/pallas_call | solution.py:228
  120.8 0.7 broadcast_in_dim.36
  121.7 0.6 add.404.refs_3_
  122.4 18.7 %shard_map.55 = f32[4,16,64]{2,1,0:T(8,128)} custom-call(f32[4,16,64]{2,1,0:T(8,128)} %get-tuple-element.15.refs_0_, f32[4,16,64]{2,1,0:T(8,128)} %get-tuple-element.16.refs_1_, f32[4,16,64]{2,1,0:T(8,128)} %get-tuple-element.17.refs_2_, f32[4,16,64]{2,1,0:T(8,128)} %add.404.refs_3_), custom_call_target="tpu_custom_call" | custom-call | tf_op jit(solution)/shard_map/pallas_call | solution.py:228
  141.1 0.8 copy.32
  141.9 0.2 copy.33
  142.2 0.2 copy.34
  142.3 0.7 add.405.refs_3_
  143.0 31.9 %shard_map.56 = (f32[8,32,128]{2,1,0:T(8,128)}, f32[8,32,128]{2,1,0:T(8,128)}) custom-call(f32[8,32,128]{2,1,0:T(8,128)} %refs_0_.3, f32[8,32,128]{2,1,0:T(8,128)} %refs_1_.3, f32[8,32,128]{2,1,0:T(8,128)} %refs_2_.3, f32[8,32,128]{2,1,0:T(8,128)} %add.405.refs_3_), custom_call_target="tpu_custom_call" | custom-call | tf_op jit(solution)/shard_map/pallas_call | solution.py:228
  175.0 1.6 copy.39
  176.5 1.6 copy.40
  (23 shorter events, 1.1 us)
Async XLA Ops:
  103.3 0.7 copy-start.2
  103.4 18.3 %copy-start.1 = (f32[4,16,64]{2,1,0:T(8,128)S(1)}, f32[4,16,64]{2,1,0:T(8,128)}, u32[]{:S(2)}) copy-start(f32[4,16,64]{2,1,0:T(8,128)} %get-tuple-element.18) | copy-start | bytes 49156
  103.7 38.7 %copy-start = (f32[8,32,128]{2,1,0:T(8,128)S(1)}, f32[8,32,128]{2,1,0:T(8,128)}, u32[]{:S(2)}) copy-start(f32[8,32,128]{2,1,0:T(8,128)} %get-tuple-element.14) | copy-start | bytes 393220

commit v6 on v5

--- a/solution.py
+++ b/solution.py
@@ -29,7 +29,7 @@
     v0_ref = None if zero_start else refs[3]
     n_out = 1 + (1 if residual and not restrict else 0) + (3 if restrict else 0)
     outs = refs[n_in : n_in + n_out]
-    fld, xh, yzh, coef, dbuf, send_sem, recv_sem = refs[n_in + len(outs) :]
+    fld, xh, yh, zh, zsend, coef, dbuf, send_sem, recv_sem = refs[n_in + len(outs) :]
     A, B, C = b_ref.shape
     index = [lax.axis_index(axis) for axis in AXES]
     targets = []
@@ -45,7 +45,15 @@
         targets.append((exists, device))
 
     def halo(h, slot):
-        return xh.at[h, slot] if h < 2 else yzh.at[h - 2, slot]
+        if h < 2:
+            return xh.at[h, slot]
+        return yh.at[h - 2, slot] if h < 4 else zh.at[h - 4, slot]
+
+    picks = lax.broadcasted_iota(jnp.int32, (8, C), 0)
+    lanes = lax.broadcasted_iota(jnp.int32, (8, C), 1)
+    selector = jnp.where(
+        (picks == 0) & (lanes == 0), 1.0, jnp.where((picks == 1) & (lanes == C - 1), 1.0, 0.0)
+    ).astype(jnp.float32)
 
     barrier = pltpu.get_barrier_semaphore()
     total = jnp.int32(0)
@@ -91,7 +99,12 @@
     pl.semaphore_wait(barrier, total)
 
     def exchange_start(src, slot):
-        sources = (src.at[0], src.at[A - 1], src, src, src, src)
+        block = src[...].reshape(A * B, C)
+        zsend[slot] = lax.dot_general(
+            selector, block, (((1,), (1,)), ((), ())),
+            precision=lax.Precision.HIGHEST, preferred_element_type=jnp.float32,
+        )
+        sources = (src.at[0], src.at[A - 1], src, src, zsend.at[slot], zsend.at[slot])
         waits = []
         for k, (exists, device) in enumerate(targets):
             copy = pltpu.make_async_remote_copy(
@@ -125,17 +138,20 @@
     rows = lax.broadcasted_iota(jnp.int32, (B, C), 0)
     cols = lax.broadcasted_iota(jnp.int32, (B, C), 1)
 
-    def sides(src, i, slot):
+    def z_columns(slot):
+        return (jnp.transpose(zh[0, slot]), jnp.transpose(zh[1, slot]))
+
+    def sides(src, i, slot, columns):
         here = src[i]
         lower_x = src[i - 1] if i > 0 else xh[0, slot]
         upper_x = src[i + 1] if i < A - 1 else xh[1, slot]
-        lower_y = jnp.where(rows == 0, pltpu.roll(yzh[0, slot, i], 1, 0), pltpu.roll(here, 1, 0))
+        lower_y = jnp.where(rows == 0, pltpu.roll(yh[0, slot, i], 1, 0), pltpu.roll(here, 1, 0))
         upper_y = jnp.where(
-            rows == B - 1, pltpu.roll(yzh[1, slot, i], B - 1, 0), pltpu.roll(here, B - 1, 0)
-        )
-        lower_z = jnp.where(cols == 0, pltpu.roll(yzh[2, slot, i], 1, 1), pltpu.roll(here, 1, 1))
+            rows == B - 1, pltpu.roll(yh[1, slot, i], B - 1, 0), pltpu.roll(here, B - 1, 0)
+        )
+        lower_z = jnp.where(cols == 0, columns[0][i * B : (i + 1) * B, 1:2], pltpu.roll(here, 1, 1))
         upper_z = jnp.where(
-            cols == C - 1, pltpu.roll(yzh[3, slot, i], C - 1, 1), pltpu.roll(here, C - 1, 1)
+            cols == C - 1, columns[1][i * B : (i + 1) * B, 0:1], pltpu.roll(here, C - 1, 1)
         )
         return here, (lower_x, upper_x, lower_y, upper_y, lower_z, upper_z)
 
@@ -153,8 +169,9 @@
         first_slot = next_slot()
         first_waits = exchange_start(v0_ref, first_slot)
         exchange(beta_ref, slot)
+    columns = z_columns(slot)
     for i in range(A):
-        here, others = sides(beta_ref, i, slot)
+        here, others = sides(beta_ref, i, slot, columns)
         diagonal = shift * alpha_ref[i]
         for k in range(6):
             face = 0.5 * (here + others[k])
@@ -162,8 +179,8 @@
             diagonal = diagonal + face
         coef[6, i] = diagonal
 
-    def apply_rows(src, slot, i):
-        here, others = sides(src, i, slot)
+    def apply_rows(src, slot, i, columns):
+        here, others = sides(src, i, slot, columns)
         acc = coef[0, i] * others[0]
         for k in range(1, 6):
             acc = acc + coef[k, i] * others[k]
@@ -181,8 +198,9 @@
             fld[current, i] = update
     else:
         exchange_finish(first_waits)
+        columns = z_columns(first_slot)
         for i in range(A):
-            remain = apply_rows(v0_ref, first_slot, i)
+            remain = apply_rows(v0_ref, first_slot, i, columns)
             update = remain / coef[6, i] / center
             dbuf[i] = update
             fld[current, i] = v0_ref[i] + update
@@ -193,8 +211,9 @@
         exchange(src, slot)
         last = sweep == count - 2
         dst = outs[0] if last else fld.at[1 - current]
+        columns = z_columns(slot)
         for i in range(A):
-            remain = apply_rows(src, slot, i)
+            remain = apply_rows(src, slot, i, columns)
             update = (rho_new * rho_old) * dbuf[i] + (2.0 * rho_new / half_width) * (
                 remain / coef[6, i]
             )
@@ -206,8 +225,9 @@
         slot = next_slot()
         exchange(outs[0], slot)
         remain_ref = dbuf if restrict else outs[1]
+        columns = z_columns(slot)
         for i in range(A):
-            remain_ref[i] = apply_rows(outs[0], slot, i)
+            remain_ref[i] = apply_rows(outs[0], slot, i, columns)
         if restrict:
             restrict_into(dbuf, outs[1], 0.5)
 
@@ -233,7 +253,9 @@
         scratch_shapes=[
             pltpu.VMEM((2, A, B, C), jnp.float32),
             pltpu.VMEM((2, SLOTS, B, C), jnp.float32),
-            pltpu.VMEM((4, SLOTS, A, B, C), jnp.float32),
+            pltpu.VMEM((2, SLOTS, A, B, C), jnp.float32),
+            pltpu.VMEM((2, SLOTS, 8, A * B), jnp.float32),
+            pltpu.VMEM((SLOTS, 8, A * B), jnp.float32),
             pltpu.VMEM((7, A, B, C), jnp.float32),
             pltpu.VMEM((A, B, C), jnp.float32),
             pltpu.SemaphoreType.DMA((SLOTS, 6)),

time: 179 us -> 171 us (0.955)
  Pallas kernels: 164 us -> 156 us
    pallas_call x6, Pallas kernels: 143 us -> 135 us  [smooth(): pl.pallas_call(functools.partial(level_kernel, cfg), out_shape=tuple(shap...]
where the time goes in v6:
time: 171 us; the launch traced here: 170 us
  Pallas kernels  156 us (91%)
  local copies, waits for them, and re-layouts  8.56 us (5%)
  other arithmetic  4.33 us (3%)
    pallas_call x6, Pallas kernels, smooth(): pl.pallas_call(functools.partial(level_kernel, cfg), out_shape=tuple(shap...  135 us
    pallas_call x1, Pallas kernels, gather_bottom(): pl.pallas_call(functools.partial(gather_kernel, sizes), out_shape=jax.Sha...  21.3 us

profile of v6, /device:TPU:1, one launch (start us, length us, event | category | flops | bytes accessed | tf_op | source)
XLA Modules:
  0.0 170.2 jit_solution(630941152730583310)
XLA Ops:
  0.6 28.4 %shard_map.50 = (f32[8,32,128]{2,1,0:T(8,128)}, f32[4,16,64]{2,1,0:T(8,128)}, f32[4,16,64]{2,1,0:T(8,128)}, f32[4,16,64]{2,1,0:T(8,128)}) custom-call(f32[8,32,128]{2,1,0:T(8,128)} %refs_0_.3, f32[8,32,128]{2,1,0:T(8,128)} %refs_1_.3, f32[8,32,128]{2,1,0:T(8,128)} %refs_2_.3), custom_call_target="tpu_custom_call" | custom-call | tf_op jit(solution)/shard_map/pallas_call | solution.py:248
  29.1 22.7 %shard_map.51 = (f32[4,16,64]{2,1,0:T(8,128)}, f32[2,8,32]{2,1,0:T(8,128)}, f32[2,8,32]{2,1,0:T(8,128)}, f32[2,8,32]{2,1,0:T(8,128)}) custom-call(f32[4,16,64]{2,1,0:T(8,128)} %get-tuple-element.15.refs_0_, f32[4,16,64]{2,1,0:T(8,128)} %get-tuple-element.16.refs_1_, f32[4,16,64]{2,1,0:T(8,128)} %get-tuple-element.17.refs_2_), custom_call_target="tpu_custom_call" | custom-call | tf_op jit(solution)/shard_map/pallas_call | solution.py:248
  51.8 21.4 %shard_map.52 = (f32[2,8,32]{2,1,0:T(8,128)}, f32[1,4,16]{2,1,0:T(4,128)}, f32[1,4,16]{2,1,0:T(4,128)}, f32[1,4,16]{2,1,0:T(4,128)}) custom-call(f32[2,8,32]{2,1,0:T(8,128)} %get-tuple-element.19.refs_0_, f32[2,8,32]{2,1,0:T(8,128)} %get-tuple-element.20.refs_1_, f32[2,8,32]{2,1,0:T(8,128)} %get-tuple-element.21.refs_2_), custom_call_target="tpu_custom_call" | custom-call | tf_op jit(solution)/shard_map/pallas_call | solution.py:248
  73.2 0.7 pad_maximum_fusion
  74.0 0.6 pad.41.row_ref
  74.5 21.3 %shard_map.53 = f32[4,8,8,256]{3,2,1,0:T(8,128)} custom-call(f32[1,256]{1,0:T(1,128)} %pad.41.row_ref), custom_call_target="tpu_custom_call" | custom-call | tf_op jit(solution)/shard_map/pallas_call | solution.py:331
  95.8 1.7 %reshape.44 = f32[4,8,8,3,1,4,16]{6,5,3,2,1,0,4:T(4,128)S(1)} reshape(f32[4,8,8,192]{3,2,1,0:T(8,128)} %bitcast.27) | data formatting | bytes 393216 | tf_op jit(solution)/shard_map/reshape | solution.py:345
  97.6 0.2 copy.36
  97.7 0.2 fusion.183
  97.9 0.2 squeeze.7
  98.1 0.2 mul.398
  98.3 0.2 squeeze.8
  98.6 0.1 fusion.163
  98.7 0.1 fusion.164
  98.9 0.1 fusion.165
  99.0 0.1 fusion.166
  99.1 0.1 fusion.167
  99.4 0.1 fusion.169
  99.6 0.1 fusion.171
  99.8 0.1 fusion.175
  100.3 0.6 broadcast_add_fusion.refs_3_
  100.9 16.7 %shard_map.54 = f32[2,8,32]{2,1,0:T(8,128)} custom-call(f32[2,8,32]{2,1,0:T(8,128)} %get-tuple-element.19.refs_0_, f32[2,8,32]{2,1,0:T(8,128)} %get-tuple-element.20.refs_1_, f32[2,8,32]{2,1,0:T(8,128)} %get-tuple-element.21.refs_2_, f32[2,8,32]{2,1,0:T(8,128)} %broadcast_add_fusion.refs_3_), custom_call_target="tpu_custom_call" | custom-call | tf_op jit(solution)/shard_map/pallas_call | solution.py:248
  117.6 0.7 broadcast_in_dim.36
  118.6 0.6 add.404.refs_3_
  119.2 19.0 %shard_map.55 = f32[4,16,64]{2,1,0:T(8,128)} custom-call(f32[4,16,64]{2,1,0:T(8,128)} %get-tuple-element.15.refs_0_, f32[4,16,64]{2,1,0:T(8,128)} %get-tuple-element.16.refs_1_, f32[4,16,64]{2,1,0:T(8,128)} %get-tuple-element.17.refs_2_, f32[4,16,64]{2,1,0:T(8,128)} %add.404.refs_3_), custom_call_target="tpu_custom_call" | custom-call | tf_op jit(solution)/shard_map/pallas_call | solution.py:248
  138.2 0.8 copy.32
  139.0 0.2 copy.33
  139.2 0.2 copy.34
  139.4 0.7 add.405.refs_3_
  140.1 26.9 %shard_map.56 = (f32[8,32,128]{2,1,0:T(8,128)}, f32[8,32,128]{2,1,0:T(8,128)}) custom-call(f32[8,32,128]{2,1,0:T(8,128)} %refs_0_.3, f32[8,32,128]{2,1,0:T(8,128)} %refs_1_.3, f32[8,32,128]{2,1,0:T(8,128)} %refs_2_.3, f32[8,32,128]{2,1,0:T(8,128)} %add.405.refs_3_), custom_call_target="tpu_custom_call" | custom-call | tf_op jit(solution)/shard_map/pallas_call | solution.py:248
  167.1 1.6 copy.39
  168.6 1.6 copy.40
  (23 shorter events, 1.1 us)
Async XLA Ops:
  99.6 0.7 copy-start.2
  99.8 18.8 %copy-start.1 = (f32[4,16,64]{2,1,0:T(8,128)S(1)}, f32[4,16,64]{2,1,0:T(8,128)}, u32[]{:S(2)}) copy-start(f32[4,16,64]{2,1,0:T(8,128)} %get-tuple-element.18) | copy-start | bytes 49156
  100.0 39.4 %copy-start = (f32[8,32,128]{2,1,0:T(8,128)S(1)}, f32[8,32,128]{2,1,0:T(8,128)}, u32[]{:S(2)}) copy-start(f32[8,32,128]{2,1,0:T(8,128)} %get-tuple-element.14) | copy-start | bytes 393220

commit v7 on v6

--- a/solution.py
+++ b/solution.py
@@ -104,7 +104,11 @@
             selector, block, (((1,), (1,)), ((), ())),
             precision=lax.Precision.HIGHEST, preferred_element_type=jnp.float32,
         )
-        sources = (src.at[0], src.at[A - 1], src, src, zsend.at[slot], zsend.at[slot])
+        sources = (
+            src.at[0], src.at[A - 1],
+            src.at[:, 0:8, :], src.at[:, B - 8 : B, :],
+            zsend.at[slot], zsend.at[slot],
+        )
         waits = []
         for k, (exists, device) in enumerate(targets):
             copy = pltpu.make_async_remote_copy(
@@ -145,10 +149,8 @@
         here = src[i]
         lower_x = src[i - 1] if i > 0 else xh[0, slot]
         upper_x = src[i + 1] if i < A - 1 else xh[1, slot]
-        lower_y = jnp.where(rows == 0, pltpu.roll(yh[0, slot, i], 1, 0), pltpu.roll(here, 1, 0))
-        upper_y = jnp.where(
-            rows == B - 1, pltpu.roll(yh[1, slot, i], B - 1, 0), pltpu.roll(here, B - 1, 0)
-        )
+        lower_y = jnp.where(rows == 0, yh[0, slot, i, 7:8, :], pltpu.roll(here, 1, 0))
+        upper_y = jnp.where(rows == B - 1, yh[1, slot, i, 0:1, :], pltpu.roll(here, B - 1, 0))
         lower_z = jnp.where(cols == 0, columns[0][i * B : (i + 1) * B, 1:2], pltpu.roll(here, 1, 1))
         upper_z = jnp.where(
             cols == C - 1, columns[1][i * B : (i + 1) * B, 0:1], pltpu.roll(here, C - 1, 1)
@@ -253,7 +255,7 @@
         scratch_shapes=[
             pltpu.VMEM((2, A, B, C), jnp.float32),
             pltpu.VMEM((2, SLOTS, B, C), jnp.float32),
-            pltpu.VMEM((2, SLOTS, A, B, C), jnp.float32),
+            pltpu.VMEM((2, SLOTS, A, 8, C), jnp.float32),
             pltpu.VMEM((2, SLOTS, 8, A * B), jnp.float32),
             pltpu.VMEM((SLOTS, 8, A * B), jnp.float32),
             pltpu.VMEM((7, A, B, C), jnp.float32),

time: 171 us -> 167 us (0.977)
  Pallas kernels: 156 us -> 152 us
    pallas_call x6, Pallas kernels: 135 us -> 131 us  [smooth(): pl.pallas_call(functools.partial(level_kernel, cfg), out_shape=tuple(shap...]
where the time goes in v7:
time: 167 us; the launch traced here: 166 us
  Pallas kernels  152 us (91%)
  local copies, waits for them, and re-layouts  8.56 us (5%)
  other arithmetic  4.33 us (3%)
    pallas_call x6, Pallas kernels, smooth(): pl.pallas_call(functools.partial(level_kernel, cfg), out_shape=tuple(shap...  131 us
    pallas_call x1, Pallas kernels, gather_bottom(): pl.pallas_call(functools.partial(gather_kernel, sizes), out_shape=jax.Sha...  21 us

profile of v7, /device:TPU:1, one launch (start us, length us, event | category | flops | bytes accessed | tf_op | source)
XLA Modules:
  0.0 165.9 jit_solution(6514760330602514120)
XLA Ops:
  0.6 27.6 %shard_map.50 = (f32[8,32,128]{2,1,0:T(8,128)}, f32[4,16,64]{2,1,0:T(8,128)}, f32[4,16,64]{2,1,0:T(8,128)}, f32[4,16,64]{2,1,0:T(8,128)}) custom-call(f32[8,32,128]{2,1,0:T(8,128)} %refs_0_.3, f32[8,32,128]{2,1,0:T(8,128)} %refs_1_.3, f32[8,32,128]{2,1,0:T(8,128)} %refs_2_.3), custom_call_target="tpu_custom_call" | custom-call | tf_op jit(solution)/shard_map/pallas_call | solution.py:250
  28.2 22.5 %shard_map.51 = (f32[4,16,64]{2,1,0:T(8,128)}, f32[2,8,32]{2,1,0:T(8,128)}, f32[2,8,32]{2,1,0:T(8,128)}, f32[2,8,32]{2,1,0:T(8,128)}) custom-call(f32[4,16,64]{2,1,0:T(8,128)} %get-tuple-element.15.refs_0_, f32[4,16,64]{2,1,0:T(8,128)} %get-tuple-element.16.refs_1_, f32[4,16,64]{2,1,0:T(8,128)} %get-tuple-element.17.refs_2_), custom_call_target="tpu_custom_call" | custom-call | tf_op jit(solution)/shard_map/pallas_call | solution.py:250
  50.7 21.5 %shard_map.52 = (f32[2,8,32]{2,1,0:T(8,128)}, f32[1,4,16]{2,1,0:T(4,128)}, f32[1,4,16]{2,1,0:T(4,128)}, f32[1,4,16]{2,1,0:T(4,128)}) custom-call(f32[2,8,32]{2,1,0:T(8,128)} %get-tuple-element.19.refs_0_, f32[2,8,32]{2,1,0:T(8,128)} %get-tuple-element.20.refs_1_, f32[2,8,32]{2,1,0:T(8,128)} %get-tuple-element.21.refs_2_), custom_call_target="tpu_custom_call" | custom-call | tf_op jit(solution)/shard_map/pallas_call | solution.py:250
  72.3 0.7 pad_maximum_fusion
  73.1 0.6 pad.41.row_ref
  73.6 21.0 %shard_map.53 = f32[4,8,8,256]{3,2,1,0:T(8,128)} custom-call(f32[1,256]{1,0:T(1,128)} %pad.41.row_ref), custom_call_target="tpu_custom_call" | custom-call | tf_op jit(solution)/shard_map/pallas_call | solution.py:333
  94.7 1.7 %reshape.44 = f32[4,8,8,3,1,4,16]{6,5,3,2,1,0,4:T(4,128)S(1)} reshape(f32[4,8,8,192]{3,2,1,0:T(8,128)} %bitcast.27) | data formatting | bytes 393216 | tf_op jit(solution)/shard_map/reshape | solution.py:347
  96.4 0.2 copy.36
  96.6 0.2 fusion.183
  96.8 0.2 squeeze.7
  96.9 0.2 mul.398
  97.1 0.2 squeeze.8
  97.5 0.1 fusion.163
  97.6 0.1 fusion.164
  97.7 0.1 fusion.165
  97.8 0.1 fusion.166
  98.0 0.1 fusion.167
  98.2 0.1 fusion.169
  98.5 0.1 fusion.171
  98.6 0.1 fusion.175
  99.2 0.6 broadcast_add_fusion.refs_3_
  99.8 16.7 %shard_map.54 = f32[2,8,32]{2,1,0:T(8,128)} custom-call(f32[2,8,32]{2,1,0:T(8,128)} %get-tuple-element.19.refs_0_, f32[2,8,32]{2,1,0:T(8,128)} %get-tuple-element.20.refs_1_, f32[2,8,32]{2,1,0:T(8,128)} %get-tuple-element.21.refs_2_, f32[2,8,32]{2,1,0:T(8,128)} %broadcast_add_fusion.refs_3_), custom_call_target="tpu_custom_call" | custom-call | tf_op jit(solution)/shard_map/pallas_call | solution.py:250
  116.5 0.7 broadcast_in_dim.36
  117.4 0.6 add.404.refs_3_
  118.1 18.5 %shard_map.55 = f32[4,16,64]{2,1,0:T(8,128)} custom-call(f32[4,16,64]{2,1,0:T(8,128)} %get-tuple-element.15.refs_0_, f32[4,16,64]{2,1,0:T(8,128)} %get-tuple-element.16.refs_1_, f32[4,16,64]{2,1,0:T(8,128)} %get-tuple-element.17.refs_2_, f32[4,16,64]{2,1,0:T(8,128)} %add.404.refs_3_), custom_call_target="tpu_custom_call" | custom-call | tf_op jit(solution)/shard_map/pallas_call | solution.py:250
  136.5 0.8 copy.32
  137.4 0.2 copy.33
  137.6 0.2 copy.34
  137.8 0.7 add.405.refs_3_
  138.5 24.3 %shard_map.56 = (f32[8,32,128]{2,1,0:T(8,128)}, f32[8,32,128]{2,1,0:T(8,128)}) custom-call(f32[8,32,128]{2,1,0:T(8,128)} %refs_0_.3, f32[8,32,128]{2,1,0:T(8,128)} %refs_1_.3, f32[8,32,128]{2,1,0:T(8,128)} %refs_2_.3, f32[8,32,128]{2,1,0:T(8,128)} %add.405.refs_3_), custom_call_target="tpu_custom_call" | custom-call | tf_op jit(solution)/shard_map/pallas_call | solution.py:250
  162.8 1.6 copy.39
  164.3 1.6 copy.40
  (23 shorter events, 1.1 us)
Async XLA Ops:
  98.5 0.7 copy-start.2
  98.6 18.8 %copy-start.1 = (f32[4,16,64]{2,1,0:T(8,128)S(1)}, f32[4,16,64]{2,1,0:T(8,128)}, u32[]{:S(2)}) copy-start(f32[4,16,64]{2,1,0:T(8,128)} %get-tuple-element.18) | copy-start | bytes 49156
  98.9 38.9 %copy-start = (f32[8,32,128]{2,1,0:T(8,128)S(1)}, f32[8,32,128]{2,1,0:T(8,128)}, u32[]{:S(2)}) copy-start(f32[8,32,128]{2,1,0:T(8,128)} %get-tuple-element.14) | copy-start | bytes 393220

commit v8 on v7

--- a/solution.py
+++ b/solution.py
@@ -267,6 +267,261 @@
     )(*level_args)
 
 
+def restrict_into(src, dst, scale):
+    A, B, C = src.shape
+    coarse_rows = (
+        lax.broadcasted_iota(jnp.int32, (B // 2, B), 1) // 2
+        == lax.broadcasted_iota(jnp.int32, (B // 2, B), 0)
+    ).astype(jnp.float32)
+    coarse_cols = (
+        lax.broadcasted_iota(jnp.int32, (C, C // 2), 0) // 2
+        == lax.broadcasted_iota(jnp.int32, (C, C // 2), 1)
+    ).astype(jnp.float32)
+    for i in range(A // 2):
+        pair = src[2 * i] + src[2 * i + 1]
+        half = jnp.dot(
+            coarse_rows, pair, precision=lax.Precision.HIGHEST, preferred_element_type=jnp.float32
+        )
+        dst[i] = scale * jnp.dot(
+            half, coarse_cols, precision=lax.Precision.HIGHEST, preferred_element_type=jnp.float32
+        )
+
+
+def neighbour_targets(sizes):
+    index = [lax.axis_index(axis) for axis in AXES]
+    targets = []
+    for k in range(6):
+        axis = k // 2
+        if k % 2 == 0:
+            exists = index[axis] > 0
+            other = index[axis] - 1
+        else:
+            exists = index[axis] < sizes[axis] - 1
+            other = index[axis] + 1
+        device = tuple(other if a == axis else index[a] for a in range(3))
+        targets.append((exists, device))
+    return targets
+
+
+def level_tools(shape, level, targets, bufs, send_sem, recv_sem):
+    A, B, C = shape
+    fld, xh, yh, zh, zsend, coef, dbuf = bufs
+
+    def halo(h, slot):
+        if h < 2:
+            return xh.at[h, slot]
+        return yh.at[h - 2, slot] if h < 4 else zh.at[h - 4, slot]
+
+    picks = lax.broadcasted_iota(jnp.int32, (8, C), 0)
+    lanes = lax.broadcasted_iota(jnp.int32, (8, C), 1)
+    selector = jnp.where(
+        (picks == 0) & (lanes == 0), 1.0, jnp.where((picks == 1) & (lanes == C - 1), 1.0, 0.0)
+    ).astype(jnp.float32)
+    rows = lax.broadcasted_iota(jnp.int32, (B, C), 0)
+    cols = lax.broadcasted_iota(jnp.int32, (B, C), 1)
+
+    def zero_halos():
+        for h, (exists, device) in enumerate(targets):
+
+            @pl.when(jnp.logical_not(exists))
+            def _():
+                for slot in range(SLOTS):
+                    buf = halo(h, slot)
+                    buf[...] = jnp.zeros(buf.shape, buf.dtype)
+
+    def exchange_start(src, slot):
+        block = src[...].reshape(A * B, C)
+        zsend[slot] = lax.dot_general(
+            selector, block, (((1,), (1,)), ((), ())),
+            precision=lax.Precision.HIGHEST, preferred_element_type=jnp.float32,
+        )
+        sources = (
+            src.at[0], src.at[A - 1],
+            src.at[:, 0:8, :], src.at[:, B - 8 : B, :],
+            zsend.at[slot], zsend.at[slot],
+        )
+        waits = []
+        for k, (exists, device) in enumerate(targets):
+            copy = pltpu.make_async_remote_copy(
+                src_ref=sources[k],
+                dst_ref=halo(k ^ 1, slot),
+                send_sem=send_sem.at[level, slot, k],
+                recv_sem=recv_sem.at[level, slot, k ^ 1],
+                device_id=device,
+                device_id_type=MESH,
+            )
+            pl.when(exists)(copy.start)
+            incoming = pltpu.make_async_remote_copy(
+                src_ref=sources[k ^ 1],
+                dst_ref=halo(k, slot),
+                send_sem=send_sem.at[level, slot, k ^ 1],
+                recv_sem=recv_sem.at[level, slot, k],
+                device_id=device,
+                device_id_type=MESH,
+            )
+            waits.append((exists, copy.wait_send))
+            waits.append((exists, incoming.wait_recv))
+        return waits
+
+    def exchange_finish(waits):
+        for exists, wait in waits:
+            pl.when(exists)(wait)
+
+    def exchange(src, slot):
+        exchange_finish(exchange_start(src, slot))
+
+    def z_columns(slot):
+        return (jnp.transpose(zh[0, slot]), jnp.transpose(zh[1, slot]))
+
+    def sides(src, i, slot, columns):
+        here = src[i]
+        lower_x = src[i - 1] if i > 0 else xh[0, slot]
+        upper_x = src[i + 1] if i < A - 1 else xh[1, slot]
+        lower_y = jnp.where(rows == 0, yh[0, slot, i, 7:8, :], pltpu.roll(here, 1, 0))
+        upper_y = jnp.where(rows == B - 1, yh[1, slot, i, 0:1, :], pltpu.roll(here, B - 1, 0))
+        lower_z = jnp.where(cols == 0, columns[0][i * B : (i + 1) * B, 1:2], pltpu.roll(here, 1, 1))
+        upper_z = jnp.where(
+            cols == C - 1, columns[1][i * B : (i + 1) * B, 0:1], pltpu.roll(here, C - 1, 1)
+        )
+        return here, (lower_x, upper_x, lower_y, upper_y, lower_z, upper_z)
+
+    def build_coef(beta_ref, alpha_ref, slot, shift):
+        columns = z_columns(slot)
+        for i in range(A):
+            here, others = sides(beta_ref, i, slot, columns)
+            diagonal = shift * alpha_ref[i]
+            for k in range(6):
+                face = 0.5 * (here + others[k])
+                coef[k, i] = face
+                diagonal = diagonal + face
+            coef[6, i] = diagonal
+
+    def apply_rows(src, b_ref, slot, i, columns):
+        here, others = sides(src, i, slot, columns)
+        acc = coef[0, i] * others[0]
+        for k in range(1, 6):
+            acc = acc + coef[k, i] * others[k]
+        return b_ref[i] - (coef[6, i] * here - acc)
+
+    def smooth_down(b_ref, v_out, next_rhs, count, lower):
+        center = (UPPER_EIG + lower) / 2.0
+        half_width = (UPPER_EIG - lower) / 2.0
+        sigma_ratio = center / half_width
+        rho_old = 1.0 / sigma_ratio
+        current = 0
+        for i in range(A):
+            update = b_ref[i] / coef[6, i] / center
+            dbuf[i] = update
+            fld[current, i] = update
+        slot = 0
+        for sweep in range(count - 1):
+            rho_new = 1.0 / (2.0 * sigma_ratio - rho_old)
+            slot = (slot + 1) % SLOTS
+            src = fld.at[current]
+            exchange(src, slot)
+            columns = z_columns(slot)
+            dst = v_out if sweep == count - 2 else fld.at[1 - current]
+            for i in range(A):
+                remain = apply_rows(src, b_ref, slot, i, columns)
+                update = (rho_new * rho_old) * dbuf[i] + (2.0 * rho_new / half_width) * (
+                    remain / coef[6, i]
+                )
+                dbuf[i] = update
+                dst[i] = src[i] + update
+            rho_old = rho_new
+            current = 1 - current
+        slot = (slot + 1) % SLOTS
+        exchange(v_out, slot)
+        columns = z_columns(slot)
+        for i in range(A):
+            dbuf[i] = apply_rows(v_out, b_ref, slot, i, columns)
+        restrict_into(dbuf, next_rhs, 0.5)
+
+    return zero_halos, exchange_start, exchange_finish, build_coef, smooth_down
+
+
+def level_scratch(shape):
+    A, B, C = shape
+    return [
+        pltpu.VMEM((2, A, B, C), jnp.float32),
+        pltpu.VMEM((2, SLOTS, B, C), jnp.float32),
+        pltpu.VMEM((2, SLOTS, A, 8, C), jnp.float32),
+        pltpu.VMEM((2, SLOTS, 8, A * B), jnp.float32),
+        pltpu.VMEM((SLOTS, 8, A * B), jnp.float32),
+        pltpu.VMEM((7, A, B, C), jnp.float32),
+        pltpu.VMEM((A, B, C), jnp.float32),
+    ]
+
+
+def down_kernel(cfg, *refs):
+    sizes, shapes, shifts = cfg
+    depth = len(shapes)
+    b0, beta0, alpha0 = refs[0:3]
+    outs = refs[3 : 3 + 4 * depth]
+    iterates = outs[0:depth]
+    rhs = [b0] + list(outs[depth : 2 * depth])
+    betas = [beta0] + list(outs[2 * depth : 3 * depth])
+    alphas = [alpha0] + list(outs[3 * depth : 4 * depth])
+    scratch = refs[3 + 4 * depth :]
+    send_sem, recv_sem = scratch[7 * depth], scratch[7 * depth + 1]
+    targets = neighbour_targets(sizes)
+    barrier = pltpu.get_barrier_semaphore()
+    total = jnp.int32(0)
+    for exists, device in targets:
+
+        @pl.when(exists)
+        def _():
+            pl.semaphore_signal(barrier, inc=1, device_id=device, device_id_type=MESH)
+
+        total = total + exists.astype(jnp.int32)
+    tools = [
+        level_tools(shapes[l], l, targets, scratch[7 * l : 7 * l + 7], send_sem, recv_sem)
+        for l in range(depth)
+    ]
+    for tool in tools:
+        tool[0]()
+    for l in range(depth):
+        restrict_into(betas[l], betas[l + 1], 0.125)
+        restrict_into(alphas[l], alphas[l + 1], 0.125)
+    pl.semaphore_wait(barrier, total)
+    waits = [tools[l][1](betas[l], 0) for l in range(depth)]
+    for l in range(depth):
+        tools[l][2](waits[l])
+        tools[l][3](betas[l], alphas[l], 0, shifts[l])
+    for l in range(depth):
+        tools[l][4](rhs[l], iterates[l], rhs[l + 1], SWEEPS, SMOOTH_LOWER)
+
+
+def down_chain(right_side, beta_coef, alpha_coef):
+    sizes = tuple(lax.axis_size(axis) for axis in AXES)
+    shapes = [tuple(n >> l for n in right_side.shape) for l in range(LEVELS + 1)]
+    shifts = tuple(SHIFT_BASE * 4.0**l for l in range(LEVELS))
+    cfg = (sizes, tuple(shapes[:LEVELS]), shifts)
+    vmem = pl.BlockSpec(memory_space=pltpu.VMEM)
+    out_shapes = [jax.ShapeDtypeStruct(s, jnp.float32) for s in shapes[:LEVELS]]
+    out_shapes += [jax.ShapeDtypeStruct(s, jnp.float32) for s in shapes[1:]] * 3
+    scratch = []
+    for s in shapes[:LEVELS]:
+        scratch += level_scratch(s)
+    scratch += [
+        pltpu.SemaphoreType.DMA((LEVELS, SLOTS, 6)),
+        pltpu.SemaphoreType.DMA((LEVELS, SLOTS, 6)),
+    ]
+    outs = pl.pallas_call(
+        functools.partial(down_kernel, cfg),
+        out_shape=tuple(out_shapes),
+        in_specs=[vmem] * 3,
+        out_specs=tuple([vmem] * len(out_shapes)),
+        scratch_shapes=scratch,
+        compiler_params=pltpu.CompilerParams(collective_id=32, has_side_effects=True),
+    )(right_side, beta_coef, alpha_coef)
+    iterates = list(outs[0:LEVELS])
+    rhs_levels = [right_side] + list(outs[LEVELS : 2 * LEVELS])
+    betas = [beta_coef] + list(outs[2 * LEVELS : 3 * LEVELS])
+    alphas = [alpha_coef] + list(outs[3 * LEVELS : 4 * LEVELS])
+    return iterates, rhs_levels, betas, alphas
+
+
 def gather_kernel(sizes, row_ref, out_ref, first, dense, second, send_sem, recv_sem):
     index = [lax.axis_index(axis) for axis in AXES]
     nx, ny, nz = sizes
@@ -415,24 +670,7 @@
 
 
 def shards(right_side, alpha_coef, beta_coef):
-    betas = [beta_coef]
-    alphas = [alpha_coef]
-    rhs_levels = [right_side]
-    smoothed = []
-    for level in range(LEVELS):
-        iterate, coarse_rhs, coarse_beta, coarse_alpha = smooth(
-            (rhs_levels[level], betas[level], alphas[level]),
-            SHIFT_BASE * 4.0**level,
-            SWEEPS,
-            SMOOTH_LOWER,
-            True,
-            True,
-            True,
-        )
-        smoothed.append(iterate)
-        rhs_levels.append(coarse_rhs)
-        betas.append(coarse_beta)
-        alphas.append(coarse_alpha)
+    smoothed, rhs_levels, betas, alphas = down_chain(right_side, beta_coef, alpha_coef)
     coarse_rhs = rhs_levels[LEVELS]
     local_shape = coarse_rhs.shape
     packed = jnp.stack([coarse_rhs, betas[LEVELS], alphas[LEVELS]])

time: 167 us -> 153 us (0.916)
  Pallas kernels: 152 us -> 139 us
    pallas_call x6 -> x3, Pallas kernels: 131 us -> 59.3 us  [smooth(): pl.pallas_call(functools.partial(level_kernel, cfg), out_shape=tuple(shap...]
    pallas_call x0 -> x1, Pallas kernels: none -> 58.4 us  [down_chain(): pl.pallas_call(functools.partial(down_kernel, cfg), out_shape=tuple(out_s...]
where the time goes in v8:
time: 153 us
  Pallas kernels  139 us (91%)
  local copies, waits for them, and re-layouts  8.56 us (6%)
  other arithmetic  4.32 us (3%)
    pallas_call x3, Pallas kernels, smooth(): pl.pallas_call(functools.partial(level_kernel, cfg), out_shape=tuple(shap...  59.3 us
    pallas_call x1, Pallas kernels, down_chain(): pl.pallas_call(functools.partial(down_kernel, cfg), out_shape=tuple(out_s...  58.4 us
    pallas_call x1, Pallas kernels, gather_bottom(): pl.pallas_call(functools.partial(gather_kernel, sizes), out_shape=jax.Sha...  21.1 us
    unnamed x8, local copies, waits for them, and re-layouts  3.18 us

profile of v8, /device:TPU:1, one launch (start us, length us, event | category | flops | bytes accessed | tf_op | source)
XLA Modules:
  0.0 152.5 jit_solution(11926591626556264668)
XLA Ops:
  0.6 58.4 %shard_map.50 = (f32[8,32,128]{2,1,0:T(8,128)}, f32[4,16,64]{2,1,0:T(8,128)}, f32[2,8,32]{2,1,0:T(8,128)}, f32[4,16,64]{2,1,0:T(8,128)}, f32[2,8,32]{2,1,0:T(8,1...) custom-call(f32[8,32,128]{2,1,0:T(8,128)} %refs_0_.3, ...), custom_call_target="tpu_custom_call" | custom-call | tf_op jit(solution)/shard_map/pallas_call | solution.py:510
  59.0 0.7 pad_maximum_fusion
  59.8 0.6 pad.41.row_ref
  60.4 21.1 %shard_map.51 = f32[4,8,8,256]{3,2,1,0:T(8,128)} custom-call(f32[1,256]{1,0:T(1,128)} %pad.41.row_ref), custom_call_target="tpu_custom_call" | custom-call | tf_op jit(solution)/shard_map/pallas_call | solution.py:588
  81.5 1.7 %reshape.44 = f32[4,8,8,3,1,4,16]{6,5,3,2,1,0,4:T(4,128)S(1)} reshape(f32[4,8,8,192]{3,2,1,0:T(8,128)} %bitcast.27) | data formatting | bytes 393216 | tf_op jit(solution)/shard_map/reshape | solution.py:602
  83.2 0.2 copy.36
  83.4 0.2 fusion.183
  83.6 0.2 squeeze.7
  83.8 0.2 mul.398
  84.0 0.2 squeeze.8
  84.3 0.1 fusion.163
  84.4 0.1 fusion.164
  84.5 0.1 fusion.165
  84.7 0.1 fusion.166
  84.8 0.1 fusion.167
  84.9 0.1 fusion.168
  85.0 0.1 fusion.169
  85.2 0.1 fusion.170
  85.3 0.1 fusion.171
  85.4 0.1 fusion.175
  86.0 0.6 broadcast_add_fusion.refs_3_
  86.6 16.4 %shard_map.52 = f32[2,8,32]{2,1,0:T(8,128)} custom-call(f32[2,8,32]{2,1,0:T(8,128)} %get-tuple-element.19.refs_0_, f32[2,8,32]{2,1,0:T(8,128)} %get-tuple-element.20.refs_1_, f32[2,8,32]{2,1,0:T(8,128)} %get-tuple-element.21.refs_2_, f32[2,8,32]{2,1,0:T(8,128)} %broadcast_add_fusion.refs_3_), custom_call_target="tpu_custom_call" | custom-call | tf_op jit(solution)/shard_map/pallas_call | solution.py:250
  103.0 0.7 broadcast_in_dim.36
  103.9 0.6 add.404.refs_3_
  104.5 19.0 %shard_map.53 = f32[4,16,64]{2,1,0:T(8,128)} custom-call(f32[4,16,64]{2,1,0:T(8,128)} %get-tuple-element.15.refs_0_, f32[4,16,64]{2,1,0:T(8,128)} %get-tuple-element.16.refs_1_, f32[4,16,64]{2,1,0:T(8,128)} %get-tuple-element.17.refs_2_, f32[4,16,64]{2,1,0:T(8,128)} %add.404.refs_3_), custom_call_target="tpu_custom_call" | custom-call | tf_op jit(solution)/shard_map/pallas_call | solution.py:250
  123.5 0.8 copy.32
  124.4 0.2 copy.33
  124.6 0.2 copy.34
  124.8 0.7 add.405.refs_3_
  125.5 23.9 %shard_map.54 = (f32[8,32,128]{2,1,0:T(8,128)}, f32[8,32,128]{2,1,0:T(8,128)}) custom-call(f32[8,32,128]{2,1,0:T(8,128)} %refs_0_.3, f32[8,32,128]{2,1,0:T(8,128)} %refs_1_.3, f32[8,32,128]{2,1,0:T(8,128)} %refs_2_.3, f32[8,32,128]{2,1,0:T(8,128)} %add.405.refs_3_), custom_call_target="tpu_custom_call" | custom-call | tf_op jit(solution)/shard_map/pallas_call | solution.py:250
  149.4 1.6 %copy.39 = f32[8,32,128]{2,1,0:T(8,128)} copy(f32[8,32,128]{2,1,0:T(8,128)} %get-tuple-element.60) | data formatting | bytes 262144
  151.0 1.6 %copy.40 = f32[8,32,128]{2,1,0:T(8,128)} copy(f32[8,32,128]{2,1,0:T(8,128)} %get-tuple-element.61) | data formatting | bytes 262144
  (21 shorter events, 0.9 us)
Async XLA Ops:
  85.3 0.7 copy-start.2
  85.4 18.5 %copy-start.1 = (f32[4,16,64]{2,1,0:T(8,128)S(1)}, f32[4,16,64]{2,1,0:T(8,128)}, u32[]{:S(2)}) copy-start(f32[4,16,64]{2,1,0:T(8,128)} %get-tuple-element.18) | copy-start | bytes 49156
  85.7 39.1 %copy-start = (f32[8,32,128]{2,1,0:T(8,128)S(1)}, f32[8,32,128]{2,1,0:T(8,128)}, u32[]{:S(2)}) copy-start(f32[8,32,128]{2,1,0:T(8,128)} %get-tuple-element.14) | copy-start | bytes 393220

commit v9 on v8

--- a/solution.py
+++ b/solution.py
@@ -437,7 +437,144 @@
             dbuf[i] = apply_rows(v_out, b_ref, slot, i, columns)
         restrict_into(dbuf, next_rhs, 0.5)
 
-    return zero_halos, exchange_start, exchange_finish, build_coef, smooth_down
+    def smooth_up(b_ref, v_out, count, lower, first_slot, first_waits, residual_out):
+        start = fld.at[1]
+        if first_waits is None:
+            exchange(start, first_slot)
+        else:
+            exchange_finish(first_waits)
+        center = (UPPER_EIG + lower) / 2.0
+        half_width = (UPPER_EIG - lower) / 2.0
+        sigma_ratio = center / half_width
+        rho_old = 1.0 / sigma_ratio
+        columns = z_columns(first_slot)
+        for i in range(A):
+            remain = apply_rows(start, b_ref, first_slot, i, columns)
+            update = remain / coef[6, i] / center
+            dbuf[i] = update
+            fld[0, i] = start[i] + update
+        current = 0
+        slot = first_slot
+        for sweep in range(count - 1):
+            rho_new = 1.0 / (2.0 * sigma_ratio - rho_old)
+            slot = (slot + 1) % SLOTS
+            src = fld.at[current]
+            exchange(src, slot)
+            columns = z_columns(slot)
+            dst = v_out if sweep == count - 2 else fld.at[1 - current]
+            for i in range(A):
+                remain = apply_rows(src, b_ref, slot, i, columns)
+                update = (rho_new * rho_old) * dbuf[i] + (2.0 * rho_new / half_width) * (
+                    remain / coef[6, i]
+                )
+                dbuf[i] = update
+                dst[i] = src[i] + update
+            rho_old = rho_new
+            current = 1 - current
+        if residual_out is not None:
+            slot = (slot + 1) % SLOTS
+            exchange(v_out, slot)
+            columns = z_columns(slot)
+            for i in range(A):
+                residual_out[i] = apply_rows(v_out, b_ref, slot, i, columns)
+
+    def prolong_start(coarse, smoothed):
+        fine_rows = (
+            lax.broadcasted_iota(jnp.int32, (B, B // 2), 0) // 2
+            == lax.broadcasted_iota(jnp.int32, (B, B // 2), 1)
+        ).astype(jnp.float32)
+        fine_cols = (
+            lax.broadcasted_iota(jnp.int32, (C // 2, C), 1) // 2
+            == lax.broadcasted_iota(jnp.int32, (C // 2, C), 0)
+        ).astype(jnp.float32)
+        for i in range(A):
+            half = jnp.dot(
+                fine_rows, coarse[i // 2], precision=lax.Precision.HIGHEST,
+                preferred_element_type=jnp.float32,
+            )
+            fine = jnp.dot(
+                half, fine_cols, precision=lax.Precision.HIGHEST,
+                preferred_element_type=jnp.float32,
+            )
+            fld[1, i] = smoothed[i] + fine
+
+    return (
+        zero_halos, exchange_start, exchange_finish, build_coef, smooth_down, smooth_up,
+        prolong_start, fld,
+    )
+
+
+def up_kernel(cfg, *refs):
+    sizes, shapes, shifts = cfg
+    depth = len(shapes)
+    coarsest = refs[0]
+    level_in = [refs[1 + 4 * l : 5 + 4 * l] for l in range(depth)]
+    solution_out, residual_out = refs[1 + 4 * depth : 3 + 4 * depth]
+    scratch = refs[3 + 4 * depth :]
+    results = scratch[7 * depth : 7 * depth + depth - 1]
+    send_sem, recv_sem = scratch[8 * depth - 1], scratch[8 * depth]
+    targets = neighbour_targets(sizes)
+    barrier = pltpu.get_barrier_semaphore()
+    total = jnp.int32(0)
+    for exists, device in targets:
+
+        @pl.when(exists)
+        def _():
+            pl.semaphore_signal(barrier, inc=1, device_id=device, device_id_type=MESH)
+
+        total = total + exists.astype(jnp.int32)
+    tools = [
+        level_tools(shapes[l], l, targets, scratch[7 * l : 7 * l + 7], send_sem, recv_sem)
+        for l in range(depth)
+    ]
+    for tool in tools:
+        tool[0]()
+    top = depth - 1
+    tools[top][6](coarsest, level_in[top][0])
+    pl.semaphore_wait(barrier, total)
+    first_waits = tools[top][1](tools[top][7].at[1], 1)
+    waits = [tools[l][1](level_in[l][2], 0) for l in range(depth)]
+    for l in range(depth):
+        tools[l][2](waits[l])
+        tools[l][3](level_in[l][2], level_in[l][3], 0, shifts[l])
+    coarse = None
+    for l in range(top, -1, -1):
+        if l < top:
+            tools[l][6](coarse, level_in[l][0])
+        v_out = solution_out if l == 0 else results[l - 1]
+        tools[l][5](
+            level_in[l][1], v_out, SWEEPS, SMOOTH_LOWER, 1,
+            first_waits if l == top else None, residual_out if l == 0 else None,
+        )
+        coarse = v_out
+
+
+def up_chain(coarsest, smoothed, rhs_levels, betas, alphas):
+    sizes = tuple(lax.axis_size(axis) for axis in AXES)
+    shapes = [tuple(x.shape) for x in smoothed]
+    shifts = tuple(SHIFT_BASE * 4.0**l for l in range(LEVELS))
+    cfg = (sizes, tuple(shapes), shifts)
+    vmem = pl.BlockSpec(memory_space=pltpu.VMEM)
+    args = [coarsest]
+    for l in range(LEVELS):
+        args += [smoothed[l], rhs_levels[l], betas[l], alphas[l]]
+    scratch = []
+    for s in shapes:
+        scratch += level_scratch(s)
+    scratch += [pltpu.VMEM(s, jnp.float32) for s in shapes[1:]]
+    scratch += [
+        pltpu.SemaphoreType.DMA((LEVELS, SLOTS, 6)),
+        pltpu.SemaphoreType.DMA((LEVELS, SLOTS, 6)),
+    ]
+    fine = jax.ShapeDtypeStruct(shapes[0], jnp.float32)
+    return pl.pallas_call(
+        functools.partial(up_kernel, cfg),
+        out_shape=(fine, fine),
+        in_specs=[vmem] * len(args),
+        out_specs=(vmem, vmem),
+        scratch_shapes=scratch,
+        compiler_params=pltpu.CompilerParams(collective_id=48, has_side_effects=True),
+    )(*args)
 
 
 def level_scratch(shape):
@@ -689,18 +826,7 @@
     )
     starts = (index_x * local_shape[0], index_y * local_shape[1], index_z * local_shape[2])
     correction = lax.dynamic_slice(whole_correction, starts, local_shape)
-    for level in range(LEVELS - 1, -1, -1):
-        start_field = smoothed[level] + prolong_copy(correction)
-        outs = smooth(
-            (rhs_levels[level], betas[level], alphas[level], start_field),
-            SHIFT_BASE * 4.0**level,
-            SWEEPS,
-            SMOOTH_LOWER,
-            False,
-            level == 0,
-        )
-        correction = outs[0]
-    residual_field = outs[1]
+    correction, residual_field = up_chain(correction, smoothed, rhs_levels, betas, alphas)
     return (correction, residual_field)
 
 

time: 153 us -> 144 us (0.941)
  Pallas kernels: 139 us -> 134 us
  local copies, waits for them, and re-layouts: 8.56 us -> 6.25 us
    pallas_call x3 -> x1, Pallas kernels: 59.3 us -> 54.5 us  [up_chain(): pl.pallas_call(functools.partial(up_kernel, cfg), out_shape=(fine, fine),...]
    add x3 -> x0, other arithmetic: 1.93 us -> none  [shards(): start_field = smoothed[level] + prolong_copy(correction)]
    unnamed x8 -> x2, local copies, waits for them, and re-layouts: 3.18 us -> 3.14 us
where the time goes in v9:
time: 144 us
  Pallas kernels  134 us (93%)
  local copies, waits for them, and re-layouts  6.25 us (4%)
  other arithmetic  2.95 us (2%)
    pallas_call x1, Pallas kernels, down_chain(): pl.pallas_call(functools.partial(down_kernel, cfg), out_shape=tuple(out_s...  58.4 us
    pallas_call x1, Pallas kernels, up_chain(): pl.pallas_call(functools.partial(up_kernel, cfg), out_shape=(fine, fine),...  54.5 us
    pallas_call x1, Pallas kernels, gather_bottom(): pl.pallas_call(functools.partial(gather_kernel, sizes), out_shape=jax.Sha...  21.1 us
    unnamed x2, local copies, waits for them, and re-layouts  3.14 us

profile of v9, /device:TPU:1, one launch (start us, length us, event | category | flops | bytes accessed | tf_op | source)
XLA Modules:
  0.0 143.9 jit_solution(581353981996936710)
XLA Ops:
  0.6 58.4 %shard_map.50 = (f32[8,32,128]{2,1,0:T(8,128)}, f32[4,16,64]{2,1,0:T(8,128)}, f32[2,8,32]{2,1,0:T(8,128)}, f32[4,16,64]{2,1,0:T(8,128)}, f32[2,8,32]{2,1,0:T(8,1...) custom-call(f32[8,32,128]{2,1,0:T(8,128)} %refs_2_.3, ...), custom_call_target="tpu_custom_call" | custom-call | tf_op jit(solution)/shard_map/pallas_call | solution.py:647
  59.0 0.7 pad_maximum_fusion
  59.7 0.1 reshape.19
  59.8 0.6 pad.41.row_ref
  60.4 21.1 %shard_map.51 = f32[4,8,8,256]{3,2,1,0:T(8,128)} custom-call(f32[1,256]{1,0:T(1,128)} %pad.41.row_ref), custom_call_target="tpu_custom_call" | custom-call | tf_op jit(solution)/shard_map/pallas_call | solution.py:725
  81.5 1.7 %reshape.20 = f32[4,8,8,3,1,4,16]{6,5,3,2,1,0,4:T(4,128)S(1)} reshape(f32[4,8,8,192]{3,2,1,0:T(8,128)} %bitcast.22) | data formatting | bytes 393216 | tf_op jit(solution)/shard_map/reshape | solution.py:739
  83.2 0.2 copy.7
  83.4 0.2 fusion.182
  83.6 0.2 squeeze.7
  83.8 0.2 mul.398
  84.0 0.2 squeeze.8
  84.2 0.1 broadcast_multiply_fusion
  84.3 0.1 fusion.163
  84.4 0.1 fusion.164
  84.5 0.1 fusion.165
  84.7 0.1 fusion.166
  84.8 0.1 fusion.167
  84.9 0.1 fusion.168
  85.0 0.1 fusion.169
  85.2 0.1 fusion.170
  85.3 0.1 fusion.171
  85.4 0.1 fusion.174
  85.5 0.1 fusion.157
  85.7 0.7 dynamic-slice_add_fusion.refs_0_
  86.3 54.5 %shard_map.52 = (f32[8,32,128]{2,1,0:T(8,128)}, f32[8,32,128]{2,1,0:T(8,128)}) custom-call(f32[1,4,16]{2,1,0:T(4,128)} %dynamic-slice_add_fusion.refs_0_, f32[8,32,128]{2,1,0:T(8,128)} %get-tuple-element.17.refs_1_, f32[8,32,128]{2,1,0:T(8,128)} %refs_2_.3, f32[8,32,128]{2,1,0:T(8,128)} %refs_3_.1, f32[8,32,128]{2,1,0:T(8,128)} %refs_4_.1, ...), custom_call_target="tpu_custom_call" | custom-call | tf_op jit(solution)/shard_map/pallas_call | solution.py:570
  140.8 1.6 %copy.10 = f32[8,32,128]{2,1,0:T(8,128)} copy(f32[8,32,128]{2,1,0:T(8,128)} %get-tuple-element.60) | data formatting | bytes 262144
  142.4 1.6 %copy.11 = f32[8,32,128]{2,1,0:T(8,128)} copy(f32[8,32,128]{2,1,0:T(8,128)} %get-tuple-element.61) | data formatting | bytes 262144

commit v10 on v9

--- a/solution.py
+++ b/solution.py
@@ -659,59 +659,77 @@
     return iterates, rhs_levels, betas, alphas
 
 
-def gather_kernel(sizes, row_ref, out_ref, first, dense, second, send_sem, recv_sem):
+def gather_kernel(sizes, row_ref, out_ref, first, dense, send_sem, recv_sem):
     index = [lax.axis_index(axis) for axis in AXES]
     nx, ny, nz = sizes
-
-    def device(axis, step):
-        return tuple(
-            lax.rem(index[a] + step, sizes[a]) if a == axis else index[a] for a in range(3)
-        )
+    ix, iy, iz = index
+    line = [(ix, iy, lax.rem(iz + step, nz)) for step in range(1, nz)]
+    plane = []
+    for dx in range(nx):
+        for dy in range(ny):
+            if dx or dy:
+                plane.append(((dx, dy), (lax.rem(ix + dx, nx), lax.rem(iy + dy, ny), iz)))
 
     barrier = pltpu.get_barrier_semaphore()
-    partners = []
-    for axis in (2, 1, 0):
-        partners.append([device(axis, step) for step in range(1, sizes[axis])])
-    for group in partners:
-        for peer in group:
-            pl.semaphore_signal(barrier, inc=1, device_id=peer, device_id_type=MESH)
-    pl.semaphore_wait(barrier, sum(len(group) for group in partners))
-
-    stages = ((row_ref, first, 2), (dense, second, 1), (second, out_ref, 0))
-    for stage, (source, target, axis) in enumerate(stages):
-        mine = index[axis]
-        waits = []
-        for step in range(1, sizes[axis]):
-            peer = device(axis, step)
-            copy = pltpu.make_async_remote_copy(
-                src_ref=source,
-                dst_ref=target.at[mine],
-                send_sem=send_sem.at[stage, step],
-                recv_sem=recv_sem.at[stage, mine],
-                device_id=peer,
-                device_id_type=MESH,
-            )
-            copy.start()
-            origin = lax.rem(mine + sizes[axis] - step, sizes[axis])
-            incoming = pltpu.make_async_remote_copy(
-                src_ref=source,
-                dst_ref=target.at[origin],
-                send_sem=send_sem.at[stage, step],
-                recv_sem=recv_sem.at[stage, origin],
-                device_id=peer,
-                device_id_type=MESH,
-            )
-            waits.append((copy, incoming))
-        if stage == 0:
-            target[mine] = source[...]
-        else:
-            target[mine] = source[...]
-        for copy, incoming in waits:
-            copy.wait_send()
-            incoming.wait_recv()
-        if stage == 0:
-            for z in range(nz):
-                dense[z : z + 1, :] = first[z]
+    for peer in line + [peer for _, peer in plane]:
+        pl.semaphore_signal(barrier, inc=1, device_id=peer, device_id_type=MESH)
+    pl.semaphore_wait(barrier, len(line) + len(plane))
+
+    waits = []
+    for step in range(1, nz):
+        copy = pltpu.make_async_remote_copy(
+            src_ref=row_ref,
+            dst_ref=first.at[iz],
+            send_sem=send_sem.at[0, step],
+            recv_sem=recv_sem.at[0, iz],
+            device_id=line[step - 1],
+            device_id_type=MESH,
+        )
+        copy.start()
+        origin = lax.rem(iz + nz - step, nz)
+        incoming = pltpu.make_async_remote_copy(
+            src_ref=row_ref,
+            dst_ref=first.at[origin],
+            send_sem=send_sem.at[0, step],
+            recv_sem=recv_sem.at[0, origin],
+            device_id=line[step - 1],
+            device_id_type=MESH,
+        )
+        waits.append((copy, incoming))
+    first[iz] = row_ref[...]
+    for copy, incoming in waits:
+        copy.wait_send()
+        incoming.wait_recv()
+    for z in range(nz):
+        dense[z : z + 1, :] = first[z]
+
+    mine = ix * ny + iy
+    waits = []
+    for n, ((dx, dy), peer) in enumerate(plane):
+        copy = pltpu.make_async_remote_copy(
+            src_ref=dense,
+            dst_ref=out_ref.at[ix, iy],
+            send_sem=send_sem.at[1, n],
+            recv_sem=recv_sem.at[1, mine],
+            device_id=peer,
+            device_id_type=MESH,
+        )
+        copy.start()
+        ox = lax.rem(ix + nx - dx, nx)
+        oy = lax.rem(iy + ny - dy, ny)
+        incoming = pltpu.make_async_remote_copy(
+            src_ref=dense,
+            dst_ref=out_ref.at[ox, oy],
+            send_sem=send_sem.at[1, n],
+            recv_sem=recv_sem.at[1, ox * ny + oy],
+            device_id=peer,
+            device_id_type=MESH,
+        )
+        waits.append((copy, incoming))
+    out_ref[ix, iy] = dense[...]
+    for copy, incoming in waits:
+        copy.wait_send()
+        incoming.wait_recv()
 
 
 def gather_bottom(packed):
@@ -721,7 +739,7 @@
     lanes = -(-width // 128) * 128
     row = jnp.pad(packed.reshape(1, width), ((0, 0), (0, lanes - width)))
     vmem = pl.BlockSpec(memory_space=pltpu.VMEM)
-    top = max(sizes)
+    top = max(nz, nx * ny)
     whole = pl.pallas_call(
         functools.partial(gather_kernel, sizes),
         out_shape=jax.ShapeDtypeStruct((nx, ny, nz, lanes), jnp.float32),
@@ -730,9 +748,8 @@
         scratch_shapes=[
             pltpu.VMEM((nz, 1, lanes), jnp.float32),
             pltpu.VMEM((nz, lanes), jnp.float32),
-            pltpu.VMEM((ny, nz, lanes), jnp.float32),
-            pltpu.SemaphoreType.DMA((3, top)),
-            pltpu.SemaphoreType.DMA((3, top)),
+            pltpu.SemaphoreType.DMA((2, top)),
+            pltpu.SemaphoreType.DMA((2, top)),
         ],
         compiler_params=pltpu.CompilerParams(collective_id=64, has_side_effects=True),
     )(row)

time: 144 us -> 142 us (0.986)
  Pallas kernels: 134 us -> 131 us
    pallas_call x1, Pallas kernels: 21.1 us -> 18.9 us  [gather_bottom(): pl.pallas_call(functools.partial(gather_kernel, sizes), out_shape=jax.Sha...]
where the time goes in v10:
time: 142 us; the launch traced here: 141 us
  Pallas kernels  131 us (92%)
  local copies, waits for them, and re-layouts  6.25 us (4%)
  other arithmetic  2.95 us (2%)
    pallas_call x1, Pallas kernels, down_chain(): pl.pallas_call(functools.partial(down_kernel, cfg), out_shape=tuple(out_s...  58.4 us
    pallas_call x1, Pallas kernels, up_chain(): pl.pallas_call(functools.partial(up_kernel, cfg), out_shape=(fine, fine),...  54 us
    pallas_call x1, Pallas kernels, gather_bottom(): pl.pallas_call(functools.partial(gather_kernel, sizes), out_shape=jax.Sha...  18.9 us
    unnamed x2, local copies, waits for them, and re-layouts  3.14 us

profile of v10, /device:TPU:1, one launch (start us, length us, event | category | flops | bytes accessed | tf_op | source)
XLA Modules:
  0.0 141.3 jit_solution(1077100094964123391)
XLA Ops:
  0.6 58.4 %shard_map.50 = (f32[8,32,128]{2,1,0:T(8,128)}, f32[4,16,64]{2,1,0:T(8,128)}, f32[2,8,32]{2,1,0:T(8,128)}, f32[4,16,64]{2,1,0:T(8,128)}, f32[2,8,32]{2,1,0:T(8,1...) custom-call(f32[8,32,128]{2,1,0:T(8,128)} %refs_2_.3, ...), custom_call_target="tpu_custom_call" | custom-call | tf_op jit(solution)/shard_map/pallas_call | solution.py:647
  59.0 0.7 pad_maximum_fusion
  59.7 0.1 reshape.19
  59.8 0.6 pad.41.row_ref
  60.4 18.9 %shard_map.51 = f32[4,8,8,256]{3,2,1,0:T(8,128)} custom-call(f32[1,256]{1,0:T(1,128)} %pad.41.row_ref), custom_call_target="tpu_custom_call" | custom-call | tf_op jit(solution)/shard_map/pallas_call | solution.py:743
  79.3 1.7 %reshape.20 = f32[4,8,8,3,1,4,16]{6,5,3,2,1,0,4:T(4,128)S(1)} reshape(f32[4,8,8,192]{3,2,1,0:T(8,128)} %bitcast.22) | data formatting | bytes 393216 | tf_op jit(solution)/shard_map/reshape | solution.py:756
  81.0 0.2 copy.7
  81.2 0.2 fusion.182
  81.4 0.2 squeeze.7
  81.6 0.2 mul.398
  81.8 0.2 squeeze.8
  82.0 0.1 broadcast_multiply_fusion
  82.1 0.1 fusion.163
  82.2 0.1 fusion.164
  82.3 0.1 fusion.165
  82.5 0.1 fusion.166
  82.6 0.1 fusion.167
  82.7 0.1 fusion.168
  82.8 0.1 fusion.169
  83.0 0.1 fusion.170
  83.1 0.1 fusion.171
  83.2 0.1 fusion.174
  83.4 0.1 fusion.157
  83.5 0.7 dynamic-slice_add_fusion.refs_0_
  84.1 54.0 %shard_map.52 = (f32[8,32,128]{2,1,0:T(8,128)}, f32[8,32,128]{2,1,0:T(8,128)}) custom-call(f32[1,4,16]{2,1,0:T(4,128)} %dynamic-slice_add_fusion.refs_0_, f32[8,32,128]{2,1,0:T(8,128)} %get-tuple-element.17.refs_1_, f32[8,32,128]{2,1,0:T(8,128)} %refs_2_.3, f32[8,32,128]{2,1,0:T(8,128)} %refs_3_.1, f32[8,32,128]{2,1,0:T(8,128)} %refs_4_.1, ...), custom_call_target="tpu_custom_call" | custom-call | tf_op jit(solution)/shard_map/pallas_call | solution.py:570
  138.1 1.6 %copy.10 = f32[8,32,128]{2,1,0:T(8,128)} copy(f32[8,32,128]{2,1,0:T(8,128)} %get-tuple-element.60) | data formatting | bytes 262144
  139.7 1.6 %copy.11 = f32[8,32,128]{2,1,0:T(8,128)} copy(f32[8,32,128]{2,1,0:T(8,128)} %get-tuple-element.61) | data formatting | bytes 262144

commit v11 on v10

--- a/solution.py
+++ b/solution.py
@@ -599,18 +599,16 @@
     rhs = [b0] + list(outs[depth : 2 * depth])
     betas = [beta0] + list(outs[2 * depth : 3 * depth])
     alphas = [alpha0] + list(outs[3 * depth : 4 * depth])
-    scratch = refs[3 + 4 * depth :]
+    gathered = refs[3 + 4 * depth]
+    scratch = refs[4 + 4 * depth :]
     send_sem, recv_sem = scratch[7 * depth], scratch[7 * depth + 1]
+    row, first, dense, gsend, grecv = scratch[7 * depth + 2 :]
     targets = neighbour_targets(sizes)
+    line, plane = gather_peers(sizes)
     barrier = pltpu.get_barrier_semaphore()
-    total = jnp.int32(0)
-    for exists, device in targets:
-
-        @pl.when(exists)
-        def _():
-            pl.semaphore_signal(barrier, inc=1, device_id=device, device_id_type=MESH)
-
-        total = total + exists.astype(jnp.int32)
+    for peer in line + [peer for _, peer in plane]:
+        pl.semaphore_signal(barrier, inc=1, device_id=peer, device_id_type=MESH)
+    total = len(line) + len(plane)
     tools = [
         level_tools(shapes[l], l, targets, scratch[7 * l : 7 * l + 7], send_sem, recv_sem)
         for l in range(depth)
@@ -627,6 +625,29 @@
         tools[l][3](betas[l], alphas[l], 0, shifts[l])
     for l in range(depth):
         tools[l][4](rhs[l], iterates[l], rhs[l + 1], SWEEPS, SMOOTH_LOWER)
+    lanes = row.shape[1]
+    packed = jnp.zeros((1, lanes), jnp.float32)
+    offset = 0
+    for part in (rhs[depth], betas[depth], alphas[depth]):
+        pa, pb, pc = part.shape
+        for x in range(pa):
+            for j in range(pb):
+                pick = (lax.broadcasted_iota(jnp.int32, (1, pb), 1) == j).astype(jnp.float32)
+                line_values = jnp.dot(
+                    pick, part[x], precision=lax.Precision.HIGHEST,
+                    preferred_element_type=jnp.float32,
+                )
+                place = (
+                    lax.broadcasted_iota(jnp.int32, (pc, lanes), 0) + offset
+                    == lax.broadcasted_iota(jnp.int32, (pc, lanes), 1)
+                ).astype(jnp.float32)
+                packed = packed + jnp.dot(
+                    line_values, place, precision=lax.Precision.HIGHEST,
+                    preferred_element_type=jnp.float32,
+                )
+                offset += pc
+    row[...] = packed
+    gather_stages(sizes, line, plane, row, gathered, first, dense, gsend, grecv)
 
 
 def down_chain(right_side, beta_coef, alpha_coef):
@@ -640,9 +661,19 @@
     scratch = []
     for s in shapes[:LEVELS]:
         scratch += level_scratch(s)
+    nx, ny, nz = sizes
+    width = 3 * shapes[LEVELS][0] * shapes[LEVELS][1] * shapes[LEVELS][2]
+    lanes = -(-width // 128) * 128
+    top = max(nz, nx * ny)
+    out_shapes.append(jax.ShapeDtypeStruct((nx, ny, nz, lanes), jnp.float32))
     scratch += [
         pltpu.SemaphoreType.DMA((LEVELS, SLOTS, 6)),
         pltpu.SemaphoreType.DMA((LEVELS, SLOTS, 6)),
+        pltpu.VMEM((1, lanes), jnp.float32),
+        pltpu.VMEM((nz, 1, lanes), jnp.float32),
+        pltpu.VMEM((nz, lanes), jnp.float32),
+        pltpu.SemaphoreType.DMA((2, top)),
+        pltpu.SemaphoreType.DMA((2, top)),
     ]
     outs = pl.pallas_call(
         functools.partial(down_kernel, cfg),
@@ -656,10 +687,13 @@
     rhs_levels = [right_side] + list(outs[LEVELS : 2 * LEVELS])
     betas = [beta_coef] + list(outs[2 * LEVELS : 3 * LEVELS])
     alphas = [alpha_coef] + list(outs[3 * LEVELS : 4 * LEVELS])
-    return iterates, rhs_levels, betas, alphas
-
-
-def gather_kernel(sizes, row_ref, out_ref, first, dense, send_sem, recv_sem):
+    whole = outs[4 * LEVELS][..., :width].reshape((nx, ny, nz, 3) + shapes[LEVELS])
+    whole = whole.transpose(3, 0, 4, 1, 5, 2, 6)
+    whole = whole.reshape((3,) + tuple(n * s for n, s in zip(sizes, shapes[LEVELS])))
+    return iterates, rhs_levels, betas, alphas, whole
+
+
+def gather_peers(sizes):
     index = [lax.axis_index(axis) for axis in AXES]
     nx, ny, nz = sizes
     ix, iy, iz = index
@@ -670,11 +704,13 @@
             if dx or dy:
                 plane.append(((dx, dy), (lax.rem(ix + dx, nx), lax.rem(iy + dy, ny), iz)))
 
-    barrier = pltpu.get_barrier_semaphore()
-    for peer in line + [peer for _, peer in plane]:
-        pl.semaphore_signal(barrier, inc=1, device_id=peer, device_id_type=MESH)
-    pl.semaphore_wait(barrier, len(line) + len(plane))
-
+    return line, plane
+
+
+def gather_stages(sizes, line, plane, row_ref, out_ref, first, dense, send_sem, recv_sem):
+    index = [lax.axis_index(axis) for axis in AXES]
+    nx, ny, nz = sizes
+    ix, iy, iz = index
     waits = []
     for step in range(1, nz):
         copy = pltpu.make_async_remote_copy(
@@ -730,6 +766,15 @@
     for copy, incoming in waits:
         copy.wait_send()
         incoming.wait_recv()
+
+
+def gather_kernel(sizes, row_ref, out_ref, first, dense, send_sem, recv_sem):
+    line, plane = gather_peers(sizes)
+    barrier = pltpu.get_barrier_semaphore()
+    for peer in line + [peer for _, peer in plane]:
+        pl.semaphore_signal(barrier, inc=1, device_id=peer, device_id_type=MESH)
+    pl.semaphore_wait(barrier, len(line) + len(plane))
+    gather_stages(sizes, line, plane, row_ref, out_ref, first, dense, send_sem, recv_sem)
 
 
 def gather_bottom(packed):
@@ -824,14 +869,11 @@
 
 
 def shards(right_side, alpha_coef, beta_coef):
-    smoothed, rhs_levels, betas, alphas = down_chain(right_side, beta_coef, alpha_coef)
-    coarse_rhs = rhs_levels[LEVELS]
-    local_shape = coarse_rhs.shape
-    packed = jnp.stack([coarse_rhs, betas[LEVELS], alphas[LEVELS]])
+    smoothed, rhs_levels, betas, alphas, packed = down_chain(right_side, beta_coef, alpha_coef)
+    local_shape = rhs_levels[LEVELS].shape
     index_x = lax.axis_index("gx")
     index_y = lax.axis_index("gy")
     index_z = lax.axis_index("gz")
-    packed = gather_bottom(packed)
     whole_rhs = packed[0]
     whole_beta = packed[1]
     whole_alpha = packed[2]

time: 142 us -> 137 us (0.965)
  Pallas kernels: 131 us -> 128 us
    pallas_call x1 -> x0, Pallas kernels: 18.9 us -> none  [gather_bottom(): pl.pallas_call(functools.partial(gather_kernel, sizes), out_shape=jax.Sha...]
    pallas_call x1, Pallas kernels: 58.4 us -> 76.2 us  [down_chain(): pl.pallas_call(functools.partial(down_kernel, cfg), out_shape=tuple(out_s...]
    pallas_call x1, Pallas kernels: 54 us -> 51.5 us  [up_chain(): pl.pallas_call(functools.partial(up_kernel, cfg), out_shape=(fine, fine),...]
where the time goes in v11:
time: 137 us; the launch traced here: 136 us
  Pallas kernels  128 us (93%)
  local copies, waits for them, and re-layouts  5.59 us (4%)
  other arithmetic  2.28 us (2%)
    pallas_call x1, Pallas kernels, down_chain(): pl.pallas_call(functools.partial(down_kernel, cfg), out_shape=tuple(out_s...  76.2 us
    pallas_call x1, Pallas kernels, up_chain(): pl.pallas_call(functools.partial(up_kernel, cfg), out_shape=(fine, fine),...  51.5 us
    unnamed x2, local copies, waits for them, and re-layouts  3.14 us

profile of v11, /device:TPU:1, one launch (start us, length us, event | category | flops | bytes accessed | tf_op | source)
XLA Modules:
  0.0 136.4 jit_solution(4186017781228860471)
XLA Ops:
  0.6 76.2 %shard_map.50 = (f32[8,32,128]{2,1,0:T(8,128)}, f32[4,16,64]{2,1,0:T(8,128)}, f32[2,8,32]{2,1,0:T(8,128)}, f32[4,16,64]{2,1,0:T(8,128)}, f32[2,8,32]{2,1,0:T(8,1...) custom-call(f32[8,32,128]{2,1,0:T(8,128)} %refs_2_.3, ...), custom_call_target="tpu_custom_call" | custom-call | tf_op jit(solution)/shard_map/pallas_call | solution.py:678
  76.8 1.7 %reshape.16 = f32[4,8,8,3,1,4,16]{6,5,3,2,1,0,4:T(4,128)S(1)} reshape(f32[4,8,8,192]{3,2,1,0:T(8,128)} %bitcast.19) | data formatting | bytes 393216 | tf_op jit(solution)/shard_map/reshape | solution.py:690
  78.6 0.2 copy.7
  78.7 0.2 fusion.182
  78.9 0.2 squeeze.7
  79.1 0.2 mul.398
  79.3 0.2 squeeze.8
  79.5 0.1 broadcast_multiply_fusion
  79.6 0.1 fusion.163
  79.8 0.1 fusion.164
  79.9 0.1 fusion.165
  80.0 0.1 fusion.166
  80.1 0.1 fusion.167
  80.3 0.1 fusion.168
  80.4 0.1 fusion.169
  80.5 0.1 fusion.170
  80.6 0.1 fusion.171
  80.8 0.1 fusion.174
  80.9 0.1 fusion.157
  81.0 0.7 dynamic-slice_add_fusion.refs_0_
  81.7 51.5 %shard_map.51 = (f32[8,32,128]{2,1,0:T(8,128)}, f32[8,32,128]{2,1,0:T(8,128)}) custom-call(f32[1,4,16]{2,1,0:T(4,128)} %dynamic-slice_add_fusion.refs_0_, f32[8,32,128]{2,1,0:T(8,128)} %get-tuple-element.13.refs_1_, f32[8,32,128]{2,1,0:T(8,128)} %refs_2_.3, f32[8,32,128]{2,1,0:T(8,128)} %refs_3_.1, f32[8,32,128]{2,1,0:T(8,128)} %refs_4_.1, ...), custom_call_target="tpu_custom_call" | custom-call | tf_op jit(solution)/shard_map/pallas_call | solution.py:570
  133.2 1.6 %copy.10 = f32[8,32,128]{2,1,0:T(8,128)} copy(f32[8,32,128]{2,1,0:T(8,128)} %get-tuple-element.56) | data formatting | bytes 262144
  134.8 1.6 %copy.11 = f32[8,32,128]{2,1,0:T(8,128)} copy(f32[8,32,128]{2,1,0:T(8,128)} %get-tuple-element.57) | data formatting | bytes 262144

commit v12 on v11

--- a/solution.py
+++ b/solution.py
@@ -396,12 +396,15 @@
                 diagonal = diagonal + face
             coef[6, i] = diagonal
 
-    def apply_rows(src, b_ref, slot, i, columns):
+    def apply_op(src, slot, i, columns):
         here, others = sides(src, i, slot, columns)
         acc = coef[0, i] * others[0]
         for k in range(1, 6):
             acc = acc + coef[k, i] * others[k]
-        return b_ref[i] - (coef[6, i] * here - acc)
+        return coef[6, i] * here - acc
+
+    def apply_rows(src, b_ref, slot, i, columns):
+        return b_ref[i] - apply_op(src, slot, i, columns)
 
     def smooth_down(b_ref, v_out, next_rhs, count, lower):
         center = (UPPER_EIG + lower) / 2.0
@@ -437,7 +440,7 @@
             dbuf[i] = apply_rows(v_out, b_ref, slot, i, columns)
         restrict_into(dbuf, next_rhs, 0.5)
 
-    def smooth_up(b_ref, v_out, count, lower, first_slot, first_waits, residual_out):
+    def smooth_up(b_ref, v_out, count, lower, first_slot, first_waits, residual_out, split):
         start = fld.at[1]
         if first_waits is None:
             exchange(start, first_slot)
@@ -469,6 +472,9 @@
                 )
                 dbuf[i] = update
                 dst[i] = src[i] + update
+                if split is not None and sweep == count - 2:
+                    split[0][i] = src[i]
+                    split[1][i] = update
             rho_old = rho_new
             current = 1 - current
         if residual_out is not None:
@@ -476,7 +482,7 @@
             exchange(v_out, slot)
             columns = z_columns(slot)
             for i in range(A):
-                residual_out[i] = apply_rows(v_out, b_ref, slot, i, columns)
+                residual_out[i] = apply_op(v_out, slot, i, columns)
 
     def prolong_start(coarse, smoothed):
         fine_rows = (
@@ -509,10 +515,10 @@
     depth = len(shapes)
     coarsest = refs[0]
     level_in = [refs[1 + 4 * l : 5 + 4 * l] for l in range(depth)]
-    solution_out, residual_out = refs[1 + 4 * depth : 3 + 4 * depth]
-    scratch = refs[3 + 4 * depth :]
-    results = scratch[7 * depth : 7 * depth + depth - 1]
-    send_sem, recv_sem = scratch[8 * depth - 1], scratch[8 * depth]
+    previous_out, update_out, operator_out = refs[1 + 4 * depth : 4 + 4 * depth]
+    scratch = refs[4 + 4 * depth :]
+    results = scratch[7 * depth : 8 * depth]
+    send_sem, recv_sem = scratch[8 * depth], scratch[8 * depth + 1]
     targets = neighbour_targets(sizes)
     barrier = pltpu.get_barrier_semaphore()
     total = jnp.int32(0)
@@ -541,10 +547,11 @@
     for l in range(top, -1, -1):
         if l < top:
             tools[l][6](coarse, level_in[l][0])
-        v_out = solution_out if l == 0 else results[l - 1]
+        v_out = results[l]
         tools[l][5](
             level_in[l][1], v_out, SWEEPS, SMOOTH_LOWER, 1,
-            first_waits if l == top else None, residual_out if l == 0 else None,
+            first_waits if l == top else None, operator_out if l == 0 else None,
+            (previous_out, update_out) if l == 0 else None,
         )
         coarse = v_out
 
@@ -561,20 +568,21 @@
     scratch = []
     for s in shapes:
         scratch += level_scratch(s)
-    scratch += [pltpu.VMEM(s, jnp.float32) for s in shapes[1:]]
+    scratch += [pltpu.VMEM(s, jnp.float32) for s in shapes]
     scratch += [
         pltpu.SemaphoreType.DMA((LEVELS, SLOTS, 6)),
         pltpu.SemaphoreType.DMA((LEVELS, SLOTS, 6)),
     ]
     fine = jax.ShapeDtypeStruct(shapes[0], jnp.float32)
-    return pl.pallas_call(
+    previous, update, operator = pl.pallas_call(
         functools.partial(up_kernel, cfg),
-        out_shape=(fine, fine),
+        out_shape=(fine, fine, fine),
         in_specs=[vmem] * len(args),
-        out_specs=(vmem, vmem),
+        out_specs=(vmem, vmem, vmem),
         scratch_shapes=scratch,
         compiler_params=pltpu.CompilerParams(collective_id=48, has_side_effects=True),
     )(*args)
+    return previous + update, rhs_levels[0] - operator
 
 
 def level_scratch(shape):

time: 137 us -> 137 us (level)
  other arithmetic: 2.28 us -> 5.49 us
  local copies, waits for them, and re-layouts: 5.59 us -> 2.46 us
    unnamed x2, local copies, waits for them, and re-layouts: 3.14 us -> 0.01 us
    add x0 -> x1, other arithmetic: none -> 1.64 us  [up_chain(): return (previous + update, rhs_levels[0] - operator)]
    sub x0 -> x1, other arithmetic: none -> 1.58 us  [up_chain(): return (previous + update, rhs_levels[0] - operator)]
where the time goes in v12:
time: 137 us; the launch traced here: 136 us
  Pallas kernels  128 us (93%)
  other arithmetic  5.49 us (4%)
  local copies, waits for them, and re-layouts  2.46 us (2%)
    pallas_call x1, Pallas kernels, down_chain(): pl.pallas_call(functools.partial(down_kernel, cfg), out_shape=tuple(out_s...  76.2 us
    pallas_call x1, Pallas kernels, up_chain(): pl.pallas_call(functools.partial(up_kernel, cfg), out_shape=(fine, fine,...  51.6 us

profile of v12, /device:TPU:1, one launch (start us, length us, event | category | flops | bytes accessed | tf_op | source)
XLA Modules:
  0.0 136.5 jit_solution(11112449510421003546)
XLA Ops:
  0.6 76.2 %shard_map.50 = (f32[8,32,128]{2,1,0:T(8,128)}, f32[4,16,64]{2,1,0:T(8,128)}, f32[2,8,32]{2,1,0:T(8,128)}, f32[4,16,64]{2,1,0:T(8,128)}, f32[2,8,32]{2,1,0:T(8,1...) custom-call(f32[8,32,128]{2,1,0:T(8,128)} %refs_2_.3, ...), custom_call_target="tpu_custom_call" | custom-call | tf_op jit(solution)/shard_map/pallas_call | solution.py:686
  76.8 1.7 %reshape.16 = f32[4,8,8,3,1,4,16]{6,5,3,2,1,0,4:T(4,128)S(1)} reshape(f32[4,8,8,192]{3,2,1,0:T(8,128)} %bitcast.19) | data formatting | bytes 393216 | tf_op jit(solution)/shard_map/reshape | solution.py:698
  78.6 0.2 copy.7
  78.7 0.2 fusion.182
  78.9 0.2 squeeze.7
  79.1 0.2 mul.398
  79.3 0.2 squeeze.8
  79.5 0.1 broadcast_multiply_fusion
  79.6 0.1 fusion.163
  79.8 0.1 fusion.164
  79.9 0.1 fusion.165
  80.0 0.1 fusion.166
  80.1 0.1 fusion.167
  80.3 0.1 fusion.168
  80.4 0.1 fusion.169
  80.5 0.1 fusion.170
  80.6 0.1 fusion.171
  80.8 0.0 copy-start
  80.8 0.1 fusion.174
  80.9 0.1 fusion.157
  81.0 0.7 dynamic-slice_add_fusion.refs_0_
  81.7 51.6 %shard_map.51 = (f32[8,32,128]{2,1,0:T(8,128)}, f32[8,32,128]{2,1,0:T(8,128)}, f32[8,32,128]{2,1,0:T(8,128)}) custom-call(f32[1,4,16]{2,1,0:T(4,128)} %dynamic-slice_add_fusion.refs_0_, f32[8,32,128]{2,1,0:T(8,128)} %get-tuple-element.16.refs_1_, f32[8,32,128]{2,1,0:T(8,128)} %refs_2_.3, f32[8,32,128]{2,1,0:T(8,128)} %refs_3_.1, f32[8,32,128]{2,1,0:T(8,128)} %refs_4_.1, ...), custom_call_target="tpu_custom_call" | custom-call | tf_op jit(solution)/shard_map/pallas_call | solution.py:577
  133.3 1.6 %add.395 = f32[8,32,128]{2,1,0:T(8,128)} add(f32[8,32,128]{2,1,0:T(8,128)} %get-tuple-element.25, f32[8,32,128]{2,1,0:T(8,128)} %get-tuple-element.26) | non-fusion elementwise | flops 32768 | bytes 393216 | tf_op jit(solution)/shard_map/add | solution.py:585
  134.9 0.0 copy-done
  134.9 1.6 %sub.91 = f32[8,32,128]{2,1,0:T(8,128)} subtract(f32[8,32,128]{2,1,0:T(8,128)S(1)} %copy-done, f32[8,32,128]{2,1,0:T(8,128)} %get-tuple-element.27) | non-fusion elementwise | flops 32768 | bytes 393216 | tf_op jit(solution)/shard_map/sub | solution.py:585
Async XLA Ops:
  80.8 54.1 %copy-start = (f32[8,32,128]{2,1,0:T(8,128)S(1)}, f32[8,32,128]{2,1,0:T(8,128)}, u32[]{:S(2)}) copy-start(f32[8,32,128]{2,1,0:T(8,128)} %refs_2_.3) | copy-start | bytes 393220

commit v13 on v12

--- a/solution.py
+++ b/solution.py
@@ -515,8 +515,9 @@
     depth = len(shapes)
     coarsest = refs[0]
     level_in = [refs[1 + 4 * l : 5 + 4 * l] for l in range(depth)]
-    previous_out, update_out, operator_out = refs[1 + 4 * depth : 4 + 4 * depth]
-    scratch = refs[4 + 4 * depth :]
+    parts_out = refs[1 + 4 * depth]
+    previous_out, update_out, operator_out = (parts_out.at[n] for n in range(3))
+    scratch = refs[2 + 4 * depth :]
     results = scratch[7 * depth : 8 * depth]
     send_sem, recv_sem = scratch[8 * depth], scratch[8 * depth + 1]
     targets = neighbour_targets(sizes)
@@ -574,15 +575,26 @@
         pltpu.SemaphoreType.DMA((LEVELS, SLOTS, 6)),
     ]
     fine = jax.ShapeDtypeStruct(shapes[0], jnp.float32)
-    previous, update, operator = pl.pallas_call(
+    stacked = jax.ShapeDtypeStruct((3,) + shapes[0], jnp.float32)
+    parts = pl.pallas_call(
         functools.partial(up_kernel, cfg),
-        out_shape=(fine, fine, fine),
+        out_shape=stacked,
         in_specs=[vmem] * len(args),
-        out_specs=(vmem, vmem, vmem),
+        out_specs=vmem,
         scratch_shapes=scratch,
         compiler_params=pltpu.CompilerParams(collective_id=48, has_side_effects=True),
     )(*args)
-    return previous + update, rhs_levels[0] - operator
+    return pl.pallas_call(
+        finish_kernel,
+        out_shape=(fine, fine),
+        in_specs=[vmem, vmem],
+        out_specs=(vmem, vmem),
+    )(parts, rhs_levels[0])
+
+
+def finish_kernel(parts_ref, rhs_ref, solution_ref, residual_ref):
+    solution_ref[...] = parts_ref[0] + parts_ref[1]
+    residual_ref[...] = rhs_ref[...] - parts_ref[2]
 
 
 def level_scratch(shape):

time: 137 us -> 135 us (0.985)
  other arithmetic: 5.49 us -> 2.28 us
  Pallas kernels: 128 us -> 130 us
    pallas_call x1 -> x2, Pallas kernels: 51.6 us -> 53.4 us  [the longest x1 51.6 us: up_chain(): pl.pallas_call(functools.partial(up_kernel, cfg), out_shape=stacked, in_s...]
    add x1 -> x0, other arithmetic: 1.64 us -> none  [up_chain(): return (previous + update, rhs_levels[0] - operator)]
    sub x1 -> x0, other arithmetic: 1.58 us -> none  [up_chain(): return (previous + update, rhs_levels[0] - operator)]
where the time goes in v13:
time: 135 us
  Pallas kernels  130 us (96%)
  local copies, waits for them, and re-layouts  2.45 us (2%)
  other arithmetic  2.28 us (2%)
    pallas_call x1, Pallas kernels, down_chain(): pl.pallas_call(functools.partial(down_kernel, cfg), out_shape=tuple(out_s...  76.2 us
    pallas_call x1, Pallas kernels, up_chain(): pl.pallas_call(functools.partial(up_kernel, cfg), out_shape=stacked, in_s...  51.6 us

profile of v13, /device:TPU:1, one launch (start us, length us, event | category | flops | bytes accessed | tf_op | source)
XLA Modules:
  0.0 135.0 jit_solution(18273583560265189180)
XLA Ops:
  0.6 76.2 %shard_map.50 = (f32[8,32,128]{2,1,0:T(8,128)}, f32[4,16,64]{2,1,0:T(8,128)}, f32[2,8,32]{2,1,0:T(8,128)}, f32[4,16,64]{2,1,0:T(8,128)}, f32[2,8,32]{2,1,0:T(8,1...) custom-call(f32[8,32,128]{2,1,0:T(8,128)} %rhs_ref.1, ...), custom_call_target="tpu_custom_call" | custom-call | tf_op jit(solution)/shard_map/pallas_call | solution.py:698
  76.8 1.7 %reshape.16 = f32[4,8,8,3,1,4,16]{6,5,3,2,1,0,4:T(4,128)S(1)} reshape(f32[4,8,8,192]{3,2,1,0:T(8,128)} %bitcast.19) | data formatting | bytes 393216 | tf_op jit(solution)/shard_map/reshape | solution.py:710
  78.6 0.2 copy.7
  78.7 0.2 fusion.182
  78.9 0.2 squeeze.7
  79.1 0.2 mul.398
  79.3 0.2 squeeze.8
  79.5 0.1 broadcast_multiply_fusion
  79.6 0.1 fusion.163
  79.8 0.1 fusion.164
  79.9 0.1 fusion.165
  80.0 0.1 fusion.166
  80.1 0.1 fusion.167
  80.3 0.1 fusion.168
  80.4 0.1 fusion.169
  80.5 0.1 fusion.170
  80.6 0.1 fusion.171
  80.8 0.1 fusion.174
  80.9 0.1 fusion.157
  81.0 0.7 dynamic-slice_add_fusion.refs_0_
  81.7 51.6 %shard_map.51.parts_ref = f32[3,8,32,128]{3,2,1,0:T(8,128)} custom-call(f32[1,4,16]{2,1,0:T(4,128)} %dynamic-slice_add_fusion.refs_0_, f32[8,32,128]{2,1,0:T(8,128)} %get-tuple-element.13.refs_1_, f32[8,32,128]{2,1,0:T(8,128)} %rhs_ref.1, f32[8,32,128]{2,1,0:T(8,128)} %refs_3_.1, f32[8,32,128]{2,1,0:T(8,128)} %refs_4_.1, ...), custom_call_target="tpu_custom_call" | custom-call | tf_op jit(solution)/shard_map/pallas_call | solution.py:579
  133.3 1.7 %shard_map.52 = (f32[8,32,128]{2,1,0:T(8,128)}, f32[8,32,128]{2,1,0:T(8,128)}) custom-call(f32[3,8,32,128]{3,2,1,0:T(8,128)} %shard_map.51.parts_ref, f32[8,32,128]{2,1,0:T(8,128)} %rhs_ref.1), custom_call_target="tpu_custom_call" | custom-call | tf_op jit(solution)/shard_map/pallas_call | solution.py:587

commit v14 on v13

--- a/solution.py
+++ b/solution.py
@@ -622,7 +622,7 @@
     gathered = refs[3 + 4 * depth]
     scratch = refs[4 + 4 * depth :]
     send_sem, recv_sem = scratch[7 * depth], scratch[7 * depth + 1]
-    row, first, dense, gsend, grecv = scratch[7 * depth + 2 :]
+    row, first, dense, grouped, gsend, grecv = scratch[7 * depth + 2 :]
     targets = neighbour_targets(sizes)
     line, plane = gather_peers(sizes)
     barrier = pltpu.get_barrier_semaphore()
@@ -667,7 +667,9 @@
                 )
                 offset += pc
     row[...] = packed
-    gather_stages(sizes, line, plane, row, gathered, first, dense, gsend, grecv)
+    gather_stages(
+        sizes, line, plane, row, gathered, first, dense, gsend, grecv, rhs[depth].shape, grouped
+    )
 
 
 def down_chain(right_side, beta_coef, alpha_coef):
@@ -685,13 +687,17 @@
     width = 3 * shapes[LEVELS][0] * shapes[LEVELS][1] * shapes[LEVELS][2]
     lanes = -(-width // 128) * 128
     top = max(nz, nx * ny)
-    out_shapes.append(jax.ShapeDtypeStruct((nx, ny, nz, lanes), jnp.float32))
+    a3, b3, c3 = shapes[LEVELS]
+    count = 3 * a3 * b3
+    height = -(-count // 8) * 8
+    out_shapes.append(jax.ShapeDtypeStruct((nx, ny, height, nz * c3), jnp.float32))
     scratch += [
         pltpu.SemaphoreType.DMA((LEVELS, SLOTS, 6)),
         pltpu.SemaphoreType.DMA((LEVELS, SLOTS, 6)),
         pltpu.VMEM((1, lanes), jnp.float32),
         pltpu.VMEM((nz, 1, lanes), jnp.float32),
         pltpu.VMEM((nz, lanes), jnp.float32),
+        pltpu.VMEM((height, nz * c3), jnp.float32),
         pltpu.SemaphoreType.DMA((2, top)),
         pltpu.SemaphoreType.DMA((2, top)),
     ]
@@ -707,8 +713,8 @@
     rhs_levels = [right_side] + list(outs[LEVELS : 2 * LEVELS])
     betas = [beta_coef] + list(outs[2 * LEVELS : 3 * LEVELS])
     alphas = [alpha_coef] + list(outs[3 * LEVELS : 4 * LEVELS])
-    whole = outs[4 * LEVELS][..., :width].reshape((nx, ny, nz, 3) + shapes[LEVELS])
-    whole = whole.transpose(3, 0, 4, 1, 5, 2, 6)
+    whole = outs[4 * LEVELS][:, :, :count].reshape((nx, ny, 3, a3, b3, nz * c3))
+    whole = whole.transpose(2, 0, 3, 1, 4, 5)
     whole = whole.reshape((3,) + tuple(n * s for n, s in zip(sizes, shapes[LEVELS])))
     return iterates, rhs_levels, betas, alphas, whole
 
@@ -727,7 +733,7 @@
     return line, plane
 
 
-def gather_stages(sizes, line, plane, row_ref, out_ref, first, dense, send_sem, recv_sem):
+def gather_stages(sizes, line, plane, row_ref, out_ref, first, dense, send_sem, recv_sem, block, grouped):
     index = [lax.axis_index(axis) for axis in AXES]
     nx, ny, nz = sizes
     ix, iy, iz = index
@@ -758,12 +764,35 @@
         incoming.wait_recv()
     for z in range(nz):
         dense[z : z + 1, :] = first[z]
+    pa, pb, pc = block
+    count = 3 * pa * pb
+    height, lanes = grouped.shape
+    flipped = jnp.transpose(dense[...])
+    regrouped = jnp.zeros((height, lanes), jnp.float32)
+    for k in range(pc):
+        pick = (
+            lax.broadcasted_iota(jnp.int32, (height, dense.shape[1]), 0) * pc + k
+            == lax.broadcasted_iota(jnp.int32, (height, dense.shape[1]), 1)
+        ) & (lax.broadcasted_iota(jnp.int32, (height, dense.shape[1]), 0) < count)
+        spread = (
+            lax.broadcasted_iota(jnp.int32, (nz, lanes), 0) * pc + k
+            == lax.broadcasted_iota(jnp.int32, (nz, lanes), 1)
+        )
+        chosen = jnp.dot(
+            pick.astype(jnp.float32), flipped, precision=lax.Precision.HIGHEST,
+            preferred_element_type=jnp.float32,
+        )
+        regrouped = regrouped + jnp.dot(
+            chosen, spread.astype(jnp.float32), precision=lax.Precision.HIGHEST,
+            preferred_element_type=jnp.float32,
+        )
+    grouped[...] = regrouped
 
     mine = ix * ny + iy
     waits = []
     for n, ((dx, dy), peer) in enumerate(plane):
         copy = pltpu.make_async_remote_copy(
-            src_ref=dense,
+            src_ref=grouped,
             dst_ref=out_ref.at[ix, iy],
             send_sem=send_sem.at[1, n],
             recv_sem=recv_sem.at[1, mine],
@@ -774,7 +803,7 @@
         ox = lax.rem(ix + nx - dx, nx)
         oy = lax.rem(iy + ny - dy, ny)
         incoming = pltpu.make_async_remote_copy(
-            src_ref=dense,
+            src_ref=grouped,
             dst_ref=out_ref.at[ox, oy],
             send_sem=send_sem.at[1, n],
             recv_sem=recv_sem.at[1, ox * ny + oy],
@@ -782,7 +811,7 @@
             device_id_type=MESH,
         )
         waits.append((copy, incoming))
-    out_ref[ix, iy] = dense[...]
+    out_ref[ix, iy] = grouped[...]
     for copy, incoming in waits:
         copy.wait_send()
         incoming.wait_recv()

time: 135 us -> 135 us (level)
  local copies, waits for them, and re-layouts: 2.45 us -> 1.07 us
    reshape x2 -> x0, local copies, waits for them, and re-layouts: 1.89 us -> none  [down_chain(): outs[4 * LEVELS][..., :width].reshape((nx, ny, nz, 3) + shapes[LEVELS])]
where the time goes in v14:
time: 135 us
  Pallas kernels  131 us (97%)
  other arithmetic  2.13 us (2%)
    pallas_call x1, Pallas kernels, down_chain(): pl.pallas_call(functools.partial(down_kernel, cfg), out_shape=tuple(out_s...  77.5 us
    pallas_call x1, Pallas kernels, up_chain(): pl.pallas_call(functools.partial(up_kernel, cfg), out_shape=stacked, in_s...  51.6 us

profile of v14, /device:TPU:1, one launch (start us, length us, event | category | flops | bytes accessed | tf_op | source)
XLA Modules:
  0.0 134.8 jit_solution(13609691780867089021)
XLA Ops:
  0.6 77.5 %shard_map.50 = (f32[8,32,128]{2,1,0:T(8,128)}, f32[4,16,64]{2,1,0:T(8,128)}, f32[2,8,32]{2,1,0:T(8,128)}, f32[4,16,64]{2,1,0:T(8,128)}, f32[2,8,32]{2,1,0:T(8,1...) custom-call(f32[8,32,128]{2,1,0:T(8,128)} %rhs_ref.1, ...), custom_call_target="tpu_custom_call" | custom-call | tf_op jit(solution)/shard_map/pallas_call | solution.py:704
  78.1 1.0 copy.6
  79.3 0.1 broadcast_multiply_fusion
  79.4 0.1 fusion.163
  79.5 0.1 fusion.164
  79.6 0.1 fusion.165
  79.8 0.1 fusion.166
  79.9 0.1 fusion.167
  80.0 0.1 fusion.168
  80.1 0.1 fusion.169
  80.3 0.1 fusion.170
  80.4 0.1 fusion.171
  80.5 0.1 fusion.174
  80.6 0.1 fusion.157
  80.8 0.7 dynamic-slice_add_fusion.refs_0_
  81.4 51.6 %shard_map.51.parts_ref = f32[3,8,32,128]{3,2,1,0:T(8,128)} custom-call(f32[1,4,16]{2,1,0:T(4,128)} %dynamic-slice_add_fusion.refs_0_, f32[8,32,128]{2,1,0:T(8,128)} %get-tuple-element.13.refs_1_, f32[8,32,128]{2,1,0:T(8,128)} %rhs_ref.1, f32[8,32,128]{2,1,0:T(8,128)} %refs_3_.1, f32[8,32,128]{2,1,0:T(8,128)} %refs_4_.1, ...), custom_call_target="tpu_custom_call" | custom-call | tf_op jit(solution)/shard_map/pallas_call | solution.py:579
  133.1 1.7 %shard_map.52 = (f32[8,32,128]{2,1,0:T(8,128)}, f32[8,32,128]{2,1,0:T(8,128)}) custom-call(f32[3,8,32,128]{3,2,1,0:T(8,128)} %shard_map.51.parts_ref, f32[8,32,128]{2,1,0:T(8,128)} %rhs_ref.1), custom_call_target="tpu_custom_call" | custom-call | tf_op jit(solution)/shard_map/pallas_call | solution.py:587
  (4 shorter events, 0.1 us)

commit v15 on v14

--- a/solution.py
+++ b/solution.py
@@ -767,23 +767,20 @@
     pa, pb, pc = block
     count = 3 * pa * pb
     height, lanes = grouped.shape
-    flipped = jnp.transpose(dense[...])
+    width = dense.shape[1]
+    owner = (
+        lax.broadcasted_iota(jnp.int32, (height, width), 1) // pc
+        == lax.broadcasted_iota(jnp.int32, (height, width), 0)
+    ) & (lax.broadcasted_iota(jnp.int32, (height, width), 0) < count)
     regrouped = jnp.zeros((height, lanes), jnp.float32)
-    for k in range(pc):
-        pick = (
-            lax.broadcasted_iota(jnp.int32, (height, dense.shape[1]), 0) * pc + k
-            == lax.broadcasted_iota(jnp.int32, (height, dense.shape[1]), 1)
-        ) & (lax.broadcasted_iota(jnp.int32, (height, dense.shape[1]), 0) < count)
+    for z in range(nz):
         spread = (
-            lax.broadcasted_iota(jnp.int32, (nz, lanes), 0) * pc + k
-            == lax.broadcasted_iota(jnp.int32, (nz, lanes), 1)
-        )
-        chosen = jnp.dot(
-            pick.astype(jnp.float32), flipped, precision=lax.Precision.HIGHEST,
-            preferred_element_type=jnp.float32,
-        )
+            lax.broadcasted_iota(jnp.int32, (width, lanes), 0) % pc + z * pc
+            == lax.broadcasted_iota(jnp.int32, (width, lanes), 1)
+        )
+        rows_z = jnp.where(owner, jnp.broadcast_to(dense[z : z + 1, :], (height, width)), 0.0)
         regrouped = regrouped + jnp.dot(
-            chosen, spread.astype(jnp.float32), precision=lax.Precision.HIGHEST,
+            rows_z, spread.astype(jnp.float32), precision=lax.Precision.HIGHEST,
             preferred_element_type=jnp.float32,
         )
     grouped[...] = regrouped

time: 135 us -> 134 us (level)
  no operation moved by 1% of the time
where the time goes in v15:
time: 134 us
  Pallas kernels  130 us (97%)
  other arithmetic  2.13 us (2%)
    pallas_call x1, Pallas kernels, down_chain(): pl.pallas_call(functools.partial(down_kernel, cfg), out_shape=tuple(out_s...  76.9 us
    pallas_call x1, Pallas kernels, up_chain(): pl.pallas_call(functools.partial(up_kernel, cfg), out_shape=stacked, in_s...  51.6 us

profile of v15, /device:TPU:1, one launch (start us, length us, event | category | flops | bytes accessed | tf_op | source)
XLA Modules:
  0.0 134.2 jit_solution(12272671524398760425)
XLA Ops:
  0.6 76.9 %shard_map.50 = (f32[8,32,128]{2,1,0:T(8,128)}, f32[4,16,64]{2,1,0:T(8,128)}, f32[2,8,32]{2,1,0:T(8,128)}, f32[4,16,64]{2,1,0:T(8,128)}, f32[2,8,32]{2,1,0:T(8,1...) custom-call(f32[8,32,128]{2,1,0:T(8,128)} %rhs_ref.1, ...), custom_call_target="tpu_custom_call" | custom-call | tf_op jit(solution)/shard_map/pallas_call | solution.py:704
  77.5 1.0 copy.6
  78.6 0.1 broadcast_multiply_fusion
  78.7 0.1 fusion.163
  78.9 0.1 fusion.164
  79.0 0.1 fusion.165
  79.1 0.1 fusion.166
  79.2 0.1 fusion.167
  79.4 0.1 fusion.168
  79.5 0.1 fusion.169
  79.6 0.1 fusion.170
  79.7 0.1 fusion.171
  79.9 0.1 fusion.174
  80.0 0.1 fusion.157
  80.1 0.7 dynamic-slice_add_fusion.refs_0_
  80.8 51.6 %shard_map.51.parts_ref = f32[3,8,32,128]{3,2,1,0:T(8,128)} custom-call(f32[1,4,16]{2,1,0:T(4,128)} %dynamic-slice_add_fusion.refs_0_, f32[8,32,128]{2,1,0:T(8,128)} %get-tuple-element.13.refs_1_, f32[8,32,128]{2,1,0:T(8,128)} %rhs_ref.1, f32[8,32,128]{2,1,0:T(8,128)} %refs_3_.1, f32[8,32,128]{2,1,0:T(8,128)} %refs_4_.1, ...), custom_call_target="tpu_custom_call" | custom-call | tf_op jit(solution)/shard_map/pallas_call | solution.py:579
  132.4 1.7 %shard_map.52 = (f32[8,32,128]{2,1,0:T(8,128)}, f32[8,32,128]{2,1,0:T(8,128)}) custom-call(f32[3,8,32,128]{3,2,1,0:T(8,128)} %shard_map.51.parts_ref, f32[8,32,128]{2,1,0:T(8,128)} %rhs_ref.1), custom_call_target="tpu_custom_call" | custom-call | tf_op jit(solution)/shard_map/pallas_call | solution.py:587
  (4 shorter events, 0.1 us)
